TPU v7x, 128 devices: a whole 4x4x4 slice. The times are simulated.
128 devices in a mesh: grp: 4 (over z), rve: 32 (over y, x, core).
Axes of the slice: x: 4, y: 4, z: 4, core: 2. Of those that a mesh axis runs over, the one named last changes fastest.
Arguments:
- displacement: float32 [3, 256, 32, 128], P(None, ('grp', 'rve')), may hold values from -6 to 6
- stiffness: bfloat16 [27, 3, 3, 256, 32, 128], P(None, None, None, ('grp', 'rve')), may hold values from -0.65625 to 0.65625
- external: float32 [3, 256, 32, 128], P(None, ('grp', 'rve')), may hold values from -6 to 6
- point_node: int32 [8], P('grp'), may hold values from 0 to 262143
- point_owner: int32 [8, 1], P('grp'), may hold values from 0 to 3; in each aligned block of 2 rows (0 to 1, 2 to 3, ...) no two rows name the same one
- point_load: float32 [8, 18], P('grp'), may hold values from -6 to 6
- moduli_diag: float32 [4, 6, 32, 64, 128], P('grp', None, 'rve'), may hold values from 1.5 to 4
- moduli_off: float32 [4, 36, 32, 64, 128], P('grp', None, 'rve'), may hold values from -1 to 1
- schmid: float32 [4, 72, 32, 64, 128], P('grp', None, 'rve'), may hold values from -1 to 1
- crss: float32 [4, 12, 32, 64, 128], P('grp', None, 'rve'), may hold values from 0.3 to 3
- branch: int32 [4, 32, 64, 128], P('grp', 'rve'), may hold values from 0 to 4095
- rate: float32 [4, 32, 64, 128], P('grp', 'rve'), may hold values from 0.03 to 0.3
Outputs:
- residual: float32 [3, 256, 32, 128], P(None, ('grp', 'rve'))
- point_stress: float32 [8, 6], P('grp')
Inputs may be any that keep to these rules, and one draw needn't show every extreme that they name: `point_owner`: among the 2 points of one quarter's list, at most 1 name the same volume, a bound that some block reaches.
All inputs are finite; a program needn't handle non-finite values.
Results may differ from a plain program's by a relative error of at most 0.0003.
Values sent between devices are 32-bit elements; how exact they have to be, the bound alone decides.
No kernel may reach another device: no remote copies, remote signals or barrier semaphores. Data moves between devices by JAX's collectives and lax.ppermute only.
A program may use at most 128 MiB of HBM per device.

v0:
```python
import jax
import jax.numpy as jnp
from jax import lax
from jax.experimental import pallas as pl
from jax.experimental.pallas import tpu as pltpu
from jax.sharding import PartitionSpec as P

SLIP = 12
RELAX = 0.15
SHARE = RELAX / 6.0
ROWS = 64
LANES = 128
SLOTS = 2
FIELDS = SLOTS * 6
VMEM_LIMIT = 56 * 1024 * 1024
F32 = jnp.float32

VM = pl.BlockSpec(memory_space=pltpu.VMEM)
SM = pl.BlockSpec(memory_space=pltpu.SMEM)


def call(kernel, name, in_specs, outs, scratch=(), out_specs=None):
    return pl.pallas_call(
        kernel,
        name=name,
        in_specs=in_specs,
        out_specs=[VM] * len(outs) if out_specs is None else out_specs,
        out_shape=[jax.ShapeDtypeStruct(s, F32) for s in outs],
        scratch_shapes=list(scratch),
        compiler_params=pltpu.CompilerParams(vmem_limit_bytes=VMEM_LIMIT),
    )


def chunks(body):
    def step(k, carry):
        body(pl.ds(pl.multiple_of(k * 8, 8), 8))
        return carry

    lax.fori_loop(0, ROWS // 8, step, 0)


def pack_kernel(diag, off, schmid, crss, branch, rate, c_ref, s_ref):
    for i in range(6):
        for j in range(6):
            v = off[6 * i + j]
            c_ref[6 * i + j] = v + diag[i] if i == j else v
    bits = branch[...]
    speed = rate[...]
    for a in range(SLIP):
        limit = crss[a]
        inverse = 1.0 / limit
        for j in range(6):
            s_ref[6 * a + j] = schmid[6 * a + j] * inverse
        active = (jnp.right_shift(bits, a) & 1).astype(F32)
        s_ref[6 * SLIP + a] = active * speed * (limit * limit)


def pack(diag, off, schmid, crss, branch, rate):
    block = lambda n: pl.BlockSpec((n, 8, LANES), lambda k: (0, k, 0))
    flat = pl.BlockSpec((8, LANES), lambda k: (k, 0))
    return pl.pallas_call(
        pack_kernel,
        name="pack",
        grid=(ROWS // 8,),
        in_specs=[block(6), block(36), block(72), block(12), flat, flat],
        out_specs=[block(36), block(84)],
        out_shape=[
            jax.ShapeDtypeStruct((36, ROWS, LANES), F32),
            jax.ShapeDtypeStruct((84, ROWS, LANES), F32),
        ],
        compiler_params=pltpu.CompilerParams(vmem_limit_bytes=VMEM_LIMIT),
    )(diag, off, schmid, crss, branch, rate)


def times(c_ref, at, vectors):
    sums = [[None] * 6 for _ in vectors]
    for i in range(6):
        for j in range(6):
            c = c_ref[6 * i + j, at, :]
            for s, vector in enumerate(vectors):
                term = c * vector[j]
                sums[s][i] = term if j == 0 else sums[s][i] + term
    return sums


def load(ref, at):
    return [[ref[6 * s + i, at, :] for i in range(6)] for s in range(SLOTS)]


def store(ref, at, values):
    for s in range(SLOTS):
        for i in range(6):
            ref[6 * s + i, at, :] = values[s][i]


def slip(s_ref, at, stress, total):
    total = [list(t) for t in total]
    for a in range(SLIP):
        rows = [s_ref[6 * a + j, at, :] for j in range(6)]
        gain = s_ref[6 * SLIP + a, at, :]
        for s in range(SLOTS):
            t = rows[0] * stress[s][0]
            for j in range(1, 6):
                t = t + rows[j] * stress[s][j]
            w = gain * (t - jnp.tanh(t))
            for j in range(6):
                total[s][j] = total[s][j] - rows[j] * w
    return total


def around(x):
    rows = pltpu.roll(x, 1, axis=0) + pltpu.roll(x, ROWS - 1, axis=0)
    return rows + (pltpu.roll(x, 1, axis=1) + pltpu.roll(x, LANES - 1, axis=1))


def beside(sig_a, sig_b, base_a, base_b):
    def step(f, carry):
        a = sig_a[f]
        b = sig_b[f]
        base_a[f] = base_a[f] + SHARE * (around(a) + b)
        base_b[f] = base_b[f] + SHARE * (around(b) + a)
        return carry

    lax.fori_loop(0, FIELDS, step, 0)


def combine(x, y, fn):
    return [[fn(x[s][i], y[s][i]) for i in range(6)] for s in range(SLOTS)]


def relaxed(e, sig):
    return combine(e, sig, lambda u, v: u - RELAX * v)


def first_kernel(ebar, c_a, c_b, g_a, g_b, s_a, s_b, e_a, e_b, sig_a, sig_b, t_a, t_b):
    for c_ref, g_ref, t_ref, e_ref in ((c_a, g_a, t_a, e_a), (c_b, g_b, t_b, e_b)):

        def body(at, c_ref=c_ref, g_ref=g_ref, t_ref=t_ref, e_ref=e_ref):
            strain = [
                [jnp.full((8, LANES), ebar[s, i], F32) for i in range(6)] for s in range(SLOTS)
            ]
            sig = times(c_ref, at, strain)
            outer = times(g_ref, at, strain)
            store(t_ref, at, sig)
            base = combine(relaxed(strain, sig), outer, lambda u, v: u + SHARE * v)
            store(e_ref, at, base)

        chunks(body)
    beside(t_a, t_b, e_a, e_b)
    advance(((c_a, s_a, t_a, e_a, e_a, sig_a), (c_b, s_b, t_b, e_b, e_b, sig_b)))


def advance(planes):
    for c_ref, s_ref, t_ref, base_ref, e_ref, sig_ref in planes:

        def body(at, c_ref=c_ref, s_ref=s_ref, t_ref=t_ref, base_ref=base_ref, e_ref=e_ref, sig_ref=sig_ref):
            e = slip(s_ref, at, load(t_ref, at), load(base_ref, at))
            store(e_ref, at, e)
            store(sig_ref, at, times(c_ref, at, e))

        chunks(body)


def settle_kernel(e_a, e_b, sig_a, sig_b, s_a, s_b, r_a, r_b):
    for e_ref, sig_ref, s_ref, r_ref in ((e_a, sig_a, s_a, r_a), (e_b, sig_b, s_b, r_b)):

        def body(at, e_ref=e_ref, sig_ref=sig_ref, s_ref=s_ref, r_ref=r_ref):
            sig = load(sig_ref, at)
            store(r_ref, at, slip(s_ref, at, sig, relaxed(load(e_ref, at), sig)))

        chunks(body)
    beside(sig_a, sig_b, r_a, r_b)


def arrive(planes):
    for r_ref, sig_ref, far_sig, far_r, c_ref, g_ref, t_ref, base_ref in planes:

        def body(
            at,
            r_ref=r_ref,
            sig_ref=sig_ref,
            far_sig=far_sig,
            far_r=far_r,
            c_ref=c_ref,
            g_ref=g_ref,
            t_ref=t_ref,
            base_ref=base_ref,
        ):
            add = lambda u, v: u + SHARE * v
            e = combine(load(r_ref, at), load(far_sig, at), add)
            sig = times(c_ref, at, e)
            store(t_ref, at, sig)
            base = relaxed(e, sig)
            outer = times(g_ref, at, combine(load(far_r, at), load(sig_ref, at), add))
            store(base_ref, at, combine(base, outer, add))

        chunks(body)


def pair_kernel(
    r_a, r_b, sig_a, sig_b, fs_a, fs_b, fr_a, fr_b, c_a, c_b, g_a, g_b, s_a, s_b, e_a, e_b, n_a, n_b, t_a, t_b
):
    arrive(
        (
            (r_a, sig_a, fs_a, fr_a, c_a, g_a, t_a, e_a),
            (r_b, sig_b, fs_b, fr_b, c_b, g_b, t_b, e_b),
        )
    )
    beside(t_a, t_b, e_a, e_b)
    advance(((c_a, s_a, t_a, e_a, e_a, n_a), (c_b, s_b, t_b, e_b, e_b, n_b)))


def last_kernel(
    r_a, r_b, sig_a, sig_b, fs_a, fs_b, fr_a, fr_b, c_a, c_b, g_a, g_b, s_a, s_b, out, e_a, e_b, n_a, n_b, t_a, t_b
):
    pair_kernel(
        r_a, r_b, sig_a, sig_b, fs_a, fs_b, fr_a, fr_b, c_a, c_b, g_a, g_b, s_a, s_b, e_a, e_b, n_a, n_b, t_a, t_b
    )
    settle_kernel(e_a, e_b, n_a, n_b, s_a, s_b, t_a, t_b)
    for k in range(FIELDS):
        out[k] = jnp.zeros((8, LANES), F32)
    for t_ref, n_ref, c_ref, g_ref in ((t_a, n_a, c_a, g_a), (t_b, n_b, c_b, g_b)):

        def body(at, t_ref=t_ref, n_ref=n_ref, c_ref=c_ref, g_ref=g_ref):
            own = times(c_ref, at, load(t_ref, at))
            far = times(g_ref, at, load(n_ref, at))
            for s in range(SLOTS):
                for i in range(6):
                    out[6 * s + i] = out[6 * s + i] + (own[s][i] + SHARE * far[s][i])

        chunks(body)


def strain_kernel(node, owner, member, disp, before, after, out, grid):
    grid[:, 0:1] = before[...]
    grid[:, 1:3] = disp[...]
    grid[:, 3:4] = after[...]
    lane = lax.broadcasted_iota(jnp.int32, (1, LANES), 1)
    group = lax.broadcasted_iota(jnp.int32, (8, LANES), 0)
    total = jnp.zeros((8, LANES), F32)
    for p in range(2):
        local = node[p] - member[0] * (2 * 32 * LANES)
        present = (local >= 0) & (local < 2 * 32 * LANES)
        local = jnp.clip(local, 0, 2 * 32 * LANES - 1)
        x = local // (32 * LANES)
        y = (local // LANES) % 32
        z = local % LANES
        up_y = jnp.minimum(y + 1, 31)
        down_y = jnp.maximum(y - 1, 0)
        has_up = jnp.where(y < 31, 1.0, 0.0).astype(F32)
        has_down = jnp.where(y > 0, 1.0, 0.0).astype(F32)
        slope = []
        for c in range(3):
            row = lambda dx, yy: grid[c, x + dx, pl.ds(yy, 1), :]
            gx = (row(2, y) - row(0, y)) * 0.5
            gy = (row(1, up_y) * has_up - row(1, down_y) * has_down) * 0.5
            mid = row(1, y)
            right = jnp.where(lane < LANES - 1, pltpu.roll(mid, LANES - 1, axis=1), 0.0)
            left = jnp.where(lane > 0, pltpu.roll(mid, 1, axis=1), 0.0)
            slope.append((gx, gy, (right - left) * 0.5))
        parts = [
            slope[0][0],
            slope[1][1],
            slope[2][2],
            slope[1][2] + slope[2][1],
            slope[0][2] + slope[2][0],
            slope[0][1] + slope[1][0],
        ]
        here = (lane == z) & present
        line = jnp.zeros((1, LANES), F32)
        for j, part in enumerate(parts):
            value = jnp.sum(jnp.where(here, part, 0.0), axis=1, keepdims=True)
            line = line + jnp.where(lane == j, value, 0.0)
        total = total + jnp.where(group == owner[p, 0], line, 0.0)
    out[...] = total


def stencil_kernel(blocks, disp, before, after, external, out, moved, total):
    step = pl.program_id(0)

    @pl.when(step == 0)
    def _():
        lane = lax.broadcasted_iota(jnp.int32, (32, LANES), 1)
        row = lax.broadcasted_iota(jnp.int32, (32, LANES), 0)
        total[...] = jnp.zeros_like(total)
        for c in range(3):
            for x in range(4):
                v = before[c, 0] if x == 0 else (after[c, 0] if x == 3 else disp[c, x - 1])
                for j in range(3):
                    w = v
                    if j == 0:
                        w = jnp.where(row > 0, pltpu.roll(v, 1, axis=0), 0.0)
                    if j == 2:
                        w = jnp.where(row < 31, pltpu.roll(v, 31, axis=0), 0.0)
                    moved[j, 0, c, x] = jnp.where(lane > 0, pltpu.roll(w, 1, axis=1), 0.0)
                    moved[j, 1, c, x] = w
                    moved[j, 2, c, x] = jnp.where(lane < LANES - 1, pltpu.roll(w, LANES - 1, axis=1), 0.0)

    i = step // 3
    j = step % 3
    for c in range(3):
        for x in range(2):
            s = total[c, x]
            for k in range(3):
                for d in range(3):
                    s = s + blocks[k, c, d, x].astype(F32) * moved[j, k, d, i + x]
            total[c, x] = s

    @pl.when(step == 8)
    def _():
        out[...] = external[...] - total[...]


def stencil(stiffness, disp, before, after, external):
    whole = lambda n: pl.BlockSpec((3, n, 32, LANES), lambda s: (0, 0, 0, 0))
    return pl.pallas_call(
        stencil_kernel,
        name="stencil",
        grid=(9,),
        in_specs=[
            pl.BlockSpec((3, 3, 3, 2, 32, LANES), lambda s: (s, 0, 0, 0, 0, 0)),
            whole(2),
            whole(1),
            whole(1),
            whole(2),
        ],
        out_specs=whole(2),
        out_shape=jax.ShapeDtypeStruct((3, 2, 32, LANES), F32),
        scratch_shapes=[
            pltpu.VMEM((3, 3, 3, 4, 32, LANES), F32),
            pltpu.VMEM((3, 2, 32, LANES), F32),
        ],
        compiler_params=pltpu.CompilerParams(vmem_limit_bytes=VMEM_LIMIT),
    )(stiffness, disp, before, after, external)


def final_kernel(node, owner, member, received, loads, base, residual, stress):
    residual[...] = base[...]
    lane = lax.broadcasted_iota(jnp.int32, (1, LANES), 1)
    sums = [jnp.sum(received[g], axis=0, keepdims=True) for g in range(4)]
    for p in range(2):
        line = jnp.zeros((1, LANES), F32)
        for g in range(4):
            line = line + jnp.where(owner[p, 0] == g, sums[g], 0.0)
        line = line * (1.0 / 262144.0)
        stress[p : p + 1, :] = line[:, 0:6]
        local = node[p] - member[0] * (2 * 32 * LANES)
        present = (local >= 0) & (local < 2 * 32 * LANES)
        local = jnp.clip(local, 0, 2 * 32 * LANES - 1)
        x = local // (32 * LANES)
        y = (local // LANES) % 32
        z = local % LANES
        here = (lane == z) & present
        for c in range(3):
            force = jnp.sum(loads[p, c : c + 1, :] * line, axis=1, keepdims=True)
            row = residual[c, x, pl.ds(y, 1), :]
            residual[c, x, pl.ds(y, 1), :] = row - jnp.where(here, force, 0.0)


def per_device(
    displacement,
    stiffness,
    external,
    point_node,
    point_owner,
    point_load,
    moduli_diag,
    moduli_off,
    schmid,
    crss,
    branch,
    rate,
):
    groups = lax.axis_size("grp")
    members = lax.axis_size("rve")
    member = lax.axis_index("rve")
    everyone = groups * members

    def over(value, pairs, axis="rve"):
        return lax.ppermute(value, axis, pairs)

    partner = [(i, i ^ 1) for i in range(members)]
    send_a = [(i, (i - 2 if i % 2 == 0 else i + 2) % members) for i in range(members)]
    send_b = [(i, (i + 2 if i % 2 == 0 else i - 2) % members) for i in range(members)]

    both = ("grp", "rve")
    upward = [(i, i + 1) for i in range(everyone - 1)]
    downward = [(i + 1, i) for i in range(everyone - 1)]
    before = over(displacement[:, 1:2], upward, both)
    after = over(displacement[:, 0:1], downward, both)

    c_a, s_a = pack(moduli_diag[0, :, 0], moduli_off[0, :, 0], schmid[0, :, 0], crss[0, :, 0], branch[0, 0], rate[0, 0])
    c_b = over(c_a, partner)
    g_b = over(c_a, send_a)
    g_a = over(c_b, send_b)
    s_b = over(s_a, partner)

    where = member.reshape(1).astype(jnp.int32)
    message = call(
        strain_kernel,
        "strain",
        [SM, SM, SM, VM, VM, VM],
        [(8, LANES)],
        [pltpu.VMEM((3, 4, 32, LANES), F32)],
    )(point_node, point_owner, where, displacement, before, after)[0]
    message = jnp.broadcast_to(message[:groups, None, None, :], (groups, members, 1, LANES))
    arrived = lax.all_to_all(message.reshape(everyone, 1, LANES), both, 0, 0, tiled=True)
    strains = jnp.sum(arrived.reshape(groups, members, LANES), axis=1)
    core = member % 2
    ebar = lax.dynamic_slice_in_dim(strains, core * SLOTS, SLOTS, axis=0)

    base = stencil(stiffness, displacement, before, after, external)

    plane = (FIELDS, ROWS, LANES)
    temps = [pltpu.VMEM(plane, F32)] * 2
    e_a, e_b, sig_a, sig_b = call(first_kernel, "first", [SM] + [VM] * 6, [plane] * 4, temps)(
        ebar, c_a, c_b, g_a, g_b, s_a, s_b
    )
    for pair in range(4):
        fs_b = over(sig_a, send_a)
        fs_a = over(sig_b, send_b)
        r_a, r_b = call(settle_kernel, "settle", [VM] * 6, [plane] * 2)(e_a, e_b, sig_a, sig_b, s_a, s_b)
        fr_b = over(r_a, send_a)
        fr_a = over(r_b, send_b)
        operands = (r_a, r_b, sig_a, sig_b, fs_a, fs_b, fr_a, fr_b, c_a, c_b, g_a, g_b, s_a, s_b)
        if pair < 3:
            e_a, e_b, sig_a, sig_b = call(pair_kernel, "pair", [VM] * 14, [plane] * 4, temps)(*operands)
        else:
            sums = call(last_kernel, "last", [VM] * 14, [(FIELDS, 8, LANES)], temps * 3)(*operands)[0]

    totals = jnp.sum(sums, axis=(1, 2)).reshape(SLOTS, 6)
    totals = jnp.pad(totals, ((0, 0), (0, LANES - 6)))
    mine = jnp.zeros((groups, LANES), F32)
    mine = lax.dynamic_update_slice_in_dim(mine, totals, core * SLOTS, axis=0)
    reply = jnp.broadcast_to(mine[:, None, None, :], (groups, members, 1, LANES))
    received = lax.all_to_all(reply.reshape(everyone, 1, LANES), both, 0, 0, tiled=True)
    loads = jnp.pad(point_load.reshape(-1, 3, 6), ((0, 0), (0, 0), (0, LANES - 6)))
    residual, point_stress = call(
        final_kernel, "final", [SM, SM, SM, VM, VM, VM], [(3, 2, 32, LANES), (2, 6)]
    )(point_node, point_owner, where, received.reshape(groups, members, LANES), loads, base)
    return (residual, point_stress)


def solution(mesh):
    in_specs = (
        P(None, ("grp", "rve"), None, None),
        P(None, None, None, ("grp", "rve"), None, None),
        P(None, ("grp", "rve"), None, None),
        P("grp"),
        P("grp", None),
        P("grp", None),
        P("grp", None, "rve", None, None),
        P("grp", None, "rve", None, None),
        P("grp", None, "rve", None, None),
        P("grp", None, "rve", None, None),
        P("grp", "rve", None, None),
        P("grp", "rve", None, None),
    )
    out_specs = (P(None, ("grp", "rve"), None, None), P("grp", None))
    return jax.shard_map(
        per_device, mesh=mesh, in_specs=in_specs, out_specs=out_specs, check_vma=False
    )
```

profile of v0, /device:TPU:1, one launch (start us, length us, event | category | flops | bytes accessed | tf_op | source)
XLA Modules:
  0.0 257.9 jit_solution(13922355072518393047)
XLA Ops:
  0.7 6.7 %pack.1 = (f32[36,64,128]{2,1,0:T(8,128)}, f32[84,64,128]{2,1,0:T(8,128)}) custom-call(f32[6,64,128]{2,1,0:T(8,128)} %bitcast.18, f32[36,64,128]{2,1,0:T(8,128)} %bitcast.14, f32[72,64,128]{2,1,0:T(8,128)} %bitcast.13, f32[12,64,128]{2,1,0:T(8,128)} %bitcast.15, s32[64,128]{1,0:T(8,128)} %bitcast.19, f32[64,128]{1,0:T(8,128)} %bitcast.20), custom_call_target="tpu_custom_call" | custom-call | tf_op jit(solution)/shard_map/pack/pallas_call | solution.py:61
  7.4 1.4 collective-permute-start.5
  8.8 0.1 collective-permute-start.2
  8.9 1.3 collective-permute-start.4
  10.2 5.2 %collective-permute-done.2.c_b = f32[36,64,128]{2,1,0:T(8,128)} collective-permute-done((f32[36,64,128]{2,1,0:T(8,128)}, f32[36,64,128]{2,1,0:T(8,128)}, u32[]{:S(2)}, u32[]{:S(2)}) %collective-permute-start.2) | collective-permute-done | bytes 1179680 | tf_op jit(solution)/shard_map/ppermute | solution.py:380
  15.4 5.0 %collective-permute-start.3 = (f32[36,64,128]{2,1,0:T(8,128)}, f32[36,64,128]{2,1,0:T(8,128)}, u32[]{:S(2)}, u32[]{:S(2)}) collective-permute-start(f32[36,64,128]{2,1,0:T(8,128)} %collective-permute-done.2.c_b), channel_id=1, source_target_pairs={{0,2},{1,31},{2,4},{3,1},{4,6},{5,3},{6,8},{7,5},{8,10},{9,7},{10,... | collective-permute-start | bytes 3538952 | tf_op jit(solution)/shard_map/ppermute | solution.py:380
  20.4 1.9 collective-permute-start
  22.4 2.4 collective-permute-start.1
  24.8 0.7 copy.19.owner
  25.5 4.6 %collective-permute-done.before = f32[3,1,32,128]{3,2,1,0:T(8,128)S(1)} collective-permute-done((f32[3,1,32,128]{3,2,1,0:T(8,128)S(1)}, f32[3,1,32,128]{3,2,1,0:T(8,128)S(1)}, u32[]{:S(2)}, u32[]{:S(2)}) %collective-permute-start) | collective-permute-done | bytes 49184 | tf_op jit(solution)/shard_map/ppermute | solution.py:380
  30.0 3.4 %collective-permute-done.1.after = f32[3,1,32,128]{3,2,1,0:T(8,128)S(1)} collective-permute-done((f32[3,1,32,128]{3,2,1,0:T(8,128)S(1)}, f32[3,1,32,128]{3,2,1,0:T(8,128)S(1)}, u32[]{:S(2)}, u32[]{:S(2)}) %collective-permute-start.1) | collective-permute-done | bytes 49184 | tf_op jit(solution)/shard_map/ppermute | solution.py:380
  33.4 0.6 copy-done.28
  34.0 1.7 strain.1
  35.7 0.7 slice.11
  36.4 0.6 broadcast_in_dim.20
  37.1 13.6 %all-to-all-start = ((f32[128,1,128]{2,1,0:T(1,128)}), f32[128,1,128]{2,1,0:T(1,128)S(1)}, u32[]{:S(2)}, u32[]{:S(2)}) async-start(f32[128,1,128]{2,1,0:T(1,128)} %bitcast.1), calls=%async_computation | async-start | bytes 131072 | tf_op jit(solution)/shard_map/all_to_all | solution.py:407
  50.7 9.5 %all-to-all-done = f32[128,1,128]{2,1,0:T(1,128)S(1)} async-done(((f32[128,1,128]{2,1,0:T(1,128)}), f32[128,1,128]{2,1,0:T(1,128)S(1)}, u32[]{:S(2)}, u32[]{:S(2)}) %all-to-all-start) | async-done | bytes 65568 | tf_op jit(solution)/shard_map/all_to_all | solution.py:407
  60.2 0.6 constant_dynamic-slice_fusion.ebar
  60.8 1.5 copy-done
  62.3 9.5 %first.1 = (f32[12,64,128]{2,1,0:T(8,128)}, f32[12,64,128]{2,1,0:T(8,128)}, f32[12,64,128]{2,1,0:T(8,128)}, f32[12,64,128]{2,1,0:T(8,128)}) custom-call(f32[2,128]{1,0:T(2,128)} %constant_dynamic-slice_fusion.ebar, f32[36,64,128]{2,1,0:T(8,128)} %get-tuple-element.28.c_a, f32[36,64,128]{2,1,0:T(8,128)} %collective-permute-done.2.c_b, ...), custom_call_target="tpu_custom_call" | custom-call | tf_op jit(solution)/shard_map/first/pallas_call | solution.py:416
  71.8 7.2 %settle.4 = (f32[12,64,128]{2,1,0:T(8,128)}, f32[12,64,128]{2,1,0:T(8,128)}) custom-call(f32[12,64,128]{2,1,0:T(8,128)} %get-tuple-element.30.e_a, f32[12,64,128]{2,1,0:T(8,128)} %get-tuple-element.31.e_b, f32[12,64,128]{2,1,0:T(8,128)} %get-tuple-element.32.sig_a, f32[12,64,128]{2,1,0:T(8,128)} %get-tuple-element.33.sig_b, ...), custom_call_target="tpu_custom_call" | custom-call | tf_op jit(solution)/shard_map/settle/pallas_call | solution.py:422
  79.0 1.6 collective-permute-start.8
  80.6 4.8 %collective-permute-start.6 = (f32[12,64,128]{2,1,0:T(8,128)S(1)}, f32[12,64,128]{2,1,0:T(8,128)S(1)}, u32[]{:S(2)}, u32[]{:S(2)}) collective-permute-start(f32[12,64,128]{2,1,0:T(8,128)S(1)} %copy-done.8), channel_id=1, source_target_pairs={{0,2},{1,31},{2,4},{3,1},{4,6},{5,3},{6,8},{7,5},{8,10},{9,7},{10,... | collective-permute-start | bytes 1179656 | tf_op jit(solution)/shard_map/ppermute | solution.py:380
  85.4 3.1 %collective-permute-done.8.fr_a = f32[12,64,128]{2,1,0:T(8,128)S(1)} collective-permute-done((f32[12,64,128]{2,1,0:T(8,128)}, f32[12,64,128]{2,1,0:T(8,128)S(1)}, u32[]{:S(2)}, u32[]{:S(2)}) %collective-permute-start.8) | collective-permute-done | bytes 393248 | tf_op jit(solution)/shard_map/ppermute | solution.py:380
  88.5 6.7 %collective-permute-done.9.fr_b = f32[12,64,128]{2,1,0:T(8,128)S(1)} collective-permute-done((f32[12,64,128]{2,1,0:T(8,128)}, f32[12,64,128]{2,1,0:T(8,128)S(1)}, u32[]{:S(2)}, u32[]{:S(2)}) %collective-permute-start.9) | collective-permute-done | bytes 393248 | tf_op jit(solution)/shard_map/ppermute | solution.py:380
  95.2 1.7 collective-permute-done.6.fs_a
  96.9 6.1 %collective-permute-done.7.fs_b = f32[12,64,128]{2,1,0:T(8,128)S(1)} collective-permute-done((f32[12,64,128]{2,1,0:T(8,128)S(1)}, f32[12,64,128]{2,1,0:T(8,128)S(1)}, u32[]{:S(2)}, u32[]{:S(2)}) %collective-permute-start.7) | collective-permute-done | bytes 393248 | tf_op jit(solution)/shard_map/ppermute | solution.py:380
  103.0 0.7 copy-done.23
  103.8 10.8 %pair.3 = (f32[12,64,128]{2,1,0:T(8,128)}, f32[12,64,128]{2,1,0:T(8,128)}, f32[12,64,128]{2,1,0:T(8,128)}, f32[12,64,128]{2,1,0:T(8,128)}) custom-call(f32[12,64,128]{2,1,0:T(8,128)} %get-tuple-element.34.r_a, f32[12,64,128]{2,1,0:T(8,128)} %get-tuple-element.35.r_b, f32[12,64,128]{2,1,0:T(8,128)} %get-tuple-element.32.sig_a, ...), custom_call_target="tpu_custom_call" | custom-call | tf_op jit(solution)/shard_map/pair/pallas_call | solution.py:427
  114.6 7.2 %settle.5 = (f32[12,64,128]{2,1,0:T(8,128)}, f32[12,64,128]{2,1,0:T(8,128)}) custom-call(f32[12,64,128]{2,1,0:T(8,128)} %get-tuple-element.36.e_a, f32[12,64,128]{2,1,0:T(8,128)} %get-tuple-element.37.e_b, f32[12,64,128]{2,1,0:T(8,128)} %get-tuple-element.38.sig_a, f32[12,64,128]{2,1,0:T(8,128)} %get-tuple-element.39.sig_b, ...), custom_call_target="tpu_custom_call" | custom-call | tf_op jit(solution)/shard_map/settle/pallas_call | solution.py:422
  121.8 1.5 collective-permute-start.13
  123.3 3.3 %collective-permute-start.10 = (f32[12,64,128]{2,1,0:T(8,128)S(1)}, f32[12,64,128]{2,1,0:T(8,128)S(1)}, u32[]{:S(2)}, u32[]{:S(2)}) collective-permute-start(f32[12,64,128]{2,1,0:T(8,128)S(1)} %copy-done.4), channel_id=1, source_target_pairs={{0,2},{1,31},{2,4},{3,1},{4,6},{5,3},{6,8},{7,5},{8,10},{9,7},{10,... | collective-permute-start | bytes 1179656 | tf_op jit(solution)/shard_map/ppermute | solution.py:380
  126.6 4.9 %collective-permute-done.12.fr_a = f32[12,64,128]{2,1,0:T(8,128)S(1)} collective-permute-done((f32[12,64,128]{2,1,0:T(8,128)}, f32[12,64,128]{2,1,0:T(8,128)S(1)}, u32[]{:S(2)}, u32[]{:S(2)}) %collective-permute-start.12) | collective-permute-done | bytes 393248 | tf_op jit(solution)/shard_map/ppermute | solution.py:380
  131.5 3.3 %collective-permute-done.13.fr_b = f32[12,64,128]{2,1,0:T(8,128)S(1)} collective-permute-done((f32[12,64,128]{2,1,0:T(8,128)}, f32[12,64,128]{2,1,0:T(8,128)S(1)}, u32[]{:S(2)}, u32[]{:S(2)}) %collective-permute-start.13) | collective-permute-done | bytes 393248 | tf_op jit(solution)/shard_map/ppermute | solution.py:380
  134.9 5.1 %collective-permute-done.10.fs_a = f32[12,64,128]{2,1,0:T(8,128)S(1)} collective-permute-done((f32[12,64,128]{2,1,0:T(8,128)S(1)}, f32[12,64,128]{2,1,0:T(8,128)S(1)}, u32[]{:S(2)}, u32[]{:S(2)}) %collective-permute-start.10) | collective-permute-done | bytes 393248 | tf_op jit(solution)/shard_map/ppermute | solution.py:380
  140.0 3.3 %collective-permute-done.11.fs_b = f32[12,64,128]{2,1,0:T(8,128)S(1)} collective-permute-done((f32[12,64,128]{2,1,0:T(8,128)S(1)}, f32[12,64,128]{2,1,0:T(8,128)S(1)}, u32[]{:S(2)}, u32[]{:S(2)}) %collective-permute-start.11) | collective-permute-done | bytes 393248 | tf_op jit(solution)/shard_map/ppermute | solution.py:380
  143.3 0.7 copy-done.24
  144.1 10.8 %pair.4 = (f32[12,64,128]{2,1,0:T(8,128)}, f32[12,64,128]{2,1,0:T(8,128)}, f32[12,64,128]{2,1,0:T(8,128)}, f32[12,64,128]{2,1,0:T(8,128)}) custom-call(f32[12,64,128]{2,1,0:T(8,128)} %get-tuple-element.40.r_a, f32[12,64,128]{2,1,0:T(8,128)} %get-tuple-element.41.r_b, f32[12,64,128]{2,1,0:T(8,128)} %get-tuple-element.38.sig_a, ...), custom_call_target="tpu_custom_call" | custom-call | tf_op jit(solution)/shard_map/pair/pallas_call | solution.py:427
  154.8 7.2 %settle.6 = (f32[12,64,128]{2,1,0:T(8,128)}, f32[12,64,128]{2,1,0:T(8,128)}) custom-call(f32[12,64,128]{2,1,0:T(8,128)} %get-tuple-element.42.e_a, f32[12,64,128]{2,1,0:T(8,128)} %get-tuple-element.43.e_b, f32[12,64,128]{2,1,0:T(8,128)} %get-tuple-element.44.sig_a, f32[12,64,128]{2,1,0:T(8,128)} %get-tuple-element.45.sig_b, ...), custom_call_target="tpu_custom_call" | custom-call | tf_op jit(solution)/shard_map/settle/pallas_call | solution.py:422
  162.1 1.5 collective-permute-start.17
  163.5 3.3 %collective-permute-start.14 = (f32[12,64,128]{2,1,0:T(8,128)S(1)}, f32[12,64,128]{2,1,0:T(8,128)S(1)}, u32[]{:S(2)}, u32[]{:S(2)}) collective-permute-start(f32[12,64,128]{2,1,0:T(8,128)S(1)} %copy-done.6), channel_id=1, source_target_pairs={{0,2},{1,31},{2,4},{3,1},{4,6},{5,3},{6,8},{7,5},{8,10},{9,7},{10,... | collective-permute-start | bytes 1179656 | tf_op jit(solution)/shard_map/ppermute | solution.py:380
  166.9 3.3 %collective-permute-done.16.fr_a = f32[12,64,128]{2,1,0:T(8,128)S(1)} collective-permute-done((f32[12,64,128]{2,1,0:T(8,128)}, f32[12,64,128]{2,1,0:T(8,128)S(1)}, u32[]{:S(2)}, u32[]{:S(2)}) %collective-permute-start.16) | collective-permute-done | bytes 393248 | tf_op jit(solution)/shard_map/ppermute | solution.py:380
  170.2 3.3 %collective-permute-done.17.fr_b = f32[12,64,128]{2,1,0:T(8,128)S(1)} collective-permute-done((f32[12,64,128]{2,1,0:T(8,128)}, f32[12,64,128]{2,1,0:T(8,128)S(1)}, u32[]{:S(2)}, u32[]{:S(2)}) %collective-permute-start.17) | collective-permute-done | bytes 393248 | tf_op jit(solution)/shard_map/ppermute | solution.py:380
  173.5 5.1 %collective-permute-done.14.fs_a = f32[12,64,128]{2,1,0:T(8,128)S(1)} collective-permute-done((f32[12,64,128]{2,1,0:T(8,128)S(1)}, f32[12,64,128]{2,1,0:T(8,128)S(1)}, u32[]{:S(2)}, u32[]{:S(2)}) %collective-permute-start.14) | collective-permute-done | bytes 393248 | tf_op jit(solution)/shard_map/ppermute | solution.py:380
  178.6 3.3 %collective-permute-done.15.fs_b = f32[12,64,128]{2,1,0:T(8,128)S(1)} collective-permute-done((f32[12,64,128]{2,1,0:T(8,128)S(1)}, f32[12,64,128]{2,1,0:T(8,128)S(1)}, u32[]{:S(2)}, u32[]{:S(2)}) %collective-permute-start.15) | collective-permute-done | bytes 393248 | tf_op jit(solution)/shard_map/ppermute | solution.py:380
  181.9 0.7 copy-done.25
  182.7 10.8 %pair.5 = (f32[12,64,128]{2,1,0:T(8,128)}, f32[12,64,128]{2,1,0:T(8,128)}, f32[12,64,128]{2,1,0:T(8,128)}, f32[12,64,128]{2,1,0:T(8,128)}) custom-call(f32[12,64,128]{2,1,0:T(8,128)} %get-tuple-element.46.r_a, f32[12,64,128]{2,1,0:T(8,128)} %get-tuple-element.47.r_b, f32[12,64,128]{2,1,0:T(8,128)} %get-tuple-element.44.sig_a, ...), custom_call_target="tpu_custom_call" | custom-call | tf_op jit(solution)/shard_map/pair/pallas_call | solution.py:427
  193.5 7.2 %settle.7 = (f32[12,64,128]{2,1,0:T(8,128)}, f32[12,64,128]{2,1,0:T(8,128)}) custom-call(f32[12,64,128]{2,1,0:T(8,128)} %get-tuple-element.48.e_a, f32[12,64,128]{2,1,0:T(8,128)} %get-tuple-element.49.e_b, f32[12,64,128]{2,1,0:T(8,128)} %get-tuple-element.50.sig_a, f32[12,64,128]{2,1,0:T(8,128)} %get-tuple-element.51.sig_b, ...), custom_call_target="tpu_custom_call" | custom-call | tf_op jit(solution)/shard_map/settle/pallas_call | solution.py:422
  200.7 1.5 collective-permute-start.21
  202.1 3.4 %collective-permute-start.18 = (f32[12,64,128]{2,1,0:T(8,128)S(1)}, f32[12,64,128]{2,1,0:T(8,128)S(1)}, u32[]{:S(2)}, u32[]{:S(2)}) collective-permute-start(f32[12,64,128]{2,1,0:T(8,128)S(1)} %copy-done.2), channel_id=1, source_target_pairs={{0,2},{1,31},{2,4},{3,1},{4,6},{5,3},{6,8},{7,5},{8,10},{9,7},{10,... | collective-permute-start | bytes 1179656 | tf_op jit(solution)/shard_map/ppermute | solution.py:380
  205.5 2.0 collective-permute-done.20.fr_a
  207.5 3.4 %collective-permute-done.21.fr_b = f32[12,64,128]{2,1,0:T(8,128)S(1)} collective-permute-done((f32[12,64,128]{2,1,0:T(8,128)}, f32[12,64,128]{2,1,0:T(8,128)S(1)}, u32[]{:S(2)}, u32[]{:S(2)}) %collective-permute-start.21) | collective-permute-done | bytes 393248 | tf_op jit(solution)/shard_map/ppermute | solution.py:380
  210.9 4.6 %collective-permute-done.18.fs_a = f32[12,64,128]{2,1,0:T(8,128)S(1)} collective-permute-done((f32[12,64,128]{2,1,0:T(8,128)S(1)}, f32[12,64,128]{2,1,0:T(8,128)S(1)}, u32[]{:S(2)}, u32[]{:S(2)}) %collective-permute-start.18) | collective-permute-done | bytes 393248 | tf_op jit(solution)/shard_map/ppermute | solution.py:380
  215.4 4.3 %collective-permute-done.19.fs_b = f32[12,64,128]{2,1,0:T(8,128)S(1)} collective-permute-done((f32[12,64,128]{2,1,0:T(8,128)S(1)}, f32[12,64,128]{2,1,0:T(8,128)S(1)}, u32[]{:S(2)}, u32[]{:S(2)}) %collective-permute-start.19) | collective-permute-done | bytes 393248 | tf_op jit(solution)/shard_map/ppermute | solution.py:380
  219.8 0.8 copy-done.22
  220.6 14.7 %last.1 = f32[12,8,128]{2,1,0:T(8,128)} custom-call(f32[12,64,128]{2,1,0:T(8,128)} %get-tuple-element.52.r_a, f32[12,64,128]{2,1,0:T(8,128)} %get-tuple-element.53.r_b, f32[12,64,128]{2,1,0:T(8,128)} %get-tuple-element.50.sig_a, f32[12,64,128]{2,1,0:T(8,128)} %get-tuple-element.51.sig_b, f32[12,64,128]{2,1,0:T(8,128)} %copy-done.18, ...), custom_call_target="tpu_custom_call" | custom-call | tf_op jit(solution)/shard_map/last/pallas_call | solution.py:429
  235.2 1.0 reduce_sum.19
  236.3 0.6 broadcast_in_dim.22
  236.9 8.9 %all-to-all-start.1 = ((f32[128,1,128]{2,1,0:T(1,128)}), f32[128,1,128]{2,1,0:T(1,128)S(1)}, u32[]{:S(2)}, u32[]{:S(2)}) async-start(f32[128,1,128]{2,1,0:T(1,128)} %bitcast.9), calls=%async_computation.1 | async-start | bytes 131072 | tf_op jit(solution)/shard_map/all_to_all | solution.py:436
  246.0 0.6 pad.9.loads
  246.6 6.8 %stencil.1.base = f32[3,2,32,128]{3,2,1,0:T(8,128)} custom-call(bf16[27,3,3,2,32,128]{5,4,3,2,1,0:T(8,128)(2,1)} %blocks.1, f32[3,2,32,128]{3,2,1,0:T(8,128)} %disp.3, f32[3,1,32,128]{3,2,1,0:T(8,128)} %copy-done.27, f32[3,1,32,128]{3,2,1,0:T(8,128)} %copy-done.28, f32[3,2,32,128]{3,2,1,0:T(8,128)} %external.1), custom_call_target="tpu_custom_call" | custom-call | tf_op jit(solution)/shard_map/stencil/pallas_call | solution.py:316
  253.4 2.2 all-to-all-done.1
  255.6 0.6 copy-done.26
  256.2 1.7 final.1
  (72 shorter events, 0.3 us)
Async XLA Ops:
  0.6 19.8 %copy-start.9 = (f32[3,2,32,128]{3,2,1,0:T(8,128)S(1)}, f32[3,2,32,128]{3,2,1,0:T(8,128)}, u32[]{:S(2)}) copy-start(f32[3,2,32,128]{3,2,1,0:T(8,128)} %disp.3) | copy-start | bytes 294916
  0.6 24.1 %copy-start.30 = (s32[2,1]{0,1:T(1,128)S(1)}, s32[2,1]{0,1:T(1,128)}, u32[]{:S(2)}) copy-start(s32[2,1]{0,1:T(1,128)} %param.16) | copy-start | bytes 28
  7.4 53.4 %collective-permute-start.5 = (f32[84,64,128]{2,1,0:T(8,128)}, f32[84,64,128]{2,1,0:T(8,128)S(1)}, u32[]{:S(2)}, u32[]{:S(2)}) collective-permute-start(f32[84,64,128]{2,1,0:T(8,128)} %get-tuple-element.29.s_a), channel_id=1, source_target_pairs={{0,1},{1,0},{2,3},{3,2},{4,5},{5,4},{6,7},{7,6},{8,9},{9,8},{10,11... | collective-permute-start | bytes 8257544 | tf_op jit(solution)/shard_map/ppermute | solution.py:380
  8.8 6.6 %collective-permute-start.2 = (f32[36,64,128]{2,1,0:T(8,128)}, f32[36,64,128]{2,1,0:T(8,128)}, u32[]{:S(2)}, u32[]{:S(2)}) collective-permute-start(f32[36,64,128]{2,1,0:T(8,128)} %get-tuple-element.28.c_a), channel_id=1, source_target_pairs={{0,1},{1,0},{2,3},{3,2},{4,5},{5,4},{6,7},{7,6},{8,9},{9,8},{10,11... | collective-permute-start | bytes 3538952 | tf_op jit(solution)/shard_map/ppermute | solution.py:380
  8.9 51.9 %collective-permute-start.4 = (f32[36,64,128]{2,1,0:T(8,128)}, f32[36,64,128]{2,1,0:T(8,128)}, u32[]{:S(2)}, u32[]{:S(2)}) collective-permute-start(f32[36,64,128]{2,1,0:T(8,128)} %get-tuple-element.28.c_a), channel_id=1, source_target_pairs={{0,30},{1,3},{2,0},{3,5},{4,2},{5,7},{6,4},{7,9},{8,6},{9,11},{10,... | collective-permute-start | bytes 3538952 | tf_op jit(solution)/shard_map/ppermute | solution.py:380
  15.4 45.4 %collective-permute-start.3 = (f32[36,64,128]{2,1,0:T(8,128)}, f32[36,64,128]{2,1,0:T(8,128)}, u32[]{:S(2)}, u32[]{:S(2)}) collective-permute-start(f32[36,64,128]{2,1,0:T(8,128)} %collective-permute-done.2.c_b), channel_id=1, source_target_pairs={{0,2},{1,31},{2,4},{3,1},{4,6},{5,3},{6,8},{7,5},{8,10},{9,7},{10,... | collective-permute-start | bytes 3538952 | tf_op jit(solution)/shard_map/ppermute | solution.py:380
  20.4 9.6 %collective-permute-start = (f32[3,1,32,128]{3,2,1,0:T(8,128)S(1)}, f32[3,1,32,128]{3,2,1,0:T(8,128)S(1)}, u32[]{:S(2)}, u32[]{:S(2)}) collective-permute-start(f32[3,1,32,128]{3,2,1,0:T(8,128)S(1)} %get-tuple-element.55), channel_id=1, source_target_pairs={{0,1},{1,2},{2,3},{3,4},{4,5},{5,6},{6,7},{7,8},{8,9},{9,10},{10,1... | collective-permute-start | bytes 147464 | tf_op jit(solution)/shard_map/ppermute | solution.py:380
  22.4 11.0 %collective-permute-start.1 = (f32[3,1,32,128]{3,2,1,0:T(8,128)S(1)}, f32[3,1,32,128]{3,2,1,0:T(8,128)S(1)}, u32[]{:S(2)}, u32[]{:S(2)}) collective-permute-start(f32[3,1,32,128]{3,2,1,0:T(8,128)S(1)} %get-tuple-element.54), channel_id=1, source_target_pairs={{1,0},{2,1},{3,2},{4,3},{5,4},{6,5},{7,6},{8,7},{9,8},{10,9},{11,1... | collective-permute-start | bytes 147464 | tf_op jit(solution)/shard_map/ppermute | solution.py:380
  30.0 3.4 %copy-start.27 = (f32[3,1,32,128]{3,2,1,0:T(8,128)}, f32[3,1,32,128]{3,2,1,0:T(8,128)S(1)}, u32[]{:S(2)}) copy-start(f32[3,1,32,128]{3,2,1,0:T(8,128)S(1)} %collective-permute-done.before) | copy-start | bytes 147460
  33.4 0.6 copy-start.28
  37.1 23.1 %all-to-all-start = ((f32[128,1,128]{2,1,0:T(1,128)}), f32[128,1,128]{2,1,0:T(1,128)S(1)}, u32[]{:S(2)}, u32[]{:S(2)}) async-start(f32[128,1,128]{2,1,0:T(1,128)} %bitcast.1), calls=%async_computation | async-start | bytes 131072 | tf_op jit(solution)/shard_map/all_to_all | solution.py:407
  60.8 1.5 copy-start
  71.8 8.8 %copy-start.8 = (f32[12,64,128]{2,1,0:T(8,128)S(1)}, f32[12,64,128]{2,1,0:T(8,128)}, u32[]{:S(2)}) copy-start(f32[12,64,128]{2,1,0:T(8,128)} %get-tuple-element.33.sig_b) | copy-start | bytes 1179652
  71.8 13.6 %copy-start.7 = (f32[12,64,128]{2,1,0:T(8,128)S(1)}, f32[12,64,128]{2,1,0:T(8,128)}, u32[]{:S(2)}) copy-start(f32[12,64,128]{2,1,0:T(8,128)} %get-tuple-element.32.sig_a) | copy-start | bytes 1179652
  79.0 9.5 %collective-permute-start.8 = (f32[12,64,128]{2,1,0:T(8,128)}, f32[12,64,128]{2,1,0:T(8,128)S(1)}, u32[]{:S(2)}, u32[]{:S(2)}) collective-permute-start(f32[12,64,128]{2,1,0:T(8,128)} %get-tuple-element.35.r_b), channel_id=1, source_target_pairs={{0,2},{1,31},{2,4},{3,1},{4,6},{5,3},{6,8},{7,5},{8,10},{9,7},{10,... | collective-permute-start | bytes 1179656 | tf_op jit(solution)/shard_map/ppermute | solution.py:380
  80.6 14.7 %collective-permute-start.9 = (f32[12,64,128]{2,1,0:T(8,128)}, f32[12,64,128]{2,1,0:T(8,128)S(1)}, u32[]{:S(2)}, u32[]{:S(2)}) collective-permute-start(f32[12,64,128]{2,1,0:T(8,128)} %get-tuple-element.34.r_a), channel_id=1, source_target_pairs={{0,30},{1,3},{2,0},{3,5},{4,2},{5,7},{6,4},{7,9},{8,6},{9,11},{10,... | collective-permute-start | bytes 1179656 | tf_op jit(solution)/shard_map/ppermute | solution.py:380
  80.6 16.3 %collective-permute-start.6 = (f32[12,64,128]{2,1,0:T(8,128)S(1)}, f32[12,64,128]{2,1,0:T(8,128)S(1)}, u32[]{:S(2)}, u32[]{:S(2)}) collective-permute-start(f32[12,64,128]{2,1,0:T(8,128)S(1)} %copy-done.8), channel_id=1, source_target_pairs={{0,2},{1,31},{2,4},{3,1},{4,6},{5,3},{6,8},{7,5},{8,10},{9,7},{10,... | collective-permute-start | bytes 1179656 | tf_op jit(solution)/shard_map/ppermute | solution.py:380
  85.4 17.7 %collective-permute-start.7 = (f32[12,64,128]{2,1,0:T(8,128)S(1)}, f32[12,64,128]{2,1,0:T(8,128)S(1)}, u32[]{:S(2)}, u32[]{:S(2)}) collective-permute-start(f32[12,64,128]{2,1,0:T(8,128)S(1)} %copy-done.7), channel_id=1, source_target_pairs={{0,30},{1,3},{2,0},{3,5},{4,2},{5,7},{6,4},{7,9},{8,6},{9,11},{10,... | collective-permute-start | bytes 1179656 | tf_op jit(solution)/shard_map/ppermute | solution.py:380
  88.5 14.5 %copy-start.11 = (f32[12,64,128]{2,1,0:T(8,128)}, f32[12,64,128]{2,1,0:T(8,128)S(1)}, u32[]{:S(2)}) copy-start(f32[12,64,128]{2,1,0:T(8,128)S(1)} %collective-permute-done.8.fr_a) | copy-start | bytes 1179652
  95.2 7.8 %copy-start.15 = (f32[12,64,128]{2,1,0:T(8,128)}, f32[12,64,128]{2,1,0:T(8,128)S(1)}, u32[]{:S(2)}) copy-start(f32[12,64,128]{2,1,0:T(8,128)S(1)} %collective-permute-done.9.fr_b) | copy-start | bytes 1179652
  96.9 6.1 %copy-start.19 = (f32[12,64,128]{2,1,0:T(8,128)}, f32[12,64,128]{2,1,0:T(8,128)S(1)}, u32[]{:S(2)}) copy-start(f32[12,64,128]{2,1,0:T(8,128)S(1)} %collective-permute-done.6.fs_a) | copy-start | bytes 1179652
  103.0 0.8 copy-start.23
  114.6 8.7 %copy-start.4 = (f32[12,64,128]{2,1,0:T(8,128)S(1)}, f32[12,64,128]{2,1,0:T(8,128)}, u32[]{:S(2)}) copy-start(f32[12,64,128]{2,1,0:T(8,128)} %get-tuple-element.39.sig_b) | copy-start | bytes 1179652
  114.6 12.0 %copy-start.3 = (f32[12,64,128]{2,1,0:T(8,128)S(1)}, f32[12,64,128]{2,1,0:T(8,128)}, u32[]{:S(2)}) copy-start(f32[12,64,128]{2,1,0:T(8,128)} %get-tuple-element.38.sig_a) | copy-start | bytes 1179652
  121.8 9.7 %collective-permute-start.12 = (f32[12,64,128]{2,1,0:T(8,128)}, f32[12,64,128]{2,1,0:T(8,128)S(1)}, u32[]{:S(2)}, u32[]{:S(2)}) collective-permute-start(f32[12,64,128]{2,1,0:T(8,128)} %get-tuple-element.41.r_b), channel_id=1, source_target_pairs={{0,2},{1,31},{2,4},{3,1},{4,6},{5,3},{6,8},{7,5},{8,10},{9,7},{10,... | collective-permute-start | bytes 1179656 | tf_op jit(solution)/shard_map/ppermute | solution.py:380
  121.8 13.1 %collective-permute-start.13 = (f32[12,64,128]{2,1,0:T(8,128)}, f32[12,64,128]{2,1,0:T(8,128)S(1)}, u32[]{:S(2)}, u32[]{:S(2)}) collective-permute-start(f32[12,64,128]{2,1,0:T(8,128)} %get-tuple-element.40.r_a), channel_id=1, source_target_pairs={{0,30},{1,3},{2,0},{3,5},{4,2},{5,7},{6,4},{7,9},{8,6},{9,11},{10,... | collective-permute-start | bytes 1179656 | tf_op jit(solution)/shard_map/ppermute | solution.py:380
  123.3 16.7 %collective-permute-start.10 = (f32[12,64,128]{2,1,0:T(8,128)S(1)}, f32[12,64,128]{2,1,0:T(8,128)S(1)}, u32[]{:S(2)}, u32[]{:S(2)}) collective-permute-start(f32[12,64,128]{2,1,0:T(8,128)S(1)} %copy-done.4), channel_id=1, source_target_pairs={{0,2},{1,31},{2,4},{3,1},{4,6},{5,3},{6,8},{7,5},{8,10},{9,7},{10,... | collective-permute-start | bytes 1179656 | tf_op jit(solution)/shard_map/ppermute | solution.py:380
  126.6 16.7 %collective-permute-start.11 = (f32[12,64,128]{2,1,0:T(8,128)S(1)}, f32[12,64,128]{2,1,0:T(8,128)S(1)}, u32[]{:S(2)}, u32[]{:S(2)}) collective-permute-start(f32[12,64,128]{2,1,0:T(8,128)S(1)} %copy-done.3), channel_id=1, source_target_pairs={{0,30},{1,3},{2,0},{3,5},{4,2},{5,7},{6,4},{7,9},{8,6},{9,11},{10,... | collective-permute-start | bytes 1179656 | tf_op jit(solution)/shard_map/ppermute | solution.py:380
  131.5 11.8 %copy-start.12 = (f32[12,64,128]{2,1,0:T(8,128)}, f32[12,64,128]{2,1,0:T(8,128)S(1)}, u32[]{:S(2)}) copy-start(f32[12,64,128]{2,1,0:T(8,128)S(1)} %collective-permute-done.12.fr_a) | copy-start | bytes 1179652
  134.9 8.4 %copy-start.16 = (f32[12,64,128]{2,1,0:T(8,128)}, f32[12,64,128]{2,1,0:T(8,128)S(1)}, u32[]{:S(2)}) copy-start(f32[12,64,128]{2,1,0:T(8,128)S(1)} %collective-permute-done.13.fr_b) | copy-start | bytes 1179652
  140.0 3.3 %copy-start.20 = (f32[12,64,128]{2,1,0:T(8,128)}, f32[12,64,128]{2,1,0:T(8,128)S(1)}, u32[]{:S(2)}) copy-start(f32[12,64,128]{2,1,0:T(8,128)S(1)} %collective-permute-done.10.fs_a) | copy-start | bytes 1179652
  143.3 0.8 copy-start.24
  154.8 8.7 %copy-start.6 = (f32[12,64,128]{2,1,0:T(8,128)S(1)}, f32[12,64,128]{2,1,0:T(8,128)}, u32[]{:S(2)}) copy-start(f32[12,64,128]{2,1,0:T(8,128)} %get-tuple-element.45.sig_b) | copy-start | bytes 1179652
  154.8 12.0 %copy-start.5 = (f32[12,64,128]{2,1,0:T(8,128)S(1)}, f32[12,64,128]{2,1,0:T(8,128)}, u32[]{:S(2)}) copy-start(f32[12,64,128]{2,1,0:T(8,128)} %get-tuple-element.44.sig_a) | copy-start | bytes 1179652
  162.1 8.1 %collective-permute-start.16 = (f32[12,64,128]{2,1,0:T(8,128)}, f32[12,64,128]{2,1,0:T(8,128)S(1)}, u32[]{:S(2)}, u32[]{:S(2)}) collective-permute-start(f32[12,64,128]{2,1,0:T(8,128)} %get-tuple-element.47.r_b), channel_id=1, source_target_pairs={{0,2},{1,31},{2,4},{3,1},{4,6},{5,3},{6,8},{7,5},{8,10},{9,7},{10,... | collective-permute-start | bytes 1179656 | tf_op jit(solution)/shard_map/ppermute | solution.py:380
  162.1 11.4 %collective-permute-start.17 = (f32[12,64,128]{2,1,0:T(8,128)}, f32[12,64,128]{2,1,0:T(8,128)S(1)}, u32[]{:S(2)}, u32[]{:S(2)}) collective-permute-start(f32[12,64,128]{2,1,0:T(8,128)} %get-tuple-element.46.r_a), channel_id=1, source_target_pairs={{0,30},{1,3},{2,0},{3,5},{4,2},{5,7},{6,4},{7,9},{8,6},{9,11},{10,... | collective-permute-start | bytes 1179656 | tf_op jit(solution)/shard_map/ppermute | solution.py:380
  163.5 15.0 %collective-permute-start.14 = (f32[12,64,128]{2,1,0:T(8,128)S(1)}, f32[12,64,128]{2,1,0:T(8,128)S(1)}, u32[]{:S(2)}, u32[]{:S(2)}) collective-permute-start(f32[12,64,128]{2,1,0:T(8,128)S(1)} %copy-done.6), channel_id=1, source_target_pairs={{0,2},{1,31},{2,4},{3,1},{4,6},{5,3},{6,8},{7,5},{8,10},{9,7},{10,... | collective-permute-start | bytes 1179656 | tf_op jit(solution)/shard_map/ppermute | solution.py:380
  166.9 15.0 %collective-permute-start.15 = (f32[12,64,128]{2,1,0:T(8,128)S(1)}, f32[12,64,128]{2,1,0:T(8,128)S(1)}, u32[]{:S(2)}, u32[]{:S(2)}) collective-permute-start(f32[12,64,128]{2,1,0:T(8,128)S(1)} %copy-done.5), channel_id=1, source_target_pairs={{0,30},{1,3},{2,0},{3,5},{4,2},{5,7},{6,4},{7,9},{8,6},{9,11},{10,... | collective-permute-start | bytes 1179656 | tf_op jit(solution)/shard_map/ppermute | solution.py:380
  170.2 11.8 %copy-start.13 = (f32[12,64,128]{2,1,0:T(8,128)}, f32[12,64,128]{2,1,0:T(8,128)S(1)}, u32[]{:S(2)}) copy-start(f32[12,64,128]{2,1,0:T(8,128)S(1)} %collective-permute-done.16.fr_a) | copy-start | bytes 1179652
  173.5 8.4 %copy-start.17 = (f32[12,64,128]{2,1,0:T(8,128)}, f32[12,64,128]{2,1,0:T(8,128)S(1)}, u32[]{:S(2)}) copy-start(f32[12,64,128]{2,1,0:T(8,128)S(1)} %collective-permute-done.17.fr_b) | copy-start | bytes 1179652
  178.6 3.3 %copy-start.21 = (f32[12,64,128]{2,1,0:T(8,128)}, f32[12,64,128]{2,1,0:T(8,128)S(1)}, u32[]{:S(2)}) copy-start(f32[12,64,128]{2,1,0:T(8,128)S(1)} %collective-permute-done.14.fs_a) | copy-start | bytes 1179652
  181.9 0.8 copy-start.25
  193.5 8.7 %copy-start.2 = (f32[12,64,128]{2,1,0:T(8,128)S(1)}, f32[12,64,128]{2,1,0:T(8,128)}, u32[]{:S(2)}) copy-start(f32[12,64,128]{2,1,0:T(8,128)} %get-tuple-element.51.sig_b) | copy-start | bytes 1179652
  193.5 12.1 %copy-start.1 = (f32[12,64,128]{2,1,0:T(8,128)S(1)}, f32[12,64,128]{2,1,0:T(8,128)}, u32[]{:S(2)}) copy-start(f32[12,64,128]{2,1,0:T(8,128)} %get-tuple-element.50.sig_a) | copy-start | bytes 1179652
  200.7 6.8 %collective-permute-start.20 = (f32[12,64,128]{2,1,0:T(8,128)}, f32[12,64,128]{2,1,0:T(8,128)S(1)}, u32[]{:S(2)}, u32[]{:S(2)}) collective-permute-start(f32[12,64,128]{2,1,0:T(8,128)} %get-tuple-element.53.r_b), channel_id=1, source_target_pairs={{0,2},{1,31},{2,4},{3,1},{4,6},{5,3},{6,8},{7,5},{8,10},{9,7},{10,... | collective-permute-start | bytes 1179656 | tf_op jit(solution)/shard_map/ppermute | solution.py:380
  200.7 45.2 %copy-start.29 = (f32[2,18]{1,0:T(2,128)S(1)}, f32[2,18]{1,0:T(2,128)}, u32[]{:S(2)}) copy-start(f32[2,18]{1,0:T(2,128)} %param.17) | copy-start | bytes 436
  200.7 10.2 %collective-permute-start.21 = (f32[12,64,128]{2,1,0:T(8,128)}, f32[12,64,128]{2,1,0:T(8,128)S(1)}, u32[]{:S(2)}, u32[]{:S(2)}) collective-permute-start(f32[12,64,128]{2,1,0:T(8,128)} %get-tuple-element.52.r_a), channel_id=1, source_target_pairs={{0,30},{1,3},{2,0},{3,5},{4,2},{5,7},{6,4},{7,9},{8,6},{9,11},{10,... | collective-permute-start | bytes 1179656 | tf_op jit(solution)/shard_map/ppermute | solution.py:380
  202.1 13.3 %collective-permute-start.18 = (f32[12,64,128]{2,1,0:T(8,128)S(1)}, f32[12,64,128]{2,1,0:T(8,128)S(1)}, u32[]{:S(2)}, u32[]{:S(2)}) collective-permute-start(f32[12,64,128]{2,1,0:T(8,128)S(1)} %copy-done.2), channel_id=1, source_target_pairs={{0,2},{1,31},{2,4},{3,1},{4,6},{5,3},{6,8},{7,5},{8,10},{9,7},{10,... | collective-permute-start | bytes 1179656 | tf_op jit(solution)/shard_map/ppermute | solution.py:380
  205.5 14.3 %collective-permute-start.19 = (f32[12,64,128]{2,1,0:T(8,128)S(1)}, f32[12,64,128]{2,1,0:T(8,128)S(1)}, u32[]{:S(2)}, u32[]{:S(2)}) collective-permute-start(f32[12,64,128]{2,1,0:T(8,128)S(1)} %copy-done.1), channel_id=1, source_target_pairs={{0,30},{1,3},{2,0},{3,5},{4,2},{5,7},{6,4},{7,9},{8,6},{9,11},{10,... | collective-permute-start | bytes 1179656 | tf_op jit(solution)/shard_map/ppermute | solution.py:380
  207.5 12.3 %copy-start.10 = (f32[12,64,128]{2,1,0:T(8,128)}, f32[12,64,128]{2,1,0:T(8,128)S(1)}, u32[]{:S(2)}) copy-start(f32[12,64,128]{2,1,0:T(8,128)S(1)} %collective-permute-done.20.fr_a) | copy-start | bytes 1179652
  210.9 8.9 %copy-start.14 = (f32[12,64,128]{2,1,0:T(8,128)}, f32[12,64,128]{2,1,0:T(8,128)S(1)}, u32[]{:S(2)}) copy-start(f32[12,64,128]{2,1,0:T(8,128)S(1)} %collective-permute-done.21.fr_b) | copy-start | bytes 1179652
  215.4 4.3 %copy-start.18 = (f32[12,64,128]{2,1,0:T(8,128)}, f32[12,64,128]{2,1,0:T(8,128)S(1)}, u32[]{:S(2)}) copy-start(f32[12,64,128]{2,1,0:T(8,128)S(1)} %collective-permute-done.18.fs_a) | copy-start | bytes 1179652
  219.8 0.8 copy-start.22
  236.9 18.6 %all-to-all-start.1 = ((f32[128,1,128]{2,1,0:T(1,128)}), f32[128,1,128]{2,1,0:T(1,128)S(1)}, u32[]{:S(2)}, u32[]{:S(2)}) async-start(f32[128,1,128]{2,1,0:T(1,128)} %bitcast.9), calls=%async_computation.1 | async-start | bytes 131072 | tf_op jit(solution)/shard_map/all_to_all | solution.py:436
  255.6 0.6 copy-start.26
where the time goes:
time: 258 us
  Pallas kernels  102 us (40%)
  waiting for transfers between devices  88.5 us (34%)
  starting transfers between devices  55.4 us (21%)
  local copies, waits for them, and re-layouts  9.85 us (4%)
    ppermute x22, waiting for transfers between devices, over(): return lax.ppermute(value, axis, pairs)  76.8 us
    ppermute x22, starting transfers between devices, over(): return lax.ppermute(value, axis, pairs)  32.9 us
    pallas_call x3, Pallas kernels, per_device(): call(pair_kernel, 'pair', [VM] * 14, [plane] * 4, temps)(*operands)  32.3 us
    pallas_call x4, Pallas kernels, per_device(): call(settle_kernel, 'settle', [VM] * 6, [plane] * 2)  28.9 us
    pallas_call x1, Pallas kernels, per_device(): call(last_kernel, 'last', [VM] * 14, [(FIELDS, 8, LANES)], temps * 3)  14.7 us
    all_to_all x1, starting transfers between devices, per_device(): lax.all_to_all(message.reshape(everyone, 1, LANES), both, 0, 0, tiled=True)  13.6 us
    all_to_all x1, waiting for transfers between devices, per_device(): lax.all_to_all(message.reshape(everyone, 1, LANES), both, 0, 0, tiled=True)  9.52 us
    pallas_call x1, Pallas kernels, per_device(): call(first_kernel, 'first', [SM] + [VM] * 6, [plane] * 4, temps)  9.48 us
  transfers between devices with their start and end apart: 24, of which 21 were waited for; matrix products, arithmetic and copies ran while one was open for 1% of the time, Pallas kernels for 3%

commit v1 on v0

v1 whole, which is shorter than its diff:
```python
import jax
import jax.numpy as jnp
from jax import lax
from jax.experimental import pallas as pl
from jax.experimental.pallas import tpu as pltpu
from jax.sharding import PartitionSpec as P

SLIP = 12
RELAX = 0.15
SHARE = RELAX / 6.0
ROWS = 64
LANES = 128
SLOTS = 2
FIELDS = SLOTS * 6
VMEM_LIMIT = 16 * 1024 * 1024
GROUP = 12
HALF = 18
F32 = jnp.float32

VM = pl.BlockSpec(memory_space=pltpu.VMEM)
SM = pl.BlockSpec(memory_space=pltpu.SMEM)


def cost(micros):
    return pl.CostEstimate(flops=0, transcendentals=0, bytes_accessed=int(micros * 3.6e6))


def call(kernel, name, micros, in_specs, outs, scratch=()):
    return pl.pallas_call(
        kernel,
        name=name,
        in_specs=in_specs,
        out_specs=[VM] * len(outs),
        cost_estimate=cost(micros),
        out_shape=[jax.ShapeDtypeStruct(s, F32) for s in outs],
        scratch_shapes=list(scratch),
        compiler_params=pltpu.CompilerParams(vmem_limit_bytes=VMEM_LIMIT),
    )


def chunks(body):
    def step(k, carry):
        body(pl.ds(pl.multiple_of(k * 8, 8), 8))
        return carry

    lax.fori_loop(0, ROWS // 8, step, 0)


def elastic(diag, off, put):
    for i in range(6):
        for j in range(6):
            v = off[6 * i + j]
            put(6 * i + j, v + diag[i] if i == j else v)


def edge_kernel(diag, off, low, high):
    def put(k, v):
        if k < HALF:
            low[k] = v
        else:
            high[k - HALF] = v

    elastic(diag, off, put)


def pack_kernel(diag, off, schmid, crss, branch, rate, coef):
    def put(k, v):
        coef[k] = v

    elastic(diag, off, put)
    bits = branch[...]
    speed = rate[...]
    for a in range(SLIP):
        limit = crss[a]
        inverse = 1.0 / limit
        for j in range(6):
            coef[36 + 6 * a + j] = schmid[6 * a + j] * inverse
        active = (jnp.right_shift(bits, a) & 1).astype(F32)
        coef[108 + a] = active * speed * (limit * limit)


def in_hbm(*arrays):
    return [pltpu.with_memory_space_constraint(v, pltpu.HBM) for v in arrays]


def pack(kernel, name, micros, operands, planes):
    block = lambda n: pl.BlockSpec((n, 8, LANES), lambda k: (0, k, 0))
    return pl.pallas_call(
        kernel,
        name=name,
        cost_estimate=cost(micros),
        grid=(ROWS // 8,),
        in_specs=[
            block(v.shape[0]) if v.ndim == 3 else pl.BlockSpec((8, LANES), lambda k: (k, 0))
            for v in operands
        ],
        out_specs=[block(n) for n in planes],
        out_shape=[jax.ShapeDtypeStruct((n, ROWS, LANES), F32) for n in planes],
        compiler_params=pltpu.CompilerParams(vmem_limit_bytes=VMEM_LIMIT),
    )(*in_hbm(*operands))


def times(c, at, vectors):
    sums = [[None] * 6 for _ in vectors]
    for i in range(6):
        for j in range(6):
            entry = c(6 * i + j, at)
            for s, vector in enumerate(vectors):
                term = entry * vector[j]
                sums[s][i] = term if j == 0 else sums[s][i] + term
    return sums


def load(ref, at):
    return [[ref[6 * s + i, at, :] for i in range(6)] for s in range(SLOTS)]


def store(ref, at, values):
    for s in range(SLOTS):
        for i in range(6):
            ref[6 * s + i, at, :] = values[s][i]


def slip(c, at, stress, total):
    total = [list(t) for t in total]
    for a in range(SLIP):
        rows = [c(36 + 6 * a + j, at) for j in range(6)]
        gain = c(108 + a, at)
        for s in range(SLOTS):
            t = rows[0] * stress[s][0]
            for j in range(1, 6):
                t = t + rows[j] * stress[s][j]
            w = gain * (t - jnp.tanh(t))
            for j in range(6):
                total[s][j] = total[s][j] - rows[j] * w
    return total


def around(x):
    rows = pltpu.roll(x, 1, axis=0) + pltpu.roll(x, ROWS - 1, axis=0)
    return rows + (pltpu.roll(x, 1, axis=1) + pltpu.roll(x, LANES - 1, axis=1))


def beside(sig_0, sig_1, base_0, base_1):
    def step(k, carry):
        for f in [k * GROUP + j for j in range(GROUP)]:
            u = sig_0[f]
            v = sig_1[f]
            base_0[f] = base_0[f] + SHARE * (around(u) + v)
            base_1[f] = base_1[f] + SHARE * (around(v) + u)
        return carry

    lax.fori_loop(0, FIELDS // GROUP, step, 0)


def combine(x, y, fn):
    return [[fn(x[s][i], y[s][i]) for i in range(6)] for s in range(SLOTS)]


def relaxed(e, sig):
    return combine(e, sig, lambda u, v: u - RELAX * v)


def whole(ref):
    return lambda k, at: ref[k, at, :]


def joined(low, high):
    return lambda k, at: low[k, at, :] if k < HALF else high[k - HALF, at, :]


def split(side, coefficients, run):
    own, other, near, far, rest_near, rest_far = coefficients
    early = joined(near, rest_far)
    late = joined(rest_near, far)
    pl.when(side[0] == 0)(lambda: run(whole(own), whole(other), early, late))
    pl.when(side[0] == 1)(lambda: run(whole(other), whole(own), late, early))


def first_kernel(
    side, ebar, own_hbm, other_hbm, near, far, rest_near, rest_far, x_0, x_1, own, other, e_0, e_1, t_0, t_1, sems
):
    copies = [
        pltpu.make_async_copy(src.at[low:high], dst.at[low:high], sems.at[k])
        for k, (src, dst, low, high) in enumerate(
            (
                (own_hbm, own, 0, 36),
                (other_hbm, other, 0, 36),
                (own_hbm, own, 36, 120),
                (other_hbm, other, 36, 120),
            )
        )
    ]
    for copy in copies:
        copy.start()
    copies[0].wait()
    copies[1].wait()

    def start(c_0, c_1, g_0, g_1):
        for c, g, t_ref, e_ref in ((c_0, g_0, t_0, e_0), (c_1, g_1, t_1, e_1)):

            def body(at, c=c, g=g, t_ref=t_ref, e_ref=e_ref):
                strain = [
                    [jnp.full((8, LANES), ebar[s, i], F32) for i in range(6)] for s in range(SLOTS)
                ]
                sig = times(c, at, strain)
                outer = times(g, at, strain)
                store(t_ref, at, sig)
                base = combine(relaxed(strain, sig), outer, lambda u, v: u + SHARE * v)
                store(e_ref, at, base)

            chunks(body)

    coefficients = (own, other, near, far, rest_near, rest_far)
    split(side, coefficients, start)
    beside(t_0, t_1, e_0, e_1)
    copies[2].wait()
    copies[3].wait()
    split(side, coefficients, lambda c_0, c_1, g_0, g_1: advance(((c_0, t_0, e_0, x_0), (c_1, t_1, e_1, x_1))))
    beside_own(x_0, x_1)


def advance(planes):
    for c, t_ref, e_ref, x_ref in planes:

        def body(at, c=c, t_ref=t_ref, e_ref=e_ref, x_ref=x_ref):
            e = slip(c, at, load(t_ref, at), load(e_ref, at))
            sig = times(c, at, e)
            store(x_ref.at[0:FIELDS], at, sig)
            store(x_ref.at[FIELDS:], at, slip(c, at, sig, relaxed(e, sig)))

        chunks(body)


def beside_own(x_0, x_1):
    beside(x_0.at[0:FIELDS], x_1.at[0:FIELDS], x_0.at[FIELDS:], x_1.at[FIELDS:])


def arrive(planes):
    for x_ref, far_ref, c, g, t_ref, e_ref in planes:

        def body(at, x_ref=x_ref, far_ref=far_ref, c=c, g=g, t_ref=t_ref, e_ref=e_ref):
            add = lambda u, v: u + SHARE * v
            own = x_ref.at[0:FIELDS], x_ref.at[FIELDS:]
            far = far_ref.at[0:FIELDS], far_ref.at[FIELDS:]
            e = combine(load(own[1], at), load(far[0], at), add)
            sig = times(c, at, e)
            store(t_ref, at, sig)
            base = relaxed(e, sig)
            outer = times(g, at, combine(load(far[1], at), load(own[0], at), add))
            store(e_ref, at, combine(base, outer, add))

        chunks(body)


def two_sweeps(c_0, c_1, g_0, g_1, x_0, x_1, f_0, f_1, y_0, y_1, e_0, e_1, t_0, t_1):
    arrive(((x_0, f_0, c_0, g_0, t_0, e_0), (x_1, f_1, c_1, g_1, t_1, e_1)))
    beside(t_0, t_1, e_0, e_1)
    advance(((c_0, t_0, e_0, y_0), (c_1, t_1, e_1, y_1)))
    beside_own(y_0, y_1)


def pair_kernel(side, own, other, near, far, rest_near, rest_far, *refs):
    split(side, (own, other, near, far, rest_near, rest_far), lambda *c: two_sweeps(*c, *refs))


def last_kernel(side, own, other, near, far, rest_near, rest_far, x_0, x_1, f_0, f_1, out, y_0, y_1, *temps):
    def run(c_0, c_1, g_0, g_1):
        two_sweeps(c_0, c_1, g_0, g_1, x_0, x_1, f_0, f_1, y_0, y_1, *temps)
        for k in range(FIELDS):
            out[k] = jnp.zeros((8, LANES), F32)
        for y_ref, c, g in ((y_0, c_0, g_0), (y_1, c_1, g_1)):

            def body(at, y_ref=y_ref, c=c, g=g):
                mine = times(c, at, load(y_ref.at[FIELDS:], at))
                outer = times(g, at, load(y_ref.at[0:FIELDS], at))
                for s in range(SLOTS):
                    for i in range(6):
                        out[6 * s + i] = out[6 * s + i] + (mine[s][i] + SHARE * outer[s][i])

            chunks(body)

    split(side, (own, other, near, far, rest_near, rest_far), run)


def strain_kernel(node, owner, member, disp, before, after, out, grid):
    grid[:, 0:1] = before[...]
    grid[:, 1:3] = disp[...]
    grid[:, 3:4] = after[...]
    lane = lax.broadcasted_iota(jnp.int32, (1, LANES), 1)
    group = lax.broadcasted_iota(jnp.int32, (8, LANES), 0)
    total = jnp.zeros((8, LANES), F32)
    for p in range(2):
        local = node[p] - member[0] * (2 * 32 * LANES)
        present = (local >= 0) & (local < 2 * 32 * LANES)
        local = jnp.clip(local, 0, 2 * 32 * LANES - 1)
        x = local // (32 * LANES)
        y = (local // LANES) % 32
        z = local % LANES
        up_y = jnp.minimum(y + 1, 31)
        down_y = jnp.maximum(y - 1, 0)
        has_up = jnp.where(y < 31, 1.0, 0.0).astype(F32)
        has_down = jnp.where(y > 0, 1.0, 0.0).astype(F32)
        slope = []
        for c in range(3):
            row = lambda dx, yy: grid[c, x + dx, pl.ds(yy, 1), :]
            gx = (row(2, y) - row(0, y)) * 0.5
            gy = (row(1, up_y) * has_up - row(1, down_y) * has_down) * 0.5
            mid = row(1, y)
            right = jnp.where(lane < LANES - 1, pltpu.roll(mid, LANES - 1, axis=1), 0.0)
            left = jnp.where(lane > 0, pltpu.roll(mid, 1, axis=1), 0.0)
            slope.append((gx, gy, (right - left) * 0.5))
        parts = [
            slope[0][0],
            slope[1][1],
            slope[2][2],
            slope[1][2] + slope[2][1],
            slope[0][2] + slope[2][0],
            slope[0][1] + slope[1][0],
        ]
        here = (lane == z) & present
        line = jnp.zeros((1, LANES), F32)
        for j, part in enumerate(parts):
            value = jnp.sum(jnp.where(here, part, 0.0), axis=1, keepdims=True)
            line = line + jnp.where(lane == j, value, 0.0)
        total = total + jnp.where(group == owner[p, 0], line, 0.0)
    out[...] = total


def stencil_kernel(blocks, disp, before, after, external, out, moved, total):
    step = pl.program_id(0)

    @pl.when(step == 0)
    def _():
        lane = lax.broadcasted_iota(jnp.int32, (32, LANES), 1)
        row = lax.broadcasted_iota(jnp.int32, (32, LANES), 0)
        total[...] = jnp.zeros_like(total)
        for c in range(3):
            for x in range(4):
                v = before[c, 0] if x == 0 else (after[c, 0] if x == 3 else disp[c, x - 1])
                for j in range(3):
                    w = v
                    if j == 0:
                        w = jnp.where(row > 0, pltpu.roll(v, 1, axis=0), 0.0)
                    if j == 2:
                        w = jnp.where(row < 31, pltpu.roll(v, 31, axis=0), 0.0)
                    moved[j, 0, c, x] = jnp.where(lane > 0, pltpu.roll(w, 1, axis=1), 0.0)
                    moved[j, 1, c, x] = w
                    moved[j, 2, c, x] = jnp.where(lane < LANES - 1, pltpu.roll(w, LANES - 1, axis=1), 0.0)

    i = step // 3
    j = step % 3
    for c in range(3):
        for x in range(2):
            s = total[c, x]
            for k in range(3):
                for d in range(3):
                    s = s + blocks[k, c, d, x].astype(F32) * moved[j, k, d, i + x]
            total[c, x] = s

    @pl.when(step == 8)
    def _():
        out[...] = external[...] - total[...]


def stencil(stiffness, disp, before, after, external):
    whole = lambda n: pl.BlockSpec((3, n, 32, LANES), lambda s: (0, 0, 0, 0))
    return pl.pallas_call(
        stencil_kernel,
        name="stencil",
        cost_estimate=cost(5),
        grid=(9,),
        in_specs=[
            pl.BlockSpec((3, 3, 3, 2, 32, LANES), lambda s: (s, 0, 0, 0, 0, 0)),
            whole(2),
            whole(1),
            whole(1),
            whole(2),
        ],
        out_specs=whole(2),
        out_shape=jax.ShapeDtypeStruct((3, 2, 32, LANES), F32),
        scratch_shapes=[
            pltpu.VMEM((3, 3, 3, 4, 32, LANES), F32),
            pltpu.VMEM((3, 2, 32, LANES), F32),
        ],
        compiler_params=pltpu.CompilerParams(vmem_limit_bytes=VMEM_LIMIT),
    )(*in_hbm(stiffness, disp, before, after, external))


def final_kernel(node, owner, member, received, loads, base, residual, stress):
    residual[...] = base[...]
    lane = lax.broadcasted_iota(jnp.int32, (1, LANES), 1)
    sums = [jnp.sum(received[g], axis=0, keepdims=True) for g in range(4)]
    for p in range(2):
        line = jnp.zeros((1, LANES), F32)
        for g in range(4):
            line = line + jnp.where(owner[p, 0] == g, sums[g], 0.0)
        line = line * (1.0 / 262144.0)
        stress[p : p + 1, :] = line[:, 0:6]
        local = node[p] - member[0] * (2 * 32 * LANES)
        present = (local >= 0) & (local < 2 * 32 * LANES)
        local = jnp.clip(local, 0, 2 * 32 * LANES - 1)
        x = local // (32 * LANES)
        y = (local // LANES) % 32
        z = local % LANES
        here = (lane == z) & present
        for c in range(3):
            force = jnp.sum(loads[p, c : c + 1, :] * line, axis=1, keepdims=True)
            row = residual[c, x, pl.ds(y, 1), :]
            residual[c, x, pl.ds(y, 1), :] = row - jnp.where(here, force, 0.0)


def per_device(
    displacement,
    stiffness,
    external,
    point_node,
    point_owner,
    point_load,
    moduli_diag,
    moduli_off,
    schmid,
    crss,
    branch,
    rate,
):
    groups = lax.axis_size("grp")
    members = lax.axis_size("rve")
    member = lax.axis_index("rve")
    everyone = groups * members

    def over(value, pairs, axis="rve"):
        return lax.ppermute(value, axis, pairs)

    partner = [(i, i ^ 1) for i in range(members)]
    across = [(i, (i - 1 if i % 2 == 0 else i + 1) % members) for i in range(members)]
    along = [(i, (i - 2 if i % 2 == 0 else i + 2) % members) for i in range(members)]
    rightward = [(i, (i + 2) % members) for i in range(members)]
    leftward = [(i, (i - 2) % members) for i in range(members)]

    both = ("grp", "rve")
    upward = [(i, i + 1) for i in range(everyone - 1)]
    downward = [(i + 1, i) for i in range(everyone - 1)]
    before = over(displacement[:, 1:2], upward, both)
    after = over(displacement[:, 0:1], downward, both)

    diag = moduli_diag[0, :, 0]
    off = moduli_off[0, :, 0]
    low, high = pack(edge_kernel, "edge", 0.1, (diag, off), (HALF, HALF))
    near = over(low, across)
    far = over(high, along)
    flow = rate[0, 0]
    flow, low, high = lax.optimization_barrier((flow, low, high))
    own = pack(
        pack_kernel, "pack", 0.1, (diag, off, schmid[0, :, 0], crss[0, :, 0], branch[0, 0], flow), (120,)
    )[0]
    before, after, own, near, far = lax.optimization_barrier((before, after, own, near, far))
    core = member % 2

    where = member.reshape(1).astype(jnp.int32)
    message = call(
        strain_kernel,
        "strain",
        0.1,
        [SM, SM, SM, VM, VM, VM],
        [(8, LANES)],
        [pltpu.VMEM((3, 4, 32, LANES), F32)],
    )(point_node, point_owner, where, displacement, before, after)[0]
    other = over(own, partner)
    rest_near = over(near, partner)
    rest_far = over(far, partner)
    message = jnp.broadcast_to(message[:groups, None, None, :], (groups, members, 1, LANES))
    arrived = lax.all_to_all(message.reshape(everyone, 1, LANES), both, 0, 0, tiled=True)
    strains = jnp.sum(arrived.reshape(groups, members, LANES), axis=1)
    ebar = lax.dynamic_slice_in_dim(strains, core * SLOTS, SLOTS, axis=0)

    base = stencil(stiffness, displacement, before, after, external)

    plane = (FIELDS, ROWS, LANES)
    packed = (2 * FIELDS, ROWS, LANES)
    temps = [pltpu.VMEM(plane, F32)] * 4
    side = core.reshape(1).astype(jnp.int32)
    ghosts = (near, far, rest_near, rest_far)
    ANY = pl.BlockSpec(memory_space=pl.ANY)
    x_0, x_1, own, other = call(
        first_kernel,
        "first",
        5,
        [SM] * 2 + [ANY] * 2 + [VM] * 4,
        [packed] * 2 + [(120, ROWS, LANES)] * 2,
        temps + [pltpu.SemaphoreType.DMA((4,))],
    )(side, ebar, *in_hbm(own, other), *ghosts)
    fixed = (own, other, *ghosts)
    for pair in range(4):
        f_0 = over(x_1, rightward)
        f_1 = over(x_0, leftward)
        operands = (side, *fixed, x_0, x_1, f_0, f_1)
        if pair < 3:
            x_0, x_1 = call(pair_kernel, "pair", 5, [SM] + [VM] * 10, [packed] * 2, temps)(*operands)
        else:
            sizes = [pltpu.VMEM(packed, F32)] * 2 + temps
            sums = call(last_kernel, "last", 6, [SM] + [VM] * 10, [(FIELDS, 8, LANES)], sizes)(*operands)[0]

    totals = jnp.sum(sums, axis=(1, 2)).reshape(SLOTS, 6)
    totals = jnp.pad(totals, ((0, 0), (0, LANES - 6)))
    mine = jnp.zeros((groups, LANES), F32)
    mine = lax.dynamic_update_slice_in_dim(mine, totals, core * SLOTS, axis=0)
    reply = jnp.broadcast_to(mine[:, None, None, :], (groups, members, 1, LANES))
    received = lax.all_to_all(reply.reshape(everyone, 1, LANES), both, 0, 0, tiled=True)
    loads = jnp.pad(point_load.reshape(-1, 3, 6), ((0, 0), (0, 0), (0, LANES - 6)))
    residual, point_stress = call(
        final_kernel, "final", 2, [SM, SM, SM, VM, VM, VM], [(3, 2, 32, LANES), (2, 6)]
    )(point_node, point_owner, where, received.reshape(groups, members, LANES), loads, base)
    return (residual, point_stress)


def solution(mesh):
    in_specs = (
        P(None, ("grp", "rve"), None, None),
        P(None, None, None, ("grp", "rve"), None, None),
        P(None, ("grp", "rve"), None, None),
        P("grp"),
        P("grp", None),
        P("grp", None),
        P("grp", None, "rve", None, None),
        P("grp", None, "rve", None, None),
        P("grp", None, "rve", None, None),
        P("grp", None, "rve", None, None),
        P("grp", "rve", None, None),
        P("grp", "rve", None, None),
    )
    out_specs = (P(None, ("grp", "rve"), None, None), P("grp", None))
    return jax.shard_map(
        per_device, mesh=mesh, in_specs=in_specs, out_specs=out_specs, check_vma=False
    )
```

time: 258 us -> 190 us (0.74)
  Pallas kernels: 102 us -> 52.5 us
  waiting for transfers between devices: 88.5 us -> 77.6 us
  local copies, waits for them, and re-layouts: 9.85 us -> 2.43 us
    pallas_call x13 -> x10, Pallas kernels: 102 us -> 52.5 us  [the longest x3 18.2 us: per_device(): call(pair_kernel, 'pair', 5, [SM] + [VM] * 10, [packed] * 2, temps)]
    ppermute x22 -> x15, waiting for transfers between devices: 76.8 us -> 64.9 us  [over(): return lax.ppermute(value, axis, pairs)]
    unnamed x63 -> x13, local copies, waits for them, and re-layouts: 6.53 us -> 0.13 us
    all_to_all x1, starting transfers between devices: 8.95 us -> 12.6 us  [per_device(): lax.all_to_all(reply.reshape(everyone, 1, LANES), both, 0, 0, tiled=True)]
    ppermute x22 -> x15, starting transfers between devices: 32.9 us -> 31.5 us  [over(): return lax.ppermute(value, axis, pairs)]
  transfers between devices with their start and end apart: 24 -> 17, of which waited for: 21 -> 8; matrix products, arithmetic and copies ran while one was open for 1% -> 1% of each run, Pallas kernels for 3% -> 7%
where the time goes in v1:
time: 190 us; the launch traced here: 189 us
  waiting for transfers between devices  77.6 us (41%)
  starting transfers between devices  55.5 us (29%)
  Pallas kernels  52.5 us (28%)
  local copies, waits for them, and re-layouts  2.43 us (1%)
    ppermute x15, waiting for transfers between devices, over(): return lax.ppermute(value, axis, pairs)  64.9 us
    ppermute x15, starting transfers between devices, over(): return lax.ppermute(value, axis, pairs)  31.5 us
    pallas_call x3, Pallas kernels, per_device(): call(pair_kernel, 'pair', 5, [SM] + [VM] * 10, [packed] * 2, temps)  18.2 us
    all_to_all x1, starting transfers between devices, per_device(): lax.all_to_all(reply.reshape(everyone, 1, LANES), both, 0, 0, tiled=True)  12.6 us
    all_to_all x1, starting transfers between devices, per_device(): lax.all_to_all(message.reshape(everyone, 1, LANES), both, 0, 0, tiled=True)  11.5 us
    pallas_call x2, Pallas kernels, pack(): pl.pallas_call(kernel, name=name, cost_estimate=cost(micros), grid=(ROWS...  10.7 us
    all_to_all x1, waiting for transfers between devices, per_device(): lax.all_to_all(message.reshape(everyone, 1, LANES), both, 0, 0, tiled=True)  9.52 us
    pallas_call x1, Pallas kernels, per_device(): call(first_kernel, 'first', 5, [SM] * 2 + [ANY] * 2 + [VM] * 4, [packed]...  8.16 us
  transfers between devices with their start and end apart: 17, of which 8 were waited for; matrix products, arithmetic and copies ran while one was open for 1% of the time, Pallas kernels for 7%

profile of v1, /device:TPU:1, one launch (start us, length us, event | category | flops | bytes accessed | tf_op | source)
XLA Modules:
  0.0 189.2 jit_solution(4506381827203508650)
XLA Ops:
  0.6 4.0 %edge.1 = (f32[18,64,128]{2,1,0:T(8,128)S(1)}, f32[18,64,128]{2,1,0:T(8,128)S(1)}) custom-call(f32[6,64,128]{2,1,0:T(8,128)} %bitcast.18, f32[36,64,128]{2,1,0:T(8,128)} %bitcast.15), custom_call_target="tpu_custom_call" | custom-call | bytes 360000 | tf_op jit(solution)/shard_map/edge/pallas_call | solution.py:88
  4.6 2.7 %collective-permute-start.2 = (f32[18,64,128]{2,1,0:T(8,128)S(1)}, f32[18,64,128]{2,1,0:T(8,128)S(1)}, u32[]{:S(2)}, u32[]{:S(2)}) collective-permute-start(f32[18,64,128]{2,1,0:T(8,128)S(1)} %get-tuple-element.20), channel_id=1, source_target_pairs={{0,31},{1,2},{2,1},{3,4},{4,3},{5,6},{6,5},{7,8},{8,7},{9,10},{10,... | collective-permute-start | bytes 1769480 | tf_op jit(solution)/shard_map/ppermute | solution.py:433
  7.3 1.2 collective-permute-start.3
  8.5 0.8 fusion
  9.4 5.9 %collective-permute-start = (f32[3,1,32,128]{3,2,1,0:T(8,128)S(1)}, f32[3,1,32,128]{3,2,1,0:T(8,128)S(1)}, u32[]{:S(2)}, u32[]{:S(2)}) collective-permute-start(f32[3,1,32,128]{3,2,1,0:T(8,128)S(1)} %get-tuple-element.39), channel_id=1, source_target_pairs={{0,1},{1,2},{2,3},{3,4},{4,5},{5,6},{6,7},{7,8},{8,9},{9,10},{10,1... | collective-permute-start | bytes 147464 | tf_op jit(solution)/shard_map/ppermute | solution.py:433
  15.2 1.9 %collective-permute-start.1 = (f32[3,1,32,128]{3,2,1,0:T(8,128)S(1)}, f32[3,1,32,128]{3,2,1,0:T(8,128)S(1)}, u32[]{:S(2)}, u32[]{:S(2)}) collective-permute-start(f32[3,1,32,128]{3,2,1,0:T(8,128)S(1)} %get-tuple-element.38), channel_id=1, source_target_pairs={{1,0},{2,1},{3,2},{4,3},{5,4},{6,5},{7,6},{8,7},{9,8},{10,9},{11,1... | collective-permute-start | bytes 147464 | tf_op jit(solution)/shard_map/ppermute | solution.py:433
  17.2 0.0 copy-start.5
  17.2 0.0 copy-start
  17.2 0.0 copy-start.3
  17.2 6.8 %pack.1.own_hbm = f32[120,64,128]{2,1,0:T(8,128)} custom-call(f32[6,64,128]{2,1,0:T(8,128)} %bitcast.19, f32[36,64,128]{2,1,0:T(8,128)} %bitcast.16, f32[72,64,128]{2,1,0:T(8,128)} %bitcast.17, f32[12,64,128]{2,1,0:T(8,128)} %bitcast.20, s32[64,128]{1,0:T(8,128)} %bitcast.22, f32[64,128]{1,0:T(8,128)} %bitcast.23), custom_call_target="tpu_custom_call" | custom-call | bytes 360000 | tf_op jit(solution)/shard_map/pack/pallas_call | solution.py:88
  23.9 0.0 collective-permute-done.before
  23.9 0.0 copy-start.1
  24.0 0.0 collective-permute-done.1.after
  24.0 0.0 copy-start.2
  24.0 0.0 collective-permute-done.2.near
  24.0 0.4 collective-permute-done.3.far
  24.4 0.2 collective-permute-start.4
  24.6 0.3 collective-permute-start.5
  24.9 0.2 collective-permute-start.6
  25.1 0.0 copy-done.5
  25.1 0.1 copy.19.owner
  25.2 0.0 copy-done
  25.2 0.0 copy-done.3
  25.2 0.7 strain.1
  25.9 0.6 broadcast_in_dim.20
  26.6 11.5 %all-to-all-start = ((f32[128,1,128]{2,1,0:T(1,128)}), f32[128,1,128]{2,1,0:T(1,128)S(1)}, u32[]{:S(2)}, u32[]{:S(2)}) async-start(f32[128,1,128]{2,1,0:T(1,128)} %bitcast.8), calls=%async_computation | async-start | bytes 131072 | tf_op jit(solution)/shard_map/all_to_all | solution.py:473
  38.1 9.5 %all-to-all-done = f32[128,1,128]{2,1,0:T(1,128)S(1)} async-done(((f32[128,1,128]{2,1,0:T(1,128)}), f32[128,1,128]{2,1,0:T(1,128)S(1)}, u32[]{:S(2)}, u32[]{:S(2)}) %all-to-all-start) | async-done | bytes 65568 | tf_op jit(solution)/shard_map/all_to_all | solution.py:473
  47.6 0.0 collective-permute-done.5.rest_near
  47.6 0.0 collective-permute-done.6.rest_far
  47.7 0.0 collective-permute-done.4.other_hbm
  47.7 8.2 %first.1 = (f32[24,64,128]{2,1,0:T(8,128)S(1)}, f32[24,64,128]{2,1,0:T(8,128)S(1)}, f32[120,64,128]{2,1,0:T(8,128)S(1)}, f32[120,64,128]{2,1,0:T(8,128)S(1)}) custom-call(s32[1]{0:T(128)} %bitcast.1.side, f32[2,128]{1,0:T(2,128)S(1)} %constant_dynamic-slice_fusion.ebar, f32[120,64,128]{2,1,0:T(8,128)} %pack.1.own_hbm, ...), custom_call_target="tpu_custom_call" | custom-call | bytes 18000000 | tf_op jit(solution)/shard_map/first/pallas_call | solution.py:485
  55.8 0.0 copy-done.1
  55.8 0.0 copy-done.2
  55.9 0.4 collective-permute-start.7
  56.2 4.5 %collective-permute-start.8 = (f32[24,64,128]{2,1,0:T(8,128)S(1)}, f32[24,64,128]{2,1,0:T(8,128)S(1)}, u32[]{:S(2)}, u32[]{:S(2)}) collective-permute-start(f32[24,64,128]{2,1,0:T(8,128)S(1)} %get-tuple-element.30.refs_0_), channel_id=1, source_target_pairs={{0,30},{1,31},{2,0},{3,1},{4,2},{5,3},{6,4},{7,5},{8,6},{9,7},{10,... | collective-permute-start | bytes 2359304 | tf_op jit(solution)/shard_map/ppermute | solution.py:433
  60.7 16.8 %collective-permute-done.7.refs_2_ = f32[24,64,128]{2,1,0:T(8,128)S(1)} collective-permute-done((f32[24,64,128]{2,1,0:T(8,128)S(1)}, f32[24,64,128]{2,1,0:T(8,128)S(1)}, u32[]{:S(2)}, u32[]{:S(2)}) %collective-permute-start.7) | collective-permute-done | bytes 786464 | tf_op jit(solution)/shard_map/ppermute | solution.py:433
  77.6 0.0 collective-permute-done.8.refs_3_
  77.6 6.0 %pair.3 = (f32[24,64,128]{2,1,0:T(8,128)S(1)}, f32[24,64,128]{2,1,0:T(8,128)S(1)}) custom-call(s32[1]{0:T(128)} %bitcast.1.side, f32[120,64,128]{2,1,0:T(8,128)S(1)} %get-tuple-element.28.own, f32[120,64,128]{2,1,0:T(8,128)S(1)} %get-tuple-element.29.other, f32[18,64,128]{2,1,0:T(8,128)S(1)} %collective-permute-done.2.near, ...), custom_call_target="tpu_custom_call" | custom-call | bytes 18000000 | tf_op jit(solution)/shard_map/pair/pallas_call | solution.py:499
  83.6 4.5 %collective-permute-start.10 = (f32[24,64,128]{2,1,0:T(8,128)S(1)}, f32[24,64,128]{2,1,0:T(8,128)S(1)}, u32[]{:S(2)}, u32[]{:S(2)}) collective-permute-start(f32[24,64,128]{2,1,0:T(8,128)S(1)} %get-tuple-element.32.refs_0_), channel_id=1, source_target_pairs={{0,30},{1,31},{2,0},{3,1},{4,2},{5,3},{6,4},{7,5},{8,6},{9,7},{10,... | collective-permute-start | bytes 2359304 | tf_op jit(solution)/shard_map/ppermute | solution.py:433
  88.1 0.0 collective-permute-start.9
  88.1 14.9 %collective-permute-done.10.refs_3_ = f32[24,64,128]{2,1,0:T(8,128)S(1)} collective-permute-done((f32[24,64,128]{2,1,0:T(8,128)S(1)}, f32[24,64,128]{2,1,0:T(8,128)S(1)}, u32[]{:S(2)}, u32[]{:S(2)}) %collective-permute-start.10) | collective-permute-done | bytes 786464 | tf_op jit(solution)/shard_map/ppermute | solution.py:433
  103.0 5.2 %collective-permute-done.9.refs_2_ = f32[24,64,128]{2,1,0:T(8,128)S(1)} collective-permute-done((f32[24,64,128]{2,1,0:T(8,128)S(1)}, f32[24,64,128]{2,1,0:T(8,128)S(1)}, u32[]{:S(2)}, u32[]{:S(2)}) %collective-permute-start.9) | collective-permute-done | bytes 786464 | tf_op jit(solution)/shard_map/ppermute | solution.py:433
  108.2 6.1 %pair.4 = (f32[24,64,128]{2,1,0:T(8,128)S(1)}, f32[24,64,128]{2,1,0:T(8,128)S(1)}) custom-call(s32[1]{0:T(128)} %bitcast.1.side, f32[120,64,128]{2,1,0:T(8,128)S(1)} %get-tuple-element.28.own, f32[120,64,128]{2,1,0:T(8,128)S(1)} %get-tuple-element.29.other, f32[18,64,128]{2,1,0:T(8,128)S(1)} %collective-permute-done.2.near, ...), custom_call_target="tpu_custom_call" | custom-call | bytes 18000000 | tf_op jit(solution)/shard_map/pair/pallas_call | solution.py:499
  114.3 0.1 collective-permute-start.11
  114.4 4.8 %collective-permute-start.12 = (f32[24,64,128]{2,1,0:T(8,128)S(1)}, f32[24,64,128]{2,1,0:T(8,128)S(1)}, u32[]{:S(2)}, u32[]{:S(2)}) collective-permute-start(f32[24,64,128]{2,1,0:T(8,128)S(1)} %get-tuple-element.34.refs_0_), channel_id=1, source_target_pairs={{0,30},{1,31},{2,0},{3,1},{4,2},{5,3},{6,4},{7,5},{8,6},{9,7},{10,... | collective-permute-start | bytes 2359304 | tf_op jit(solution)/shard_map/ppermute | solution.py:433
  119.2 14.2 %collective-permute-done.11.refs_2_ = f32[24,64,128]{2,1,0:T(8,128)S(1)} collective-permute-done((f32[24,64,128]{2,1,0:T(8,128)S(1)}, f32[24,64,128]{2,1,0:T(8,128)S(1)}, u32[]{:S(2)}, u32[]{:S(2)}) %collective-permute-start.11) | collective-permute-done | bytes 786464 | tf_op jit(solution)/shard_map/ppermute | solution.py:433
  133.4 0.0 collective-permute-done.12.refs_3_
  133.4 6.1 %pair.5 = (f32[24,64,128]{2,1,0:T(8,128)S(1)}, f32[24,64,128]{2,1,0:T(8,128)S(1)}) custom-call(s32[1]{0:T(128)} %bitcast.1.side, f32[120,64,128]{2,1,0:T(8,128)S(1)} %get-tuple-element.28.own, f32[120,64,128]{2,1,0:T(8,128)S(1)} %get-tuple-element.29.other, f32[18,64,128]{2,1,0:T(8,128)S(1)} %collective-permute-done.2.near, ...), custom_call_target="tpu_custom_call" | custom-call | bytes 18000000 | tf_op jit(solution)/shard_map/pair/pallas_call | solution.py:499
  139.5 0.1 collective-permute-start.13
  139.6 0.0 copy-start.4
  139.6 4.8 %collective-permute-start.14 = (f32[24,64,128]{2,1,0:T(8,128)S(1)}, f32[24,64,128]{2,1,0:T(8,128)S(1)}, u32[]{:S(2)}, u32[]{:S(2)}) collective-permute-start(f32[24,64,128]{2,1,0:T(8,128)S(1)} %get-tuple-element.36.x_0), channel_id=1, source_target_pairs={{0,30},{1,31},{2,0},{3,1},{4,2},{5,3},{6,4},{7,5},{8,6},{9,7},{10,... | collective-permute-start | bytes 2359304 | tf_op jit(solution)/shard_map/ppermute | solution.py:433
  144.3 13.3 %collective-permute-done.13.f_0 = f32[24,64,128]{2,1,0:T(8,128)S(1)} collective-permute-done((f32[24,64,128]{2,1,0:T(8,128)S(1)}, f32[24,64,128]{2,1,0:T(8,128)S(1)}, u32[]{:S(2)}, u32[]{:S(2)}) %collective-permute-start.13) | collective-permute-done | bytes 786464 | tf_op jit(solution)/shard_map/ppermute | solution.py:433
  157.6 0.0 collective-permute-done.14.f_1
  157.6 7.2 %last.1 = f32[12,8,128]{2,1,0:T(8,128)S(1)} custom-call(s32[1]{0:T(128)} %bitcast.1.side, f32[120,64,128]{2,1,0:T(8,128)S(1)} %get-tuple-element.28.own, f32[120,64,128]{2,1,0:T(8,128)S(1)} %get-tuple-element.29.other, f32[18,64,128]{2,1,0:T(8,128)S(1)} %collective-permute-done.2.near, f32[18,64,128]{2,1,0:T(8,128)S(1)} %collective-permute-done.3.far, ...), custom_call_target="tpu_custom_call" | custom-call | bytes 21600000 | tf_op jit(solution)/shard_map/last/pallas_call | solution.py:502
  164.9 0.2 reduce_sum.19
  165.0 0.1 reshape.45
  165.1 0.6 broadcast_in_dim.22
  165.8 12.6 %all-to-all-start.1 = ((f32[128,1,128]{2,1,0:T(1,128)}), f32[128,1,128]{2,1,0:T(1,128)S(1)}, u32[]{:S(2)}, u32[]{:S(2)}) async-start(f32[128,1,128]{2,1,0:T(1,128)} %bitcast.10), calls=%async_computation.1 | async-start | bytes 131072 | tf_op jit(solution)/shard_map/all_to_all | solution.py:509
  178.4 0.0 copy-done.4
  178.4 0.1 reshape.47
  178.5 6.2 %stencil.1.base = f32[3,2,32,128]{3,2,1,0:T(8,128)S(1)} custom-call(bf16[27,3,3,2,32,128]{5,4,3,2,1,0:T(8,128)(2,1)} %blocks.1, f32[3,2,32,128]{3,2,1,0:T(8,128)} %disp.3, f32[3,1,32,128]{3,2,1,0:T(8,128)} %copy-done.1, f32[3,1,32,128]{3,2,1,0:T(8,128)} %copy-done.2, f32[3,2,32,128]{3,2,1,0:T(8,128)} %external.1), custom_call_target="tpu_custom_call" | custom-call | bytes 18000000 | tf_op jit(solution)/shard_map/stencil/pallas_call | solution.py:368
  184.7 3.2 %all-to-all-done.1 = f32[128,1,128]{2,1,0:T(1,128)S(1)} async-done(((f32[128,1,128]{2,1,0:T(1,128)}), f32[128,1,128]{2,1,0:T(1,128)S(1)}, u32[]{:S(2)}, u32[]{:S(2)}) %all-to-all-start.1) | async-done | bytes 65568 | tf_op jit(solution)/shard_map/all_to_all | solution.py:509
  187.9 1.3 final.1
  (6 shorter events, 0.1 us)
Async XLA Ops:
  4.6 19.3 %collective-permute-start.2 = (f32[18,64,128]{2,1,0:T(8,128)S(1)}, f32[18,64,128]{2,1,0:T(8,128)S(1)}, u32[]{:S(2)}, u32[]{:S(2)}) collective-permute-start(f32[18,64,128]{2,1,0:T(8,128)S(1)} %get-tuple-element.20), channel_id=1, source_target_pairs={{0,31},{1,2},{2,1},{3,4},{4,3},{5,6},{6,5},{7,8},{8,7},{9,10},{10,... | collective-permute-start | bytes 1769480 | tf_op jit(solution)/shard_map/ppermute | solution.py:433
  7.3 17.1 %collective-permute-start.3 = (f32[18,64,128]{2,1,0:T(8,128)S(1)}, f32[18,64,128]{2,1,0:T(8,128)S(1)}, u32[]{:S(2)}, u32[]{:S(2)}) collective-permute-start(f32[18,64,128]{2,1,0:T(8,128)S(1)} %get-tuple-element.21), channel_id=1, source_target_pairs={{0,30},{1,3},{2,0},{3,5},{4,2},{5,7},{6,4},{7,9},{8,6},{9,11},{10,... | collective-permute-start | bytes 1769480 | tf_op jit(solution)/shard_map/ppermute | solution.py:433
  9.4 14.6 %collective-permute-start = (f32[3,1,32,128]{3,2,1,0:T(8,128)S(1)}, f32[3,1,32,128]{3,2,1,0:T(8,128)S(1)}, u32[]{:S(2)}, u32[]{:S(2)}) collective-permute-start(f32[3,1,32,128]{3,2,1,0:T(8,128)S(1)} %get-tuple-element.39), channel_id=1, source_target_pairs={{0,1},{1,2},{2,3},{3,4},{4,5},{5,6},{6,7},{7,8},{8,9},{9,10},{10,1... | collective-permute-start | bytes 147464 | tf_op jit(solution)/shard_map/ppermute | solution.py:433
  15.2 8.7 %collective-permute-start.1 = (f32[3,1,32,128]{3,2,1,0:T(8,128)S(1)}, f32[3,1,32,128]{3,2,1,0:T(8,128)S(1)}, u32[]{:S(2)}, u32[]{:S(2)}) collective-permute-start(f32[3,1,32,128]{3,2,1,0:T(8,128)S(1)} %get-tuple-element.38), channel_id=1, source_target_pairs={{1,0},{2,1},{3,2},{4,3},{5,4},{6,5},{7,6},{8,7},{9,8},{10,9},{11,1... | collective-permute-start | bytes 147464 | tf_op jit(solution)/shard_map/ppermute | solution.py:433
  17.2 7.9 %copy-start.5 = (s32[2,1]{0,1:T(1,128)S(1)}, s32[2,1]{0,1:T(1,128)}, u32[]{:S(2)}) copy-start(s32[2,1]{0,1:T(1,128)} %param.16) | copy-start | bytes 28
  17.2 8.0 %copy-start = (f32[3,2,32,128]{3,2,1,0:T(8,128)S(1)}, f32[3,2,32,128]{3,2,1,0:T(8,128)}, u32[]{:S(2)}) copy-start(f32[3,2,32,128]{3,2,1,0:T(8,128)} %disp.3) | copy-start | bytes 294916
  17.2 8.0 %copy-start.3 = (s32[2]{0:T(128)S(1)}, s32[2]{0:T(128)}, u32[]{:S(2)}) copy-start(s32[2]{0:T(128)} %node.3) | copy-start | bytes 28
  23.9 31.9 %copy-start.1 = (f32[3,1,32,128]{3,2,1,0:T(8,128)}, f32[3,1,32,128]{3,2,1,0:T(8,128)S(1)}, u32[]{:S(2)}) copy-start(f32[3,1,32,128]{3,2,1,0:T(8,128)S(1)} %collective-permute-done.before) | copy-start | bytes 147460
  24.0 31.9 %copy-start.2 = (f32[3,1,32,128]{3,2,1,0:T(8,128)}, f32[3,1,32,128]{3,2,1,0:T(8,128)S(1)}, u32[]{:S(2)}) copy-start(f32[3,1,32,128]{3,2,1,0:T(8,128)S(1)} %collective-permute-done.1.after) | copy-start | bytes 147460
  24.4 23.3 %collective-permute-start.4 = (f32[120,64,128]{2,1,0:T(8,128)}, f32[120,64,128]{2,1,0:T(8,128)}, u32[]{:S(2)}, u32[]{:S(2)}) collective-permute-start(f32[120,64,128]{2,1,0:T(8,128)} %pack.1.own_hbm), channel_id=1, source_target_pairs={{0,1},{1,0},{2,3},{3,2},{4,5},{5,4},{6,7},{7,6},{8,9},{9,8},{10,11... | collective-permute-start | bytes 11796488 | tf_op jit(solution)/shard_map/ppermute | solution.py:433
  24.6 23.1 %collective-permute-start.5 = (f32[18,64,128]{2,1,0:T(8,128)S(1)}, f32[18,64,128]{2,1,0:T(8,128)S(1)}, u32[]{:S(2)}, u32[]{:S(2)}) collective-permute-start(f32[18,64,128]{2,1,0:T(8,128)S(1)} %collective-permute-done.2.near), channel_id=1, source_target_pairs={{0,1},{1,0},{2,3},{3,2},{4,5},{5,4},{6,7},{7,6},{8,9},{9,8},{10,11... | collective-permute-start | bytes 1769480 | tf_op jit(solution)/shard_map/ppermute | solution.py:433
  24.9 22.8 %collective-permute-start.6 = (f32[18,64,128]{2,1,0:T(8,128)S(1)}, f32[18,64,128]{2,1,0:T(8,128)S(1)}, u32[]{:S(2)}, u32[]{:S(2)}) collective-permute-start(f32[18,64,128]{2,1,0:T(8,128)S(1)} %collective-permute-done.3.far), channel_id=1, source_target_pairs={{0,1},{1,0},{2,3},{3,2},{4,5},{5,4},{6,7},{7,6},{8,9},{9,8},{10,11... | collective-permute-start | bytes 1769480 | tf_op jit(solution)/shard_map/ppermute | solution.py:433
  26.6 21.0 %all-to-all-start = ((f32[128,1,128]{2,1,0:T(1,128)}), f32[128,1,128]{2,1,0:T(1,128)S(1)}, u32[]{:S(2)}, u32[]{:S(2)}) async-start(f32[128,1,128]{2,1,0:T(1,128)} %bitcast.8), calls=%async_computation | async-start | bytes 131072 | tf_op jit(solution)/shard_map/all_to_all | solution.py:473
  55.9 21.7 %collective-permute-start.7 = (f32[24,64,128]{2,1,0:T(8,128)S(1)}, f32[24,64,128]{2,1,0:T(8,128)S(1)}, u32[]{:S(2)}, u32[]{:S(2)}) collective-permute-start(f32[24,64,128]{2,1,0:T(8,128)S(1)} %get-tuple-element.31.refs_1_), channel_id=1, source_target_pairs={{0,2},{1,3},{2,4},{3,5},{4,6},{5,7},{6,8},{7,9},{8,10},{9,11},{10,... | collective-permute-start | bytes 2359304 | tf_op jit(solution)/shard_map/ppermute | solution.py:433
  56.2 21.3 %collective-permute-start.8 = (f32[24,64,128]{2,1,0:T(8,128)S(1)}, f32[24,64,128]{2,1,0:T(8,128)S(1)}, u32[]{:S(2)}, u32[]{:S(2)}) collective-permute-start(f32[24,64,128]{2,1,0:T(8,128)S(1)} %get-tuple-element.30.refs_0_), channel_id=1, source_target_pairs={{0,30},{1,31},{2,0},{3,1},{4,2},{5,3},{6,4},{7,5},{8,6},{9,7},{10,... | collective-permute-start | bytes 2359304 | tf_op jit(solution)/shard_map/ppermute | solution.py:433
  83.6 19.4 %collective-permute-start.10 = (f32[24,64,128]{2,1,0:T(8,128)S(1)}, f32[24,64,128]{2,1,0:T(8,128)S(1)}, u32[]{:S(2)}, u32[]{:S(2)}) collective-permute-start(f32[24,64,128]{2,1,0:T(8,128)S(1)} %get-tuple-element.32.refs_0_), channel_id=1, source_target_pairs={{0,30},{1,31},{2,0},{3,1},{4,2},{5,3},{6,4},{7,5},{8,6},{9,7},{10,... | collective-permute-start | bytes 2359304 | tf_op jit(solution)/shard_map/ppermute | solution.py:433
  88.1 20.1 %collective-permute-start.9 = (f32[24,64,128]{2,1,0:T(8,128)S(1)}, f32[24,64,128]{2,1,0:T(8,128)S(1)}, u32[]{:S(2)}, u32[]{:S(2)}) collective-permute-start(f32[24,64,128]{2,1,0:T(8,128)S(1)} %get-tuple-element.33.refs_1_), channel_id=1, source_target_pairs={{0,2},{1,3},{2,4},{3,5},{4,6},{5,7},{6,8},{7,9},{8,10},{9,11},{10,... | collective-permute-start | bytes 2359304 | tf_op jit(solution)/shard_map/ppermute | solution.py:433
  114.3 19.1 %collective-permute-start.11 = (f32[24,64,128]{2,1,0:T(8,128)S(1)}, f32[24,64,128]{2,1,0:T(8,128)S(1)}, u32[]{:S(2)}, u32[]{:S(2)}) collective-permute-start(f32[24,64,128]{2,1,0:T(8,128)S(1)} %get-tuple-element.35.refs_1_), channel_id=1, source_target_pairs={{0,2},{1,3},{2,4},{3,5},{4,6},{5,7},{6,8},{7,9},{8,10},{9,11},{10,... | collective-permute-start | bytes 2359304 | tf_op jit(solution)/shard_map/ppermute | solution.py:433
  114.4 19.0 %collective-permute-start.12 = (f32[24,64,128]{2,1,0:T(8,128)S(1)}, f32[24,64,128]{2,1,0:T(8,128)S(1)}, u32[]{:S(2)}, u32[]{:S(2)}) collective-permute-start(f32[24,64,128]{2,1,0:T(8,128)S(1)} %get-tuple-element.34.refs_0_), channel_id=1, source_target_pairs={{0,30},{1,31},{2,0},{3,1},{4,2},{5,3},{6,4},{7,5},{8,6},{9,7},{10,... | collective-permute-start | bytes 2359304 | tf_op jit(solution)/shard_map/ppermute | solution.py:433
  139.5 18.1 %collective-permute-start.13 = (f32[24,64,128]{2,1,0:T(8,128)S(1)}, f32[24,64,128]{2,1,0:T(8,128)S(1)}, u32[]{:S(2)}, u32[]{:S(2)}) collective-permute-start(f32[24,64,128]{2,1,0:T(8,128)S(1)} %get-tuple-element.37.x_1), channel_id=1, source_target_pairs={{0,2},{1,3},{2,4},{3,5},{4,6},{5,7},{6,8},{7,9},{8,10},{9,11},{10,... | collective-permute-start | bytes 2359304 | tf_op jit(solution)/shard_map/ppermute | solution.py:433
  139.6 38.8 %copy-start.4 = (f32[2,18]{1,0:T(2,128)S(1)}, f32[2,18]{1,0:T(2,128)}, u32[]{:S(2)}) copy-start(f32[2,18]{1,0:T(2,128)} %param.17) | copy-start | bytes 436
  139.6 18.0 %collective-permute-start.14 = (f32[24,64,128]{2,1,0:T(8,128)S(1)}, f32[24,64,128]{2,1,0:T(8,128)S(1)}, u32[]{:S(2)}, u32[]{:S(2)}) collective-permute-start(f32[24,64,128]{2,1,0:T(8,128)S(1)} %get-tuple-element.36.x_0), channel_id=1, source_target_pairs={{0,30},{1,31},{2,0},{3,1},{4,2},{5,3},{6,4},{7,5},{8,6},{9,7},{10,... | collective-permute-start | bytes 2359304 | tf_op jit(solution)/shard_map/ppermute | solution.py:433
  165.8 22.1 %all-to-all-start.1 = ((f32[128,1,128]{2,1,0:T(1,128)}), f32[128,1,128]{2,1,0:T(1,128)S(1)}, u32[]{:S(2)}, u32[]{:S(2)}) async-start(f32[128,1,128]{2,1,0:T(1,128)} %bitcast.10), calls=%async_computation.1 | async-start | bytes 131072 | tf_op jit(solution)/shard_map/all_to_all | solution.py:509

commit v2 on v1

--- a/solution.py
+++ b/solution.py
@@ -10,10 +10,12 @@
 SHARE = RELAX / 6.0
 ROWS = 64
 LANES = 128
-SLOTS = 2
+PER_CORE = 2
+SLOTS = 1
 FIELDS = SLOTS * 6
 VMEM_LIMIT = 16 * 1024 * 1024
-GROUP = 12
+GROUP = 6
+CHUNK = 16
 HALF = 18
 F32 = jnp.float32
 
@@ -40,10 +42,10 @@
 
 def chunks(body):
     def step(k, carry):
-        body(pl.ds(pl.multiple_of(k * 8, 8), 8))
+        body(pl.ds(pl.multiple_of(k * CHUNK, CHUNK), CHUNK))
         return carry
 
-    lax.fori_loop(0, ROWS // 8, step, 0)
+    lax.fori_loop(0, ROWS // CHUNK, step, 0)
 
 
 def elastic(diag, off, put):
@@ -83,15 +85,15 @@
     return [pltpu.with_memory_space_constraint(v, pltpu.HBM) for v in arrays]
 
 
-def pack(kernel, name, micros, operands, planes):
-    block = lambda n: pl.BlockSpec((n, 8, LANES), lambda k: (0, k, 0))
+def pack(kernel, name, micros, operands, planes, rows):
+    block = lambda n: pl.BlockSpec((n, rows, LANES), lambda k: (0, k, 0))
     return pl.pallas_call(
         kernel,
         name=name,
         cost_estimate=cost(micros),
-        grid=(ROWS // 8,),
+        grid=(ROWS // rows,),
         in_specs=[
-            block(v.shape[0]) if v.ndim == 3 else pl.BlockSpec((8, LANES), lambda k: (k, 0))
+            block(v.shape[0]) if v.ndim == 3 else pl.BlockSpec((rows, LANES), lambda k: (k, 0))
             for v in operands
         ],
         out_specs=[block(n) for n in planes],
@@ -177,9 +179,8 @@
     pl.when(side[0] == 1)(lambda: run(whole(other), whole(own), late, early))
 
 
-def first_kernel(
-    side, ebar, own_hbm, other_hbm, near, far, rest_near, rest_far, x_0, x_1, own, other, e_0, e_1, t_0, t_1, sems
-):
+def fetch_kernel(side, ebar, own_hbm, other_hbm, near, far, rest_near, rest_far, x_0, x_1, own, other, *refs):
+    temps, sems = refs[:4], refs[4]
     copies = [
         pltpu.make_async_copy(src.at[low:high], dst.at[low:high], sems.at[k])
         for k, (src, dst, low, high) in enumerate(
@@ -193,15 +194,28 @@
     ]
     for copy in copies:
         copy.start()
-    copies[0].wait()
-    copies[1].wait()
+
+    def ready(k):
+        copies[k].wait()
+        copies[k + 1].wait()
+
+    first_sweep(side, ebar, (own, other, near, far, rest_near, rest_far), (x_0, x_1), temps, ready)
+
+
+def first_kernel(side, ebar, own, other, near, far, rest_near, rest_far, x_0, x_1, *temps):
+    first_sweep(side, ebar, (own, other, near, far, rest_near, rest_far), (x_0, x_1), temps, lambda k: None)
+
+
+def first_sweep(side, ebar, coefficients, outs, temps, ready):
+    x_0, x_1 = outs
+    e_0, e_1, t_0, t_1 = temps
 
     def start(c_0, c_1, g_0, g_1):
         for c, g, t_ref, e_ref in ((c_0, g_0, t_0, e_0), (c_1, g_1, t_1, e_1)):
 
             def body(at, c=c, g=g, t_ref=t_ref, e_ref=e_ref):
                 strain = [
-                    [jnp.full((8, LANES), ebar[s, i], F32) for i in range(6)] for s in range(SLOTS)
+                    [jnp.full((CHUNK, LANES), ebar[s, i], F32) for i in range(6)] for s in range(SLOTS)
                 ]
                 sig = times(c, at, strain)
                 outer = times(g, at, strain)
@@ -211,11 +225,10 @@
 
             chunks(body)
 
-    coefficients = (own, other, near, far, rest_near, rest_far)
+    ready(0)
     split(side, coefficients, start)
     beside(t_0, t_1, e_0, e_1)
-    copies[2].wait()
-    copies[3].wait()
+    ready(2)
     split(side, coefficients, lambda c_0, c_1, g_0, g_1: advance(((c_0, t_0, e_0, x_0), (c_1, t_1, e_1, x_1))))
     beside_own(x_0, x_1)
 
@@ -268,7 +281,7 @@
     def run(c_0, c_1, g_0, g_1):
         two_sweeps(c_0, c_1, g_0, g_1, x_0, x_1, f_0, f_1, y_0, y_1, *temps)
         for k in range(FIELDS):
-            out[k] = jnp.zeros((8, LANES), F32)
+            out[k] = jnp.zeros((CHUNK, LANES), F32)
         for y_ref, c, g in ((y_0, c_0, g_0), (y_1, c_1, g_1)):
 
             def body(at, y_ref=y_ref, c=c, g=g):
@@ -446,15 +459,15 @@
 
     diag = moduli_diag[0, :, 0]
     off = moduli_off[0, :, 0]
-    low, high = pack(edge_kernel, "edge", 0.1, (diag, off), (HALF, HALF))
+    low, high = pack(edge_kernel, "edge", 0.1, (diag, off), (HALF, HALF), 32)
     near = over(low, across)
     far = over(high, along)
-    flow = rate[0, 0]
-    flow, low, high = lax.optimization_barrier((flow, low, high))
+    flow, low, high = lax.optimization_barrier((rate[0, 0], low, high))
     own = pack(
-        pack_kernel, "pack", 0.1, (diag, off, schmid[0, :, 0], crss[0, :, 0], branch[0, 0], flow), (120,)
+        pack_kernel, "pack", 0.1, (diag, off, schmid[0, :, 0], crss[0, :, 0], branch[0, 0], flow), (120,), 16
     )[0]
-    before, after, own, near, far = lax.optimization_barrier((before, after, own, near, far))
+    other = over(own, partner)
+    before, after, near, far, own = lax.optimization_barrier((before, after, near, far, own))
     core = member % 2
 
     where = member.reshape(1).astype(jnp.int32)
@@ -466,13 +479,12 @@
         [(8, LANES)],
         [pltpu.VMEM((3, 4, 32, LANES), F32)],
     )(point_node, point_owner, where, displacement, before, after)[0]
-    other = over(own, partner)
     rest_near = over(near, partner)
     rest_far = over(far, partner)
     message = jnp.broadcast_to(message[:groups, None, None, :], (groups, members, 1, LANES))
     arrived = lax.all_to_all(message.reshape(everyone, 1, LANES), both, 0, 0, tiled=True)
     strains = jnp.sum(arrived.reshape(groups, members, LANES), axis=1)
-    ebar = lax.dynamic_slice_in_dim(strains, core * SLOTS, SLOTS, axis=0)
+    ebar = [lax.dynamic_slice_in_dim(strains, core * PER_CORE + k, 1, axis=0) for k in range(PER_CORE)]
 
     base = stencil(stiffness, displacement, before, after, external)
 
@@ -483,28 +495,36 @@
     ghosts = (near, far, rest_near, rest_far)
     ANY = pl.BlockSpec(memory_space=pl.ANY)
     x_0, x_1, own, other = call(
-        first_kernel,
-        "first",
+        fetch_kernel,
+        "fetch",
         5,
         [SM] * 2 + [ANY] * 2 + [VM] * 4,
         [packed] * 2 + [(120, ROWS, LANES)] * 2,
         temps + [pltpu.SemaphoreType.DMA((4,))],
-    )(side, ebar, *in_hbm(own, other), *ghosts)
+    )(side, ebar[0], *in_hbm(own, other), *ghosts)
     fixed = (own, other, *ghosts)
+    state = [(x_0, x_1)]
+    for k in range(1, PER_CORE):
+        state.append(
+            call(first_kernel, "first", 5, [SM] * 2 + [VM] * 6, [packed] * 2, temps)(side, ebar[k], *fixed)
+        )
+    sums = []
     for pair in range(4):
-        f_0 = over(x_1, rightward)
-        f_1 = over(x_0, leftward)
-        operands = (side, *fixed, x_0, x_1, f_0, f_1)
-        if pair < 3:
-            x_0, x_1 = call(pair_kernel, "pair", 5, [SM] + [VM] * 10, [packed] * 2, temps)(*operands)
-        else:
-            sizes = [pltpu.VMEM(packed, F32)] * 2 + temps
-            sums = call(last_kernel, "last", 6, [SM] + [VM] * 10, [(FIELDS, 8, LANES)], sizes)(*operands)[0]
-
-    totals = jnp.sum(sums, axis=(1, 2)).reshape(SLOTS, 6)
+        for k in range(PER_CORE):
+            x_0, x_1 = state[k]
+            f_0 = over(x_1, rightward)
+            f_1 = over(x_0, leftward)
+            operands = (side, *fixed, x_0, x_1, f_0, f_1)
+            if pair < 3:
+                state[k] = call(pair_kernel, "pair", 5, [SM] + [VM] * 10, [packed] * 2, temps)(*operands)
+            else:
+                sizes = [pltpu.VMEM(packed, F32)] * 2 + temps
+                sums += call(last_kernel, "last", 6, [SM] + [VM] * 10, [(FIELDS, CHUNK, LANES)], sizes)(*operands)
+
+    totals = jnp.stack([jnp.sum(v, axis=(1, 2)) for v in lax.optimization_barrier(sums)])
     totals = jnp.pad(totals, ((0, 0), (0, LANES - 6)))
     mine = jnp.zeros((groups, LANES), F32)
-    mine = lax.dynamic_update_slice_in_dim(mine, totals, core * SLOTS, axis=0)
+    mine = lax.dynamic_update_slice_in_dim(mine, totals, core * PER_CORE, axis=0)
     reply = jnp.broadcast_to(mine[:, None, None, :], (groups, members, 1, LANES))
     received = lax.all_to_all(reply.reshape(everyone, 1, LANES), both, 0, 0, tiled=True)
     loads = jnp.pad(point_load.reshape(-1, 3, 6), ((0, 0), (0, 0), (0, LANES - 6)))

time: 190 us -> 163 us (0.86)
  waiting for transfers between devices: 77.6 us -> 32.8 us
  starting transfers between devices: 55.5 us -> 75.9 us
    ppermute x15 -> x23, waiting for transfers between devices: 64.9 us -> 20.1 us  [over(): return lax.ppermute(value, axis, pairs)]
    ppermute x15 -> x23, starting transfers between devices: 31.5 us -> 51.3 us  [over(): return lax.ppermute(value, axis, pairs)]
    pallas_call x2, Pallas kernels: 10.7 us -> 6.16 us  [pack(): pl.pallas_call(kernel, name=name, cost_estimate=cost(micros), grid=(ROWS...]
    pallas_call x2 -> x4, Pallas kernels: 15.4 us -> 17.4 us  [the longest x2 7.43 us: per_device(): call(last_kernel, 'last', 6, [SM] + [VM] * 10, [(FIELDS, CHUNK, LANES)],...]
    pallas_call x3 -> x6, Pallas kernels: 18.2 us -> 19.3 us  [per_device(): call(pair_kernel, 'pair', 5, [SM] + [VM] * 10, [packed] * 2, temps)]
  transfers between devices with their start and end apart: 17 -> 25, of which waited for: 8 -> 10; matrix products, arithmetic and copies ran while one was open for 1% -> 1% of each run, Pallas kernels for 7% -> 18%
where the time goes in v2:
time: 163 us
  starting transfers between devices  75.9 us (47%)
  Pallas kernels  51.1 us (31%)
  waiting for transfers between devices  32.8 us (20%)
    ppermute x23, starting transfers between devices, over(): return lax.ppermute(value, axis, pairs)  51.3 us
    ppermute x23, waiting for transfers between devices, over(): return lax.ppermute(value, axis, pairs)  20.1 us
    pallas_call x6, Pallas kernels, per_device(): call(pair_kernel, 'pair', 5, [SM] + [VM] * 10, [packed] * 2, temps)  19.3 us
    all_to_all x1, starting transfers between devices, per_device(): lax.all_to_all(reply.reshape(everyone, 1, LANES), both, 0, 0, tiled=True)  13.1 us
    all_to_all x1, starting transfers between devices, per_device(): lax.all_to_all(message.reshape(everyone, 1, LANES), both, 0, 0, tiled=True)  11.6 us
    all_to_all x1, waiting for transfers between devices, per_device(): lax.all_to_all(message.reshape(everyone, 1, LANES), both, 0, 0, tiled=True)  9.51 us
    pallas_call x2, Pallas kernels, per_device(): call(last_kernel, 'last', 6, [SM] + [VM] * 10, [(FIELDS, CHUNK, LANES)],...  7.43 us
    pallas_call x1, Pallas kernels, per_device(): call(fetch_kernel, 'fetch', 5, [SM] * 2 + [ANY] * 2 + [VM] * 4, [packed]...  6.34 us
  transfers between devices with their start and end apart: 25, of which 10 were waited for; matrix products, arithmetic and copies ran while one was open for 1% of the time, Pallas kernels for 18%

profile of v2, /device:TPU:1, one launch (start us, length us, event | category | flops | bytes accessed | tf_op | source)
XLA Modules:
  0.0 162.6 jit_solution(6837827764905045150)
XLA Ops:
  0.6 1.5 edge.1
  2.1 0.0 copy-start
  2.1 0.0 copy-start.5
  2.1 0.0 copy-start.3
  2.1 4.7 %pack.1.own_hbm = f32[120,64,128]{2,1,0:T(8,128)} custom-call(f32[6,64,128]{2,1,0:T(8,128)} %bitcast.21, f32[36,64,128]{2,1,0:T(8,128)} %bitcast.18, f32[72,64,128]{2,1,0:T(8,128)} %bitcast.19, f32[12,64,128]{2,1,0:T(8,128)} %bitcast.22, s32[64,128]{1,0:T(8,128)} %bitcast.24, f32[64,128]{1,0:T(8,128)} %bitcast.25), custom_call_target="tpu_custom_call" | custom-call | bytes 360000 | tf_op jit(solution)/shard_map/pack/pallas_call | solution.py:90
  6.8 1.4 collective-permute-start.4
  8.3 1.3 collective-permute-start.2
  9.5 1.2 collective-permute-start.3
  10.7 6.5 %collective-permute-start = (f32[3,1,32,128]{3,2,1,0:T(8,128)S(1)}, f32[3,1,32,128]{3,2,1,0:T(8,128)S(1)}, u32[]{:S(2)}, u32[]{:S(2)}) collective-permute-start(f32[3,1,32,128]{3,2,1,0:T(8,128)S(1)} %get-tuple-element.59), channel_id=1, source_target_pairs={{0,1},{1,2},{2,3},{3,4},{4,5},{5,6},{6,7},{7,8},{8,9},{9,10},{10,1... | collective-permute-start | bytes 147464 | tf_op jit(solution)/shard_map/ppermute | solution.py:446
  17.2 1.9 %collective-permute-start.1 = (f32[3,1,32,128]{3,2,1,0:T(8,128)S(1)}, f32[3,1,32,128]{3,2,1,0:T(8,128)S(1)}, u32[]{:S(2)}, u32[]{:S(2)}) collective-permute-start(f32[3,1,32,128]{3,2,1,0:T(8,128)S(1)} %get-tuple-element.58), channel_id=1, source_target_pairs={{1,0},{2,1},{3,2},{4,3},{5,4},{6,5},{7,6},{8,7},{9,8},{10,9},{11,1... | collective-permute-start | bytes 147464 | tf_op jit(solution)/shard_map/ppermute | solution.py:446
  19.2 4.0 %collective-permute-done.before = f32[3,1,32,128]{3,2,1,0:T(8,128)S(1)} collective-permute-done((f32[3,1,32,128]{3,2,1,0:T(8,128)S(1)}, f32[3,1,32,128]{3,2,1,0:T(8,128)S(1)}, u32[]{:S(2)}, u32[]{:S(2)}) %collective-permute-start) | collective-permute-done | bytes 49184 | tf_op jit(solution)/shard_map/ppermute | solution.py:446
  23.2 1.2 collective-permute-done.1.after
  24.4 0.0 collective-permute-done.2.near
  24.4 2.4 %collective-permute-done.3.far = f32[18,64,128]{2,1,0:T(8,128)S(1)} collective-permute-done((f32[18,64,128]{2,1,0:T(8,128)S(1)}, f32[18,64,128]{2,1,0:T(8,128)S(1)}, u32[]{:S(2)}, u32[]{:S(2)}) %collective-permute-start.3) | collective-permute-done | bytes 589856 | tf_op jit(solution)/shard_map/ppermute | solution.py:446
  26.9 0.5 collective-permute-start.5
  27.4 0.1 copy.19.owner
  27.5 0.7 strain.1
  28.2 0.6 broadcast_in_dim.20
  28.9 11.6 %all-to-all-start = ((f32[128,1,128]{2,1,0:T(1,128)}), f32[128,1,128]{2,1,0:T(1,128)S(1)}, u32[]{:S(2)}, u32[]{:S(2)}) async-start(f32[128,1,128]{2,1,0:T(1,128)} %bitcast.8), calls=%async_computation | async-start | bytes 131072 | tf_op jit(solution)/shard_map/all_to_all | solution.py:485
  40.5 9.5 %all-to-all-done = f32[128,1,128]{2,1,0:T(1,128)S(1)} async-done(((f32[128,1,128]{2,1,0:T(1,128)}), f32[128,1,128]{2,1,0:T(1,128)S(1)}, u32[]{:S(2)}, u32[]{:S(2)}) %all-to-all-start) | async-done | bytes 65568 | tf_op jit(solution)/shard_map/all_to_all | solution.py:485
  50.1 0.0 collective-permute-done.5.rest_near
  50.1 0.0 collective-permute-done.4.other_hbm
  50.1 6.3 %fetch.1 = (f32[12,64,128]{2,1,0:T(8,128)S(1)}, f32[12,64,128]{2,1,0:T(8,128)S(1)}, f32[120,64,128]{2,1,0:T(8,128)S(1)}, f32[120,64,128]{2,1,0:T(8,128)S(1)}) custom-call(s32[1]{0:T(128)} %bitcast.1.side, f32[1,128]{1,0:T(1,128)S(1)} %get-tuple-element.61.ebar, f32[120,64,128]{2,1,0:T(8,128)} %pack.1.own_hbm, ...), custom_call_target="tpu_custom_call" | custom-call | bytes 18000000 | tf_op jit(solution)/shard_map/fetch/pallas_call | solution.py:497
  56.5 3.7 %first.1 = (f32[12,64,128]{2,1,0:T(8,128)S(1)}, f32[12,64,128]{2,1,0:T(8,128)S(1)}) custom-call(s32[1]{0:T(128)} %bitcast.1.side, f32[1,128]{1,0:T(1,128)S(1)} %get-tuple-element.60.ebar, f32[120,64,128]{2,1,0:T(8,128)S(1)} %get-tuple-element.38.own, f32[120,64,128]{2,1,0:T(8,128)S(1)} %get-tuple-element.39.other, ...), custom_call_target="tpu_custom_call" | custom-call | bytes 18000000 | tf_op jit(solution)/shard_map/first/pallas_call | solution.py:509
  60.1 0.4 collective-permute-start.15
  60.5 4.5 %collective-permute-start.16 = (f32[12,64,128]{2,1,0:T(8,128)S(1)}, f32[12,64,128]{2,1,0:T(8,128)S(1)}, u32[]{:S(2)}, u32[]{:S(2)}) collective-permute-start(f32[12,64,128]{2,1,0:T(8,128)S(1)} %get-tuple-element.48.refs_0_), channel_id=1, source_target_pairs={{0,30},{1,31},{2,0},{3,1},{4,2},{5,3},{6,4},{7,5},{8,6},{9,7},{10,... | collective-permute-start | bytes 1179656 | tf_op jit(solution)/shard_map/ppermute | solution.py:446
  65.0 0.0 collective-permute-start.7
  65.0 4.8 %collective-permute-start.8 = (f32[12,64,128]{2,1,0:T(8,128)S(1)}, f32[12,64,128]{2,1,0:T(8,128)S(1)}, u32[]{:S(2)}, u32[]{:S(2)}) collective-permute-start(f32[12,64,128]{2,1,0:T(8,128)S(1)} %get-tuple-element.40.refs_0_), channel_id=1, source_target_pairs={{0,30},{1,31},{2,0},{3,1},{4,2},{5,3},{6,4},{7,5},{8,6},{9,7},{10,... | collective-permute-start | bytes 1179656 | tf_op jit(solution)/shard_map/ppermute | solution.py:446
  69.8 3.6 %collective-permute-done.15.refs_2_ = f32[12,64,128]{2,1,0:T(8,128)S(1)} collective-permute-done((f32[12,64,128]{2,1,0:T(8,128)S(1)}, f32[12,64,128]{2,1,0:T(8,128)S(1)}, u32[]{:S(2)}, u32[]{:S(2)}) %collective-permute-start.15) | collective-permute-done | bytes 393248 | tf_op jit(solution)/shard_map/ppermute | solution.py:446
  73.4 3.2 %pair.9 = (f32[12,64,128]{2,1,0:T(8,128)S(1)}, f32[12,64,128]{2,1,0:T(8,128)S(1)}) custom-call(s32[1]{0:T(128)} %bitcast.1.side, f32[120,64,128]{2,1,0:T(8,128)S(1)} %get-tuple-element.38.own, f32[120,64,128]{2,1,0:T(8,128)S(1)} %get-tuple-element.39.other, f32[18,64,128]{2,1,0:T(8,128)S(1)} %collective-permute-done.2.near, ...), custom_call_target="tpu_custom_call" | custom-call | bytes 18000000 | tf_op jit(solution)/shard_map/pair/pallas_call | solution.py:519
  76.6 0.1 collective-permute-start.17
  76.7 4.8 %collective-permute-start.18 = (f32[12,64,128]{2,1,0:T(8,128)S(1)}, f32[12,64,128]{2,1,0:T(8,128)S(1)}, u32[]{:S(2)}, u32[]{:S(2)}) collective-permute-start(f32[12,64,128]{2,1,0:T(8,128)S(1)} %get-tuple-element.50.refs_0_), channel_id=1, source_target_pairs={{0,30},{1,31},{2,0},{3,1},{4,2},{5,3},{6,4},{7,5},{8,6},{9,7},{10,... | collective-permute-start | bytes 1179656 | tf_op jit(solution)/shard_map/ppermute | solution.py:446
  81.5 0.4 collective-permute-done.7.refs_2_
  81.8 3.2 %pair.6 = (f32[12,64,128]{2,1,0:T(8,128)S(1)}, f32[12,64,128]{2,1,0:T(8,128)S(1)}) custom-call(s32[1]{0:T(128)} %bitcast.1.side, f32[120,64,128]{2,1,0:T(8,128)S(1)} %get-tuple-element.38.own, f32[120,64,128]{2,1,0:T(8,128)S(1)} %get-tuple-element.39.other, f32[18,64,128]{2,1,0:T(8,128)S(1)} %collective-permute-done.2.near, ...), custom_call_target="tpu_custom_call" | custom-call | bytes 18000000 | tf_op jit(solution)/shard_map/pair/pallas_call | solution.py:519
  85.1 4.5 %collective-permute-start.10 = (f32[12,64,128]{2,1,0:T(8,128)S(1)}, f32[12,64,128]{2,1,0:T(8,128)S(1)}, u32[]{:S(2)}, u32[]{:S(2)}) collective-permute-start(f32[12,64,128]{2,1,0:T(8,128)S(1)} %get-tuple-element.42.refs_0_), channel_id=1, source_target_pairs={{0,30},{1,31},{2,0},{3,1},{4,2},{5,3},{6,4},{7,5},{8,6},{9,7},{10,... | collective-permute-start | bytes 1179656 | tf_op jit(solution)/shard_map/ppermute | solution.py:446
  89.6 0.0 collective-permute-start.9
  89.6 0.0 collective-permute-done.17.refs_2_
  89.6 0.0 collective-permute-done.18.refs_3_
  89.6 3.2 %pair.10 = (f32[12,64,128]{2,1,0:T(8,128)S(1)}, f32[12,64,128]{2,1,0:T(8,128)S(1)}) custom-call(s32[1]{0:T(128)} %bitcast.1.side, f32[120,64,128]{2,1,0:T(8,128)S(1)} %get-tuple-element.38.own, f32[120,64,128]{2,1,0:T(8,128)S(1)} %get-tuple-element.39.other, f32[18,64,128]{2,1,0:T(8,128)S(1)} %collective-permute-done.2.near, ...), custom_call_target="tpu_custom_call" | custom-call | bytes 18000000 | tf_op jit(solution)/shard_map/pair/pallas_call | solution.py:519
  92.8 0.1 collective-permute-start.19
  92.9 4.8 %collective-permute-start.20 = (f32[12,64,128]{2,1,0:T(8,128)S(1)}, f32[12,64,128]{2,1,0:T(8,128)S(1)}, u32[]{:S(2)}, u32[]{:S(2)}) collective-permute-start(f32[12,64,128]{2,1,0:T(8,128)S(1)} %get-tuple-element.52.refs_0_), channel_id=1, source_target_pairs={{0,30},{1,31},{2,0},{3,1},{4,2},{5,3},{6,4},{7,5},{8,6},{9,7},{10,... | collective-permute-start | bytes 1179656 | tf_op jit(solution)/shard_map/ppermute | solution.py:446
  97.8 3.2 %collective-permute-done.9.refs_2_ = f32[12,64,128]{2,1,0:T(8,128)S(1)} collective-permute-done((f32[12,64,128]{2,1,0:T(8,128)S(1)}, f32[12,64,128]{2,1,0:T(8,128)S(1)}, u32[]{:S(2)}, u32[]{:S(2)}) %collective-permute-start.9) | collective-permute-done | bytes 393248 | tf_op jit(solution)/shard_map/ppermute | solution.py:446
  100.9 3.2 %pair.7 = (f32[12,64,128]{2,1,0:T(8,128)S(1)}, f32[12,64,128]{2,1,0:T(8,128)S(1)}) custom-call(s32[1]{0:T(128)} %bitcast.1.side, f32[120,64,128]{2,1,0:T(8,128)S(1)} %get-tuple-element.38.own, f32[120,64,128]{2,1,0:T(8,128)S(1)} %get-tuple-element.39.other, f32[18,64,128]{2,1,0:T(8,128)S(1)} %collective-permute-done.2.near, ...), custom_call_target="tpu_custom_call" | custom-call | bytes 18000000 | tf_op jit(solution)/shard_map/pair/pallas_call | solution.py:519
  104.2 0.1 collective-permute-start.11
  104.2 4.8 %collective-permute-start.12 = (f32[12,64,128]{2,1,0:T(8,128)S(1)}, f32[12,64,128]{2,1,0:T(8,128)S(1)}, u32[]{:S(2)}, u32[]{:S(2)}) collective-permute-start(f32[12,64,128]{2,1,0:T(8,128)S(1)} %get-tuple-element.44.refs_0_), channel_id=1, source_target_pairs={{0,30},{1,31},{2,0},{3,1},{4,2},{5,3},{6,4},{7,5},{8,6},{9,7},{10,... | collective-permute-start | bytes 1179656 | tf_op jit(solution)/shard_map/ppermute | solution.py:446
  109.0 0.4 collective-permute-done.19.refs_2_
  109.4 3.2 %pair.11 = (f32[12,64,128]{2,1,0:T(8,128)S(1)}, f32[12,64,128]{2,1,0:T(8,128)S(1)}) custom-call(s32[1]{0:T(128)} %bitcast.1.side, f32[120,64,128]{2,1,0:T(8,128)S(1)} %get-tuple-element.38.own, f32[120,64,128]{2,1,0:T(8,128)S(1)} %get-tuple-element.39.other, f32[18,64,128]{2,1,0:T(8,128)S(1)} %collective-permute-done.2.near, ...), custom_call_target="tpu_custom_call" | custom-call | bytes 18000000 | tf_op jit(solution)/shard_map/pair/pallas_call | solution.py:519
  112.6 0.1 collective-permute-start.21
  112.7 4.8 %collective-permute-start.22 = (f32[12,64,128]{2,1,0:T(8,128)S(1)}, f32[12,64,128]{2,1,0:T(8,128)S(1)}, u32[]{:S(2)}, u32[]{:S(2)}) collective-permute-start(f32[12,64,128]{2,1,0:T(8,128)S(1)} %get-tuple-element.54.x_0), channel_id=1, source_target_pairs={{0,30},{1,31},{2,0},{3,1},{4,2},{5,3},{6,4},{7,5},{8,6},{9,7},{10,... | collective-permute-start | bytes 1179656 | tf_op jit(solution)/shard_map/ppermute | solution.py:446
  117.5 3.2 %pair.8 = (f32[12,64,128]{2,1,0:T(8,128)S(1)}, f32[12,64,128]{2,1,0:T(8,128)S(1)}) custom-call(s32[1]{0:T(128)} %bitcast.1.side, f32[120,64,128]{2,1,0:T(8,128)S(1)} %get-tuple-element.38.own, f32[120,64,128]{2,1,0:T(8,128)S(1)} %get-tuple-element.39.other, f32[18,64,128]{2,1,0:T(8,128)S(1)} %collective-permute-done.2.near, ...), custom_call_target="tpu_custom_call" | custom-call | bytes 18000000 | tf_op jit(solution)/shard_map/pair/pallas_call | solution.py:519
  120.7 0.1 collective-permute-start.13
  120.8 4.8 %collective-permute-start.14 = (f32[12,64,128]{2,1,0:T(8,128)S(1)}, f32[12,64,128]{2,1,0:T(8,128)S(1)}, u32[]{:S(2)}, u32[]{:S(2)}) collective-permute-start(f32[12,64,128]{2,1,0:T(8,128)S(1)} %get-tuple-element.46.x_0), channel_id=1, source_target_pairs={{0,30},{1,31},{2,0},{3,1},{4,2},{5,3},{6,4},{7,5},{8,6},{9,7},{10,... | collective-permute-start | bytes 1179656 | tf_op jit(solution)/shard_map/ppermute | solution.py:446
  125.5 3.7 %last.3 = f32[6,16,128]{2,1,0:T(8,128)S(1)} custom-call(s32[1]{0:T(128)} %bitcast.1.side, f32[120,64,128]{2,1,0:T(8,128)S(1)} %get-tuple-element.38.own, f32[120,64,128]{2,1,0:T(8,128)S(1)} %get-tuple-element.39.other, f32[18,64,128]{2,1,0:T(8,128)S(1)} %collective-permute-done.2.near, f32[18,64,128]{2,1,0:T(8,128)S(1)} %collective-permute-done.3.far, ...), custom_call_target="tpu_custom_call" | custom-call | bytes 21600000 | tf_op jit(solution)/shard_map/last/pallas_call | solution.py:522
  129.3 0.0 copy-start.4
  129.3 4.8 %collective-permute-done.13.f_0 = f32[12,64,128]{2,1,0:T(8,128)S(1)} collective-permute-done((f32[12,64,128]{2,1,0:T(8,128)S(1)}, f32[12,64,128]{2,1,0:T(8,128)S(1)}, u32[]{:S(2)}, u32[]{:S(2)}) %collective-permute-start.13) | collective-permute-done | bytes 393248 | tf_op jit(solution)/shard_map/ppermute | solution.py:446
  134.1 3.7 %last.2 = f32[6,16,128]{2,1,0:T(8,128)S(1)} custom-call(s32[1]{0:T(128)} %bitcast.1.side, f32[120,64,128]{2,1,0:T(8,128)S(1)} %get-tuple-element.38.own, f32[120,64,128]{2,1,0:T(8,128)S(1)} %get-tuple-element.39.other, f32[18,64,128]{2,1,0:T(8,128)S(1)} %collective-permute-done.2.near, f32[18,64,128]{2,1,0:T(8,128)S(1)} %collective-permute-done.3.far, ...), custom_call_target="tpu_custom_call" | custom-call | bytes 21600000 | tf_op jit(solution)/shard_map/last/pallas_call | solution.py:522
  137.8 0.1 reduce_sum.28
  137.9 0.1 reduce_sum.29
  138.1 0.6 broadcast_in_dim.22
  138.7 13.1 %all-to-all-start.1 = ((f32[128,1,128]{2,1,0:T(1,128)}), f32[128,1,128]{2,1,0:T(1,128)S(1)}, u32[]{:S(2)}, u32[]{:S(2)}) async-start(f32[128,1,128]{2,1,0:T(1,128)} %bitcast.12), calls=%async_computation.1 | async-start | bytes 131072 | tf_op jit(solution)/shard_map/all_to_all | solution.py:529
  151.8 0.1 reshape.43
  151.9 6.2 %stencil.1.base = f32[3,2,32,128]{3,2,1,0:T(8,128)S(1)} custom-call(bf16[27,3,3,2,32,128]{5,4,3,2,1,0:T(8,128)(2,1)} %blocks.1, f32[3,2,32,128]{3,2,1,0:T(8,128)} %disp.3, f32[3,1,32,128]{3,2,1,0:T(8,128)} %copy-done.1, f32[3,1,32,128]{3,2,1,0:T(8,128)} %copy-done.2, f32[3,2,32,128]{3,2,1,0:T(8,128)} %external.1), custom_call_target="tpu_custom_call" | custom-call | bytes 18000000 | tf_op jit(solution)/shard_map/stencil/pallas_call | solution.py:381
  158.1 3.2 %all-to-all-done.1 = f32[128,1,128]{2,1,0:T(1,128)S(1)} async-done(((f32[128,1,128]{2,1,0:T(1,128)}), f32[128,1,128]{2,1,0:T(1,128)S(1)}, u32[]{:S(2)}, u32[]{:S(2)}) %all-to-all-start.1) | async-done | bytes 65568 | tf_op jit(solution)/shard_map/all_to_all | solution.py:529
  161.3 1.3 final.1
  (26 shorter events, 0.1 us)
Async XLA Ops:
  2.1 8.6 %copy-start = (f32[3,2,32,128]{3,2,1,0:T(8,128)S(1)}, f32[3,2,32,128]{3,2,1,0:T(8,128)}, u32[]{:S(2)}) copy-start(f32[3,2,32,128]{3,2,1,0:T(8,128)} %disp.3) | copy-start | bytes 294916
  2.1 25.3 %copy-start.5 = (s32[2,1]{0,1:T(1,128)S(1)}, s32[2,1]{0,1:T(1,128)}, u32[]{:S(2)}) copy-start(s32[2,1]{0,1:T(1,128)} %param.16) | copy-start | bytes 28
  2.1 25.4 %copy-start.3 = (s32[2]{0:T(128)S(1)}, s32[2]{0:T(128)}, u32[]{:S(2)}) copy-start(s32[2]{0:T(128)} %node.3) | copy-start | bytes 28
  6.8 43.2 %collective-permute-start.4 = (f32[120,64,128]{2,1,0:T(8,128)}, f32[120,64,128]{2,1,0:T(8,128)}, u32[]{:S(2)}, u32[]{:S(2)}) collective-permute-start(f32[120,64,128]{2,1,0:T(8,128)} %pack.1.own_hbm), channel_id=1, source_target_pairs={{0,1},{1,0},{2,3},{3,2},{4,5},{5,4},{6,7},{7,6},{8,9},{9,8},{10,11... | collective-permute-start | bytes 11796488 | tf_op jit(solution)/shard_map/ppermute | solution.py:446
  8.3 16.2 %collective-permute-start.2 = (f32[18,64,128]{2,1,0:T(8,128)S(1)}, f32[18,64,128]{2,1,0:T(8,128)S(1)}, u32[]{:S(2)}, u32[]{:S(2)}) collective-permute-start(f32[18,64,128]{2,1,0:T(8,128)S(1)} %get-tuple-element.30), channel_id=1, source_target_pairs={{0,31},{1,2},{2,1},{3,4},{4,3},{5,6},{6,5},{7,8},{8,7},{9,10},{10,... | collective-permute-start | bytes 1769480 | tf_op jit(solution)/shard_map/ppermute | solution.py:446
  9.5 17.3 %collective-permute-start.3 = (f32[18,64,128]{2,1,0:T(8,128)S(1)}, f32[18,64,128]{2,1,0:T(8,128)S(1)}, u32[]{:S(2)}, u32[]{:S(2)}) collective-permute-start(f32[18,64,128]{2,1,0:T(8,128)S(1)} %get-tuple-element.31), channel_id=1, source_target_pairs={{0,30},{1,3},{2,0},{3,5},{4,2},{5,7},{6,4},{7,9},{8,6},{9,11},{10,... | collective-permute-start | bytes 1769480 | tf_op jit(solution)/shard_map/ppermute | solution.py:446
  10.7 12.4 %collective-permute-start = (f32[3,1,32,128]{3,2,1,0:T(8,128)S(1)}, f32[3,1,32,128]{3,2,1,0:T(8,128)S(1)}, u32[]{:S(2)}, u32[]{:S(2)}) collective-permute-start(f32[3,1,32,128]{3,2,1,0:T(8,128)S(1)} %get-tuple-element.59), channel_id=1, source_target_pairs={{0,1},{1,2},{2,3},{3,4},{4,5},{5,6},{6,7},{7,8},{8,9},{9,10},{10,1... | collective-permute-start | bytes 147464 | tf_op jit(solution)/shard_map/ppermute | solution.py:446
  17.2 7.2 %collective-permute-start.1 = (f32[3,1,32,128]{3,2,1,0:T(8,128)S(1)}, f32[3,1,32,128]{3,2,1,0:T(8,128)S(1)}, u32[]{:S(2)}, u32[]{:S(2)}) collective-permute-start(f32[3,1,32,128]{3,2,1,0:T(8,128)S(1)} %get-tuple-element.58), channel_id=1, source_target_pairs={{1,0},{2,1},{3,2},{4,3},{5,4},{6,5},{7,6},{8,7},{9,8},{10,9},{11,1... | collective-permute-start | bytes 147464 | tf_op jit(solution)/shard_map/ppermute | solution.py:446
  23.2 33.2 %copy-start.1 = (f32[3,1,32,128]{3,2,1,0:T(8,128)}, f32[3,1,32,128]{3,2,1,0:T(8,128)S(1)}, u32[]{:S(2)}) copy-start(f32[3,1,32,128]{3,2,1,0:T(8,128)S(1)} %collective-permute-done.before) | copy-start | bytes 147460
  24.4 32.0 %copy-start.2 = (f32[3,1,32,128]{3,2,1,0:T(8,128)}, f32[3,1,32,128]{3,2,1,0:T(8,128)S(1)}, u32[]{:S(2)}) copy-start(f32[3,1,32,128]{3,2,1,0:T(8,128)S(1)} %collective-permute-done.1.after) | copy-start | bytes 147460
  26.9 23.2 %collective-permute-start.5 = (f32[18,64,128]{2,1,0:T(8,128)S(1)}, f32[18,64,128]{2,1,0:T(8,128)S(1)}, u32[]{:S(2)}, u32[]{:S(2)}) collective-permute-start(f32[18,64,128]{2,1,0:T(8,128)S(1)} %collective-permute-done.2.near), channel_id=1, source_target_pairs={{0,1},{1,0},{2,3},{3,2},{4,5},{5,4},{6,7},{7,6},{8,9},{9,8},{10,11... | collective-permute-start | bytes 1769480 | tf_op jit(solution)/shard_map/ppermute | solution.py:446
  27.4 22.7 %collective-permute-start.6 = (f32[18,64,128]{2,1,0:T(8,128)S(1)}, f32[18,64,128]{2,1,0:T(8,128)S(1)}, u32[]{:S(2)}, u32[]{:S(2)}) collective-permute-start(f32[18,64,128]{2,1,0:T(8,128)S(1)} %collective-permute-done.3.far), channel_id=1, source_target_pairs={{0,1},{1,0},{2,3},{3,2},{4,5},{5,4},{6,7},{7,6},{8,9},{9,8},{10,11... | collective-permute-start | bytes 1769480 | tf_op jit(solution)/shard_map/ppermute | solution.py:446
  28.9 21.1 %all-to-all-start = ((f32[128,1,128]{2,1,0:T(1,128)}), f32[128,1,128]{2,1,0:T(1,128)S(1)}, u32[]{:S(2)}, u32[]{:S(2)}) async-start(f32[128,1,128]{2,1,0:T(1,128)} %bitcast.8), calls=%async_computation | async-start | bytes 131072 | tf_op jit(solution)/shard_map/all_to_all | solution.py:485
  60.1 13.3 %collective-permute-start.15 = (f32[12,64,128]{2,1,0:T(8,128)S(1)}, f32[12,64,128]{2,1,0:T(8,128)S(1)}, u32[]{:S(2)}, u32[]{:S(2)}) collective-permute-start(f32[12,64,128]{2,1,0:T(8,128)S(1)} %get-tuple-element.49.refs_1_), channel_id=1, source_target_pairs={{0,2},{1,3},{2,4},{3,5},{4,6},{5,7},{6,8},{7,9},{8,10},{9,11},{10,... | collective-permute-start | bytes 1179656 | tf_op jit(solution)/shard_map/ppermute | solution.py:446
  60.5 12.9 %collective-permute-start.16 = (f32[12,64,128]{2,1,0:T(8,128)S(1)}, f32[12,64,128]{2,1,0:T(8,128)S(1)}, u32[]{:S(2)}, u32[]{:S(2)}) collective-permute-start(f32[12,64,128]{2,1,0:T(8,128)S(1)} %get-tuple-element.48.refs_0_), channel_id=1, source_target_pairs={{0,30},{1,31},{2,0},{3,1},{4,2},{5,3},{6,4},{7,5},{8,6},{9,7},{10,... | collective-permute-start | bytes 1179656 | tf_op jit(solution)/shard_map/ppermute | solution.py:446
  65.0 16.8 %collective-permute-start.7 = (f32[12,64,128]{2,1,0:T(8,128)S(1)}, f32[12,64,128]{2,1,0:T(8,128)S(1)}, u32[]{:S(2)}, u32[]{:S(2)}) collective-permute-start(f32[12,64,128]{2,1,0:T(8,128)S(1)} %get-tuple-element.41.refs_1_), channel_id=1, source_target_pairs={{0,2},{1,3},{2,4},{3,5},{4,6},{5,7},{6,8},{7,9},{8,10},{9,11},{10,... | collective-permute-start | bytes 1179656 | tf_op jit(solution)/shard_map/ppermute | solution.py:446
  65.0 16.8 %collective-permute-start.8 = (f32[12,64,128]{2,1,0:T(8,128)S(1)}, f32[12,64,128]{2,1,0:T(8,128)S(1)}, u32[]{:S(2)}, u32[]{:S(2)}) collective-permute-start(f32[12,64,128]{2,1,0:T(8,128)S(1)} %get-tuple-element.40.refs_0_), channel_id=1, source_target_pairs={{0,30},{1,31},{2,0},{3,1},{4,2},{5,3},{6,4},{7,5},{8,6},{9,7},{10,... | collective-permute-start | bytes 1179656 | tf_op jit(solution)/shard_map/ppermute | solution.py:446
  76.6 13.0 %collective-permute-start.17 = (f32[12,64,128]{2,1,0:T(8,128)S(1)}, f32[12,64,128]{2,1,0:T(8,128)S(1)}, u32[]{:S(2)}, u32[]{:S(2)}) collective-permute-start(f32[12,64,128]{2,1,0:T(8,128)S(1)} %get-tuple-element.51.refs_1_), channel_id=1, source_target_pairs={{0,2},{1,3},{2,4},{3,5},{4,6},{5,7},{6,8},{7,9},{8,10},{9,11},{10,... | collective-permute-start | bytes 1179656 | tf_op jit(solution)/shard_map/ppermute | solution.py:446
  76.7 12.9 %collective-permute-start.18 = (f32[12,64,128]{2,1,0:T(8,128)S(1)}, f32[12,64,128]{2,1,0:T(8,128)S(1)}, u32[]{:S(2)}, u32[]{:S(2)}) collective-permute-start(f32[12,64,128]{2,1,0:T(8,128)S(1)} %get-tuple-element.50.refs_0_), channel_id=1, source_target_pairs={{0,30},{1,31},{2,0},{3,1},{4,2},{5,3},{6,4},{7,5},{8,6},{9,7},{10,... | collective-permute-start | bytes 1179656 | tf_op jit(solution)/shard_map/ppermute | solution.py:446
  85.1 12.7 %collective-permute-start.10 = (f32[12,64,128]{2,1,0:T(8,128)S(1)}, f32[12,64,128]{2,1,0:T(8,128)S(1)}, u32[]{:S(2)}, u32[]{:S(2)}) collective-permute-start(f32[12,64,128]{2,1,0:T(8,128)S(1)} %get-tuple-element.42.refs_0_), channel_id=1, source_target_pairs={{0,30},{1,31},{2,0},{3,1},{4,2},{5,3},{6,4},{7,5},{8,6},{9,7},{10,... | collective-permute-start | bytes 1179656 | tf_op jit(solution)/shard_map/ppermute | solution.py:446
  89.6 11.4 %collective-permute-start.9 = (f32[12,64,128]{2,1,0:T(8,128)S(1)}, f32[12,64,128]{2,1,0:T(8,128)S(1)}, u32[]{:S(2)}, u32[]{:S(2)}) collective-permute-start(f32[12,64,128]{2,1,0:T(8,128)S(1)} %get-tuple-element.43.refs_1_), channel_id=1, source_target_pairs={{0,2},{1,3},{2,4},{3,5},{4,6},{5,7},{6,8},{7,9},{8,10},{9,11},{10,... | collective-permute-start | bytes 1179656 | tf_op jit(solution)/shard_map/ppermute | solution.py:446
  92.8 16.5 %collective-permute-start.19 = (f32[12,64,128]{2,1,0:T(8,128)S(1)}, f32[12,64,128]{2,1,0:T(8,128)S(1)}, u32[]{:S(2)}, u32[]{:S(2)}) collective-permute-start(f32[12,64,128]{2,1,0:T(8,128)S(1)} %get-tuple-element.53.refs_1_), channel_id=1, source_target_pairs={{0,2},{1,3},{2,4},{3,5},{4,6},{5,7},{6,8},{7,9},{8,10},{9,11},{10,... | collective-permute-start | bytes 1179656 | tf_op jit(solution)/shard_map/ppermute | solution.py:446
  92.9 16.4 %collective-permute-start.20 = (f32[12,64,128]{2,1,0:T(8,128)S(1)}, f32[12,64,128]{2,1,0:T(8,128)S(1)}, u32[]{:S(2)}, u32[]{:S(2)}) collective-permute-start(f32[12,64,128]{2,1,0:T(8,128)S(1)} %get-tuple-element.52.refs_0_), channel_id=1, source_target_pairs={{0,30},{1,31},{2,0},{3,1},{4,2},{5,3},{6,4},{7,5},{8,6},{9,7},{10,... | collective-permute-start | bytes 1179656 | tf_op jit(solution)/shard_map/ppermute | solution.py:446
  104.2 13.3 %collective-permute-start.11 = (f32[12,64,128]{2,1,0:T(8,128)S(1)}, f32[12,64,128]{2,1,0:T(8,128)S(1)}, u32[]{:S(2)}, u32[]{:S(2)}) collective-permute-start(f32[12,64,128]{2,1,0:T(8,128)S(1)} %get-tuple-element.45.refs_1_), channel_id=1, source_target_pairs={{0,2},{1,3},{2,4},{3,5},{4,6},{5,7},{6,8},{7,9},{8,10},{9,11},{10,... | collective-permute-start | bytes 1179656 | tf_op jit(solution)/shard_map/ppermute | solution.py:446
  104.2 13.2 %collective-permute-start.12 = (f32[12,64,128]{2,1,0:T(8,128)S(1)}, f32[12,64,128]{2,1,0:T(8,128)S(1)}, u32[]{:S(2)}, u32[]{:S(2)}) collective-permute-start(f32[12,64,128]{2,1,0:T(8,128)S(1)} %get-tuple-element.44.refs_0_), channel_id=1, source_target_pairs={{0,30},{1,31},{2,0},{3,1},{4,2},{5,3},{6,4},{7,5},{8,6},{9,7},{10,... | collective-permute-start | bytes 1179656 | tf_op jit(solution)/shard_map/ppermute | solution.py:446
  112.6 12.9 %collective-permute-start.21 = (f32[12,64,128]{2,1,0:T(8,128)S(1)}, f32[12,64,128]{2,1,0:T(8,128)S(1)}, u32[]{:S(2)}, u32[]{:S(2)}) collective-permute-start(f32[12,64,128]{2,1,0:T(8,128)S(1)} %get-tuple-element.55.x_1), channel_id=1, source_target_pairs={{0,2},{1,3},{2,4},{3,5},{4,6},{5,7},{6,8},{7,9},{8,10},{9,11},{10,... | collective-permute-start | bytes 1179656 | tf_op jit(solution)/shard_map/ppermute | solution.py:446
  112.7 12.9 %collective-permute-start.22 = (f32[12,64,128]{2,1,0:T(8,128)S(1)}, f32[12,64,128]{2,1,0:T(8,128)S(1)}, u32[]{:S(2)}, u32[]{:S(2)}) collective-permute-start(f32[12,64,128]{2,1,0:T(8,128)S(1)} %get-tuple-element.54.x_0), channel_id=1, source_target_pairs={{0,30},{1,31},{2,0},{3,1},{4,2},{5,3},{6,4},{7,5},{8,6},{9,7},{10,... | collective-permute-start | bytes 1179656 | tf_op jit(solution)/shard_map/ppermute | solution.py:446
  120.7 13.4 %collective-permute-start.13 = (f32[12,64,128]{2,1,0:T(8,128)S(1)}, f32[12,64,128]{2,1,0:T(8,128)S(1)}, u32[]{:S(2)}, u32[]{:S(2)}) collective-permute-start(f32[12,64,128]{2,1,0:T(8,128)S(1)} %get-tuple-element.47.x_1), channel_id=1, source_target_pairs={{0,2},{1,3},{2,4},{3,5},{4,6},{5,7},{6,8},{7,9},{8,10},{9,11},{10,... | collective-permute-start | bytes 1179656 | tf_op jit(solution)/shard_map/ppermute | solution.py:446
  120.8 13.3 %collective-permute-start.14 = (f32[12,64,128]{2,1,0:T(8,128)S(1)}, f32[12,64,128]{2,1,0:T(8,128)S(1)}, u32[]{:S(2)}, u32[]{:S(2)}) collective-permute-start(f32[12,64,128]{2,1,0:T(8,128)S(1)} %get-tuple-element.46.x_0), channel_id=1, source_target_pairs={{0,30},{1,31},{2,0},{3,1},{4,2},{5,3},{6,4},{7,5},{8,6},{9,7},{10,... | collective-permute-start | bytes 1179656 | tf_op jit(solution)/shard_map/ppermute | solution.py:446
  129.3 22.5 %copy-start.4 = (f32[2,18]{1,0:T(2,128)S(1)}, f32[2,18]{1,0:T(2,128)}, u32[]{:S(2)}) copy-start(f32[2,18]{1,0:T(2,128)} %param.17) | copy-start | bytes 436
  138.7 22.6 %all-to-all-start.1 = ((f32[128,1,128]{2,1,0:T(1,128)}), f32[128,1,128]{2,1,0:T(1,128)S(1)}, u32[]{:S(2)}, u32[]{:S(2)}) async-start(f32[128,1,128]{2,1,0:T(1,128)} %bitcast.12), calls=%async_computation.1 | async-start | bytes 131072 | tf_op jit(solution)/shard_map/all_to_all | solution.py:529

commit v3 on v2

--- a/solution.py
+++ b/solution.py
@@ -1,3 +1,5 @@
+import functools
+
 import jax
 import jax.numpy as jnp
 from jax import lax
@@ -48,49 +50,37 @@
     lax.fori_loop(0, ROWS // CHUNK, step, 0)
 
 
-def elastic(diag, off, put):
+def pack_kernel(diag, off, schmid, crss, branch, rate, low, high, matrix, slips):
     for i in range(6):
         for j in range(6):
-            v = off[6 * i + j]
-            put(6 * i + j, v + diag[i] if i == j else v)
-
-
-def edge_kernel(diag, off, low, high):
-    def put(k, v):
-        if k < HALF:
-            low[k] = v
-        else:
-            high[k - HALF] = v
-
-    elastic(diag, off, put)
-
-
-def pack_kernel(diag, off, schmid, crss, branch, rate, coef):
-    def put(k, v):
-        coef[k] = v
-
-    elastic(diag, off, put)
+            k = 6 * i + j
+            v = off[k] + diag[i] if i == j else off[k]
+            matrix[k] = v
+            if k < HALF:
+                low[k] = v
+            else:
+                high[k - HALF] = v
     bits = branch[...]
     speed = rate[...]
     for a in range(SLIP):
         limit = crss[a]
         inverse = 1.0 / limit
         for j in range(6):
-            coef[36 + 6 * a + j] = schmid[6 * a + j] * inverse
+            slips[6 * a + j] = schmid[6 * a + j] * inverse
         active = (jnp.right_shift(bits, a) & 1).astype(F32)
-        coef[108 + a] = active * speed * (limit * limit)
+        slips[6 * SLIP + a] = active * speed * (limit * limit)
 
 
 def in_hbm(*arrays):
     return [pltpu.with_memory_space_constraint(v, pltpu.HBM) for v in arrays]
 
 
-def pack(kernel, name, micros, operands, planes, rows):
+def pack(operands, planes, rows):
     block = lambda n: pl.BlockSpec((n, rows, LANES), lambda k: (0, k, 0))
     return pl.pallas_call(
-        kernel,
-        name=name,
-        cost_estimate=cost(micros),
+        pack_kernel,
+        name="pack",
+        cost_estimate=cost(4),
         grid=(ROWS // rows,),
         in_specs=[
             block(v.shape[0]) if v.ndim == 3 else pl.BlockSpec((rows, LANES), lambda k: (k, 0))
@@ -179,68 +169,88 @@
     pl.when(side[0] == 1)(lambda: run(whole(other), whole(own), late, early))
 
 
-def fetch_kernel(side, ebar, own_hbm, other_hbm, near, far, rest_near, rest_far, x_0, x_1, own, other, *refs):
-    temps, sems = refs[:4], refs[4]
+def zero_kernel(side, ebar, own_c, own_s, other_c, other_s, own, other, *refs):
+    states, t_0, t_1, sems = refs[: 2 * PER_CORE], refs[-3], refs[-2], refs[-1]
     copies = [
-        pltpu.make_async_copy(src.at[low:high], dst.at[low:high], sems.at[k])
+        pltpu.make_async_copy(src, dst.at[low:high], sems.at[k])
         for k, (src, dst, low, high) in enumerate(
             (
-                (own_hbm, own, 0, 36),
-                (other_hbm, other, 0, 36),
-                (own_hbm, own, 36, 120),
-                (other_hbm, other, 36, 120),
+                (own_c, own, 0, 36),
+                (other_c, other, 0, 36),
+                (own_s, own, 36, 120),
+                (other_s, other, 36, 120),
             )
         )
     ]
     for copy in copies:
         copy.start()
-
-    def ready(k):
-        copies[k].wait()
-        copies[k + 1].wait()
-
-    first_sweep(side, ebar, (own, other, near, far, rest_near, rest_far), (x_0, x_1), temps, ready)
-
-
-def first_kernel(side, ebar, own, other, near, far, rest_near, rest_far, x_0, x_1, *temps):
-    first_sweep(side, ebar, (own, other, near, far, rest_near, rest_far), (x_0, x_1), temps, lambda k: None)
-
-
-def first_sweep(side, ebar, coefficients, outs, temps, ready):
-    x_0, x_1 = outs
-    e_0, e_1, t_0, t_1 = temps
-
-    def start(c_0, c_1, g_0, g_1):
-        for c, g, t_ref, e_ref in ((c_0, g_0, t_0, e_0), (c_1, g_1, t_1, e_1)):
-
-            def body(at, c=c, g=g, t_ref=t_ref, e_ref=e_ref):
-                strain = [
-                    [jnp.full((CHUNK, LANES), ebar[s, i], F32) for i in range(6)] for s in range(SLOTS)
-                ]
-                sig = times(c, at, strain)
-                outer = times(g, at, strain)
-                store(t_ref, at, sig)
-                base = combine(relaxed(strain, sig), outer, lambda u, v: u + SHARE * v)
-                store(e_ref, at, base)
+    copies[0].wait()
+    copies[1].wait()
+    for k in range(PER_CORE):
+        e_0, e_1 = states[2 * k : 2 * k + 2]
+
+        def start(c_0, c_1, k=k, e_0=e_0, e_1=e_1):
+            for c, t_ref, e_ref in ((c_0, t_0, e_0), (c_1, t_1, e_1)):
+
+                def body(at, c=c, t_ref=t_ref, e_ref=e_ref):
+                    strain = uniform(ebar, k)
+                    sig = times(c, at, strain)
+                    store(t_ref, at, sig)
+                    store(e_ref, at, relaxed(strain, sig))
+
+                chunks(body)
+
+        def end(c_0, c_1, e_0=e_0, e_1=e_1):
+            for c, t_ref, e_ref in ((c_0, t_0, e_0), (c_1, t_1, e_1)):
+
+                def body(at, c=c, t_ref=t_ref, e_ref=e_ref):
+                    store(e_ref, at, slip(c, at, load(t_ref, at), load(e_ref, at)))
+
+                chunks(body)
+
+        ordered(side, own, other, start)
+        beside(t_0, t_1, e_0, e_1)
+        if k == 0:
+            copies[2].wait()
+            copies[3].wait()
+        ordered(side, own, other, end)
+
+
+def ordered(side, own, other, run):
+    pl.when(side[0] == 0)(lambda: run(whole(own), whole(other)))
+    pl.when(side[0] == 1)(lambda: run(whole(other), whole(own)))
+
+
+def uniform(ebar, k):
+    return [[jnp.full((CHUNK, LANES), ebar[k, i], F32) for i in range(6)]]
+
+
+def first_kernel(slot, side, ebar, own, other, near, far, rest_near, rest_far, e_0, e_1, x_0, x_1):
+    def run(c_0, c_1, g_0, g_1):
+        for c, g, e_ref, x_ref in ((c_0, g_0, e_0, x_0), (c_1, g_1, e_1, x_1)):
+
+            def body(at, c=c, g=g, e_ref=e_ref, x_ref=x_ref):
+                outer = times(g, at, uniform(ebar, slot))
+                e = combine(load(e_ref, at), outer, lambda u, v: u + SHARE * v)
+                onward(c, at, e, x_ref)
 
             chunks(body)
 
-    ready(0)
-    split(side, coefficients, start)
-    beside(t_0, t_1, e_0, e_1)
-    ready(2)
-    split(side, coefficients, lambda c_0, c_1, g_0, g_1: advance(((c_0, t_0, e_0, x_0), (c_1, t_1, e_1, x_1))))
+    split(side, (own, other, near, far, rest_near, rest_far), run)
     beside_own(x_0, x_1)
+
+
+def onward(c, at, e, x_ref):
+    sig = times(c, at, e)
+    store(x_ref.at[0:FIELDS], at, sig)
+    store(x_ref.at[FIELDS:], at, slip(c, at, sig, relaxed(e, sig)))
 
 
 def advance(planes):
     for c, t_ref, e_ref, x_ref in planes:
 
         def body(at, c=c, t_ref=t_ref, e_ref=e_ref, x_ref=x_ref):
-            e = slip(c, at, load(t_ref, at), load(e_ref, at))
-            sig = times(c, at, e)
-            store(x_ref.at[0:FIELDS], at, sig)
-            store(x_ref.at[FIELDS:], at, slip(c, at, sig, relaxed(e, sig)))
+            onward(c, at, slip(c, at, load(t_ref, at), load(e_ref, at)), x_ref)
 
         chunks(body)
 
@@ -457,17 +467,15 @@
     before = over(displacement[:, 1:2], upward, both)
     after = over(displacement[:, 0:1], downward, both)
 
-    diag = moduli_diag[0, :, 0]
-    off = moduli_off[0, :, 0]
-    low, high = pack(edge_kernel, "edge", 0.1, (diag, off), (HALF, HALF), 32)
+    low, high, *own = pack(
+        (moduli_diag[0, :, 0], moduli_off[0, :, 0], schmid[0, :, 0], crss[0, :, 0], branch[0, 0], rate[0, 0]),
+        (HALF, HALF, 36, 84),
+        32,
+    )
+    before, after, low, high, own = lax.optimization_barrier((before, after, low, high, own))
     near = over(low, across)
     far = over(high, along)
-    flow, low, high = lax.optimization_barrier((rate[0, 0], low, high))
-    own = pack(
-        pack_kernel, "pack", 0.1, (diag, off, schmid[0, :, 0], crss[0, :, 0], branch[0, 0], flow), (120,), 16
-    )[0]
-    other = over(own, partner)
-    before, after, near, far, own = lax.optimization_barrier((before, after, near, far, own))
+    other = [over(v, partner) for v in own]
     core = member % 2
 
     where = member.reshape(1).astype(jnp.int32)
@@ -479,12 +487,13 @@
         [(8, LANES)],
         [pltpu.VMEM((3, 4, 32, LANES), F32)],
     )(point_node, point_owner, where, displacement, before, after)[0]
+    message = jnp.broadcast_to(message[:groups, None, None, :], (groups, members, 1, LANES))
+    arrived = lax.all_to_all(message.reshape(everyone, 1, LANES), both, 0, 0, tiled=True)
+    near, far, arrived = lax.optimization_barrier((near, far, arrived))
     rest_near = over(near, partner)
     rest_far = over(far, partner)
-    message = jnp.broadcast_to(message[:groups, None, None, :], (groups, members, 1, LANES))
-    arrived = lax.all_to_all(message.reshape(everyone, 1, LANES), both, 0, 0, tiled=True)
     strains = jnp.sum(arrived.reshape(groups, members, LANES), axis=1)
-    ebar = [lax.dynamic_slice_in_dim(strains, core * PER_CORE + k, 1, axis=0) for k in range(PER_CORE)]
+    ebar = lax.dynamic_slice_in_dim(strains, core * PER_CORE, PER_CORE, axis=0)
 
     base = stencil(stiffness, displacement, before, after, external)
 
@@ -494,19 +503,22 @@
     side = core.reshape(1).astype(jnp.int32)
     ghosts = (near, far, rest_near, rest_far)
     ANY = pl.BlockSpec(memory_space=pl.ANY)
-    x_0, x_1, own, other = call(
-        fetch_kernel,
-        "fetch",
+    outs = call(
+        zero_kernel,
+        "zero",
         5,
-        [SM] * 2 + [ANY] * 2 + [VM] * 4,
-        [packed] * 2 + [(120, ROWS, LANES)] * 2,
-        temps + [pltpu.SemaphoreType.DMA((4,))],
-    )(side, ebar[0], *in_hbm(own, other), *ghosts)
-    fixed = (own, other, *ghosts)
-    state = [(x_0, x_1)]
-    for k in range(1, PER_CORE):
+        [SM] * 2 + [ANY] * 4,
+        [(120, ROWS, LANES)] * 2 + [plane] * (2 * PER_CORE),
+        temps[:2] + [pltpu.SemaphoreType.DMA((4,))],
+    )(side, ebar, *in_hbm(*own, *other))
+    fixed = (*outs[:2], *ghosts)
+    state = []
+    for k in range(PER_CORE):
+        kernel = functools.partial(first_kernel, k)
         state.append(
-            call(first_kernel, "first", 5, [SM] * 2 + [VM] * 6, [packed] * 2, temps)(side, ebar[k], *fixed)
+            call(kernel, "first", 5, [SM] * 2 + [VM] * 8, [packed] * 2)(
+                side, ebar, *fixed, *outs[2 + 2 * k : 4 + 2 * k]
+            )
         )
     sums = []
     for pair in range(4):

time: 163 us -> 147 us (0.902)
  waiting for transfers between devices: 32.8 us -> 8.59 us
  blocking collectives: 0 us -> 17.3 us
  starting transfers between devices: 75.9 us -> 66.6 us
    all_to_all x0 -> x1, blocking collectives: none -> 17.3 us  [per_device(): lax.all_to_all(message.reshape(everyone, 1, LANES), both, 0, 0, tiled=True)]
    ppermute x23 -> x24, waiting for transfers between devices: 20.1 us -> 5.4 us  [over(): return lax.ppermute(value, axis, pairs)]
    all_to_all x1 -> x0, starting transfers between devices: 11.6 us -> none  [per_device(): lax.all_to_all(message.reshape(everyone, 1, LANES), both, 0, 0, tiled=True)]
    all_to_all x1 -> x0, waiting for transfers between devices: 9.51 us -> none  [per_device(): lax.all_to_all(message.reshape(everyone, 1, LANES), both, 0, 0, tiled=True)]
    ppermute x23 -> x24, starting transfers between devices: 51.3 us -> 55.6 us  [over(): return lax.ppermute(value, axis, pairs)]
    all_to_all x1, starting transfers between devices: 13.1 us -> 10.9 us  [per_device(): lax.all_to_all(reply.reshape(everyone, 1, LANES), both, 0, 0, tiled=True)]
  transfers between devices with their start and end apart: 25 -> 25, of which waited for: 10 -> 4; matrix products, arithmetic and copies ran while one was open for 1% -> 1% of each run, Pallas kernels for 18% -> 29%
where the time goes in v3:
time: 147 us; the launch traced here: 146 us
  starting transfers between devices  66.6 us (45%)
  Pallas kernels  49.9 us (34%)
  blocking collectives  17.3 us (12%)
  waiting for transfers between devices  8.59 us (6%)
  local copies, waits for them, and re-layouts  1.74 us (1%)
    ppermute x24, starting transfers between devices, over(): return lax.ppermute(value, axis, pairs)  55.6 us
    pallas_call x6, Pallas kernels, per_device(): call(pair_kernel, 'pair', 5, [SM] + [VM] * 10, [packed] * 2, temps)  19.3 us
    all_to_all x1, blocking collectives, per_device(): lax.all_to_all(message.reshape(everyone, 1, LANES), both, 0, 0, tiled=True)  17.3 us
    all_to_all x1, starting transfers between devices, per_device(): lax.all_to_all(reply.reshape(everyone, 1, LANES), both, 0, 0, tiled=True)  10.9 us
    pallas_call x2, Pallas kernels, per_device(): call(last_kernel, 'last', 6, [SM] + [VM] * 10, [(FIELDS, CHUNK, LANES)],...  7.42 us
    pallas_call x1, Pallas kernels, per_device(): call(zero_kernel, 'zero', 5, [SM] * 2 + [ANY] * 4, [(120, ROWS, LANES)] *...  6.6 us
    pallas_call x1, Pallas kernels, stencil(): pl.pallas_call(stencil_kernel, name='stencil', cost_estimate=cost(5), gri...  6.23 us
    ppermute x24, waiting for transfers between devices, over(): return lax.ppermute(value, axis, pairs)  5.4 us
  transfers between devices with their start and end apart: 25, of which 4 were waited for; matrix products, arithmetic and copies ran while one was open for 1% of the time, Pallas kernels for 29%

profile of v3, /device:TPU:1, one launch (start us, length us, event | category | flops | bytes accessed | tf_op | source)
XLA Modules:
  0.0 146.2 jit_solution(12297102514956809569)
XLA Ops:
  0.6 0.0 copy-start.1
  0.7 0.9 fusion.1
  1.5 4.5 %collective-permute-start = (f32[3,1,32,128]{3,2,1,0:T(8,128)S(1)}, f32[3,1,32,128]{3,2,1,0:T(8,128)S(1)}, u32[]{:S(2)}, u32[]{:S(2)}) collective-permute-start(f32[3,1,32,128]{3,2,1,0:T(8,128)S(1)} %get-tuple-element.77), channel_id=1, source_target_pairs={{0,1},{1,2},{2,3},{3,4},{4,5},{5,6},{6,7},{7,8},{8,9},{9,10},{10,1... | collective-permute-start | bytes 147464 | tf_op jit(solution)/shard_map/ppermute | solution.py:456
  6.0 1.9 %collective-permute-start.1 = (f32[3,1,32,128]{3,2,1,0:T(8,128)S(1)}, f32[3,1,32,128]{3,2,1,0:T(8,128)S(1)}, u32[]{:S(2)}, u32[]{:S(2)}) collective-permute-start(f32[3,1,32,128]{3,2,1,0:T(8,128)S(1)} %get-tuple-element.76), channel_id=1, source_target_pairs={{1,0},{2,1},{3,2},{4,3},{5,4},{6,5},{7,6},{8,7},{9,8},{10,9},{11,1... | collective-permute-start | bytes 147464 | tf_op jit(solution)/shard_map/ppermute | solution.py:456
  8.0 3.6 %pack.1 = (f32[18,64,128]{2,1,0:T(8,128)}, f32[18,64,128]{2,1,0:T(8,128)S(1)}, f32[36,64,128]{2,1,0:T(8,128)S(1)}, f32[84,64,128]{2,1,0:T(8,128)}) custom-call(f32[6,64,128]{2,1,0:T(8,128)} %bitcast.22, f32[36,64,128]{2,1,0:T(8,128)} %bitcast.18, f32[72,64,128]{2,1,0:T(8,128)} %bitcast.17, f32[12,64,128]{2,1,0:T(8,128)} %bitcast.19, s32[64,128]{1,0:T(8,128)} %bitcast.23, ...), custom_call_target="tpu_custom_call" | custom-call | bytes 14400000 | tf_op jit(solution)/shard_map/pack/pallas_call | solution.py:80
  11.6 0.0 collective-permute-done.1.after
  11.6 0.1 collective-permute-start.5
  11.7 1.8 %collective-permute-start.2 = (f32[18,64,128]{2,1,0:T(8,128)}, f32[18,64,128]{2,1,0:T(8,128)S(1)}, u32[]{:S(2)}, u32[]{:S(2)}) collective-permute-start(f32[18,64,128]{2,1,0:T(8,128)} %get-tuple-element.43), channel_id=1, source_target_pairs={{0,31},{1,2},{2,1},{3,4},{4,3},{5,6},{6,5},{7,8},{8,7},{9,10},{10,... | collective-permute-start | bytes 1769480 | tf_op jit(solution)/shard_map/ppermute | solution.py:456
  13.5 1.2 collective-permute-start.3
  14.7 6.6 %collective-permute-start.4 = (f32[36,64,128]{2,1,0:T(8,128)S(1)}, f32[36,64,128]{2,1,0:T(8,128)}, u32[]{:S(2)}, u32[]{:S(2)}) collective-permute-start(f32[36,64,128]{2,1,0:T(8,128)S(1)} %get-tuple-element.48.own_c), channel_id=1, source_target_pairs={{0,1},{1,0},{2,3},{3,2},{4,5},{5,4},{6,7},{7,6},{8,9},{9,8},{10,11... | collective-permute-start | bytes 3538952 | tf_op jit(solution)/shard_map/ppermute | solution.py:456
  21.4 0.1 copy.19.owner
  21.5 0.7 strain.1
  22.3 17.3 %all_to_all.10 = f32[128,1,128]{2,1,0:T(1,128)} all-to-all(f32[128,1,128]{2,1,0:T(1,128)S(1)} %bitcast.21), channel_id=1, replica_groups=mesh['grp'=4,'rve'=32] {'grp','rve'}, dimensions={0} | all-to-all | bytes 131072 | tf_op jit(solution)/shard_map/all_to_all | solution.py:491
  39.6 0.6 collective-permute-start.6
  40.2 0.1 collective-permute-start.7
  40.3 0.9 bitcast_reduce_fusion
  41.2 0.0 collective-permute-done.4.other_c
  41.2 6.6 %zero.1 = (f32[120,64,128]{2,1,0:T(8,128)S(1)}, f32[120,64,128]{2,1,0:T(8,128)S(1)}, f32[6,64,128]{2,1,0:T(8,128)S(1)}, f32[6,64,128]{2,1,0:T(8,128)S(1)}, f32[6...) custom-call(s32[1]{0:T(128)} %bitcast.1.side, f32[2,128]{1,0:T(2,128)S(1)} %constant_dynamic-slice_fusion.ebar, ...), custom_call_target="tpu_custom_call" | custom-call | bytes 18000000 | tf_op jit(solution)/shard_map/zero/pallas_call | solution.py:506
  47.8 0.0 collective-permute-done.6.rest_near
  47.8 2.3 %first.3 = (f32[12,64,128]{2,1,0:T(8,128)S(1)}, f32[12,64,128]{2,1,0:T(8,128)S(1)}) custom-call(s32[1]{0:T(128)} %bitcast.1.side, f32[2,128]{1,0:T(2,128)S(1)} %constant_dynamic-slice_fusion.ebar, f32[120,64,128]{2,1,0:T(8,128)S(1)} %get-tuple-element.50.own, f32[120,64,128]{2,1,0:T(8,128)S(1)} %get-tuple-element.51.other, ...), custom_call_target="tpu_custom_call" | custom-call | bytes 18000000 | tf_op jit(solution)/shard_map/first/pallas_call | solution.py:519
  50.2 0.1 collective-permute-start.16
  50.2 4.8 %collective-permute-start.17 = (f32[12,64,128]{2,1,0:T(8,128)S(1)}, f32[12,64,128]{2,1,0:T(8,128)S(1)}, u32[]{:S(2)}, u32[]{:S(2)}) collective-permute-start(f32[12,64,128]{2,1,0:T(8,128)S(1)} %get-tuple-element.66.refs_0_), channel_id=1, source_target_pairs={{0,30},{1,31},{2,0},{3,1},{4,2},{5,3},{6,4},{7,5},{8,6},{9,7},{10,... | collective-permute-start | bytes 1179656 | tf_op jit(solution)/shard_map/ppermute | solution.py:456
  55.0 2.3 %first.2 = (f32[12,64,128]{2,1,0:T(8,128)S(1)}, f32[12,64,128]{2,1,0:T(8,128)S(1)}) custom-call(s32[1]{0:T(128)} %bitcast.1.side, f32[2,128]{1,0:T(2,128)S(1)} %constant_dynamic-slice_fusion.ebar, f32[120,64,128]{2,1,0:T(8,128)S(1)} %get-tuple-element.50.own, f32[120,64,128]{2,1,0:T(8,128)S(1)} %get-tuple-element.51.other, ...), custom_call_target="tpu_custom_call" | custom-call | bytes 18000000 | tf_op jit(solution)/shard_map/first/pallas_call | solution.py:519
  57.3 0.1 collective-permute-start.8
  57.4 4.8 %collective-permute-start.9 = (f32[12,64,128]{2,1,0:T(8,128)S(1)}, f32[12,64,128]{2,1,0:T(8,128)S(1)}, u32[]{:S(2)}, u32[]{:S(2)}) collective-permute-start(f32[12,64,128]{2,1,0:T(8,128)S(1)} %get-tuple-element.56.refs_0_), channel_id=1, source_target_pairs={{0,30},{1,31},{2,0},{3,1},{4,2},{5,3},{6,4},{7,5},{8,6},{9,7},{10,... | collective-permute-start | bytes 1179656 | tf_op jit(solution)/shard_map/ppermute | solution.py:456
  62.2 1.6 %collective-permute-done.16.refs_2_ = f32[12,64,128]{2,1,0:T(8,128)S(1)} collective-permute-done((f32[12,64,128]{2,1,0:T(8,128)S(1)}, f32[12,64,128]{2,1,0:T(8,128)S(1)}, u32[]{:S(2)}, u32[]{:S(2)}) %collective-permute-start.16) | collective-permute-done | bytes 393248 | tf_op jit(solution)/shard_map/ppermute | solution.py:456
  63.8 0.0 collective-permute-done.17.refs_3_
  63.8 3.2 %pair.9 = (f32[12,64,128]{2,1,0:T(8,128)S(1)}, f32[12,64,128]{2,1,0:T(8,128)S(1)}) custom-call(s32[1]{0:T(128)} %bitcast.1.side, f32[120,64,128]{2,1,0:T(8,128)S(1)} %get-tuple-element.50.own, f32[120,64,128]{2,1,0:T(8,128)S(1)} %get-tuple-element.51.other, f32[18,64,128]{2,1,0:T(8,128)S(1)} %collective-permute-done.2.near, ...), custom_call_target="tpu_custom_call" | custom-call | bytes 18000000 | tf_op jit(solution)/shard_map/pair/pallas_call | solution.py:531
  67.1 0.1 collective-permute-start.18
  67.1 4.8 %collective-permute-start.19 = (f32[12,64,128]{2,1,0:T(8,128)S(1)}, f32[12,64,128]{2,1,0:T(8,128)S(1)}, u32[]{:S(2)}, u32[]{:S(2)}) collective-permute-start(f32[12,64,128]{2,1,0:T(8,128)S(1)} %get-tuple-element.68.refs_0_), channel_id=1, source_target_pairs={{0,30},{1,31},{2,0},{3,1},{4,2},{5,3},{6,4},{7,5},{8,6},{9,7},{10,... | collective-permute-start | bytes 1179656 | tf_op jit(solution)/shard_map/ppermute | solution.py:456
  71.9 0.3 collective-permute-done.8.refs_2_
  72.2 0.0 collective-permute-done.9.refs_3_
  72.2 3.2 %pair.6 = (f32[12,64,128]{2,1,0:T(8,128)S(1)}, f32[12,64,128]{2,1,0:T(8,128)S(1)}) custom-call(s32[1]{0:T(128)} %bitcast.1.side, f32[120,64,128]{2,1,0:T(8,128)S(1)} %get-tuple-element.50.own, f32[120,64,128]{2,1,0:T(8,128)S(1)} %get-tuple-element.51.other, f32[18,64,128]{2,1,0:T(8,128)S(1)} %collective-permute-done.2.near, ...), custom_call_target="tpu_custom_call" | custom-call | bytes 18000000 | tf_op jit(solution)/shard_map/pair/pallas_call | solution.py:531
  75.5 0.1 collective-permute-start.10
  75.6 4.8 %collective-permute-start.11 = (f32[12,64,128]{2,1,0:T(8,128)S(1)}, f32[12,64,128]{2,1,0:T(8,128)S(1)}, u32[]{:S(2)}, u32[]{:S(2)}) collective-permute-start(f32[12,64,128]{2,1,0:T(8,128)S(1)} %get-tuple-element.58.refs_0_), channel_id=1, source_target_pairs={{0,30},{1,31},{2,0},{3,1},{4,2},{5,3},{6,4},{7,5},{8,6},{9,7},{10,... | collective-permute-start | bytes 1179656 | tf_op jit(solution)/shard_map/ppermute | solution.py:456
  80.4 0.0 collective-permute-done.19.refs_3_
  80.4 3.2 %pair.10 = (f32[12,64,128]{2,1,0:T(8,128)S(1)}, f32[12,64,128]{2,1,0:T(8,128)S(1)}) custom-call(s32[1]{0:T(128)} %bitcast.1.side, f32[120,64,128]{2,1,0:T(8,128)S(1)} %get-tuple-element.50.own, f32[120,64,128]{2,1,0:T(8,128)S(1)} %get-tuple-element.51.other, f32[18,64,128]{2,1,0:T(8,128)S(1)} %collective-permute-done.2.near, ...), custom_call_target="tpu_custom_call" | custom-call | bytes 18000000 | tf_op jit(solution)/shard_map/pair/pallas_call | solution.py:531
  83.6 0.1 collective-permute-start.20
  83.7 4.8 %collective-permute-start.21 = (f32[12,64,128]{2,1,0:T(8,128)S(1)}, f32[12,64,128]{2,1,0:T(8,128)S(1)}, u32[]{:S(2)}, u32[]{:S(2)}) collective-permute-start(f32[12,64,128]{2,1,0:T(8,128)S(1)} %get-tuple-element.70.refs_0_), channel_id=1, source_target_pairs={{0,30},{1,31},{2,0},{3,1},{4,2},{5,3},{6,4},{7,5},{8,6},{9,7},{10,... | collective-permute-start | bytes 1179656 | tf_op jit(solution)/shard_map/ppermute | solution.py:456
  88.4 0.0 collective-permute-done.10.refs_2_
  88.4 0.0 collective-permute-done.11.refs_3_
  88.5 3.2 %pair.7 = (f32[12,64,128]{2,1,0:T(8,128)S(1)}, f32[12,64,128]{2,1,0:T(8,128)S(1)}) custom-call(s32[1]{0:T(128)} %bitcast.1.side, f32[120,64,128]{2,1,0:T(8,128)S(1)} %get-tuple-element.50.own, f32[120,64,128]{2,1,0:T(8,128)S(1)} %get-tuple-element.51.other, f32[18,64,128]{2,1,0:T(8,128)S(1)} %collective-permute-done.2.near, ...), custom_call_target="tpu_custom_call" | custom-call | bytes 18000000 | tf_op jit(solution)/shard_map/pair/pallas_call | solution.py:531
  91.7 0.1 collective-permute-start.12
  91.8 4.8 %collective-permute-start.13 = (f32[12,64,128]{2,1,0:T(8,128)S(1)}, f32[12,64,128]{2,1,0:T(8,128)S(1)}, u32[]{:S(2)}, u32[]{:S(2)}) collective-permute-start(f32[12,64,128]{2,1,0:T(8,128)S(1)} %get-tuple-element.60.refs_0_), channel_id=1, source_target_pairs={{0,30},{1,31},{2,0},{3,1},{4,2},{5,3},{6,4},{7,5},{8,6},{9,7},{10,... | collective-permute-start | bytes 1179656 | tf_op jit(solution)/shard_map/ppermute | solution.py:456
  96.5 0.0 collective-permute-done.21.refs_3_
  96.5 3.2 %pair.11 = (f32[12,64,128]{2,1,0:T(8,128)S(1)}, f32[12,64,128]{2,1,0:T(8,128)S(1)}) custom-call(s32[1]{0:T(128)} %bitcast.1.side, f32[120,64,128]{2,1,0:T(8,128)S(1)} %get-tuple-element.50.own, f32[120,64,128]{2,1,0:T(8,128)S(1)} %get-tuple-element.51.other, f32[18,64,128]{2,1,0:T(8,128)S(1)} %collective-permute-done.2.near, ...), custom_call_target="tpu_custom_call" | custom-call | bytes 18000000 | tf_op jit(solution)/shard_map/pair/pallas_call | solution.py:531
  99.8 0.1 collective-permute-start.22
  99.8 4.8 %collective-permute-start.23 = (f32[12,64,128]{2,1,0:T(8,128)S(1)}, f32[12,64,128]{2,1,0:T(8,128)S(1)}, u32[]{:S(2)}, u32[]{:S(2)}) collective-permute-start(f32[12,64,128]{2,1,0:T(8,128)S(1)} %get-tuple-element.72.x_0), channel_id=1, source_target_pairs={{0,30},{1,31},{2,0},{3,1},{4,2},{5,3},{6,4},{7,5},{8,6},{9,7},{10,... | collective-permute-start | bytes 1179656 | tf_op jit(solution)/shard_map/ppermute | solution.py:456
  104.6 0.0 collective-permute-done.12.refs_2_
  104.6 3.2 %pair.8 = (f32[12,64,128]{2,1,0:T(8,128)S(1)}, f32[12,64,128]{2,1,0:T(8,128)S(1)}) custom-call(s32[1]{0:T(128)} %bitcast.1.side, f32[120,64,128]{2,1,0:T(8,128)S(1)} %get-tuple-element.50.own, f32[120,64,128]{2,1,0:T(8,128)S(1)} %get-tuple-element.51.other, f32[18,64,128]{2,1,0:T(8,128)S(1)} %collective-permute-done.2.near, ...), custom_call_target="tpu_custom_call" | custom-call | bytes 18000000 | tf_op jit(solution)/shard_map/pair/pallas_call | solution.py:531
  107.8 0.1 collective-permute-start.14
  107.9 4.8 %collective-permute-start.15 = (f32[12,64,128]{2,1,0:T(8,128)S(1)}, f32[12,64,128]{2,1,0:T(8,128)S(1)}, u32[]{:S(2)}, u32[]{:S(2)}) collective-permute-start(f32[12,64,128]{2,1,0:T(8,128)S(1)} %get-tuple-element.62.x_0), channel_id=1, source_target_pairs={{0,30},{1,31},{2,0},{3,1},{4,2},{5,3},{6,4},{7,5},{8,6},{9,7},{10,... | collective-permute-start | bytes 1179656 | tf_op jit(solution)/shard_map/ppermute | solution.py:456
  112.7 3.7 %last.3 = f32[6,16,128]{2,1,0:T(8,128)S(1)} custom-call(s32[1]{0:T(128)} %bitcast.1.side, f32[120,64,128]{2,1,0:T(8,128)S(1)} %get-tuple-element.50.own, f32[120,64,128]{2,1,0:T(8,128)S(1)} %get-tuple-element.51.other, f32[18,64,128]{2,1,0:T(8,128)S(1)} %collective-permute-done.2.near, f32[18,64,128]{2,1,0:T(8,128)S(1)} %collective-permute-done.3.far, ...), custom_call_target="tpu_custom_call" | custom-call | bytes 21600000 | tf_op jit(solution)/shard_map/last/pallas_call | solution.py:534
  116.4 0.0 copy-start.5
  116.4 3.4 %collective-permute-done.14.f_0 = f32[12,64,128]{2,1,0:T(8,128)S(1)} collective-permute-done((f32[12,64,128]{2,1,0:T(8,128)S(1)}, f32[12,64,128]{2,1,0:T(8,128)S(1)}, u32[]{:S(2)}, u32[]{:S(2)}) %collective-permute-start.14) | collective-permute-done | bytes 393248 | tf_op jit(solution)/shard_map/ppermute | solution.py:456
  119.8 3.7 %last.2 = f32[6,16,128]{2,1,0:T(8,128)S(1)} custom-call(s32[1]{0:T(128)} %bitcast.1.side, f32[120,64,128]{2,1,0:T(8,128)S(1)} %get-tuple-element.50.own, f32[120,64,128]{2,1,0:T(8,128)S(1)} %get-tuple-element.51.other, f32[18,64,128]{2,1,0:T(8,128)S(1)} %collective-permute-done.2.near, f32[18,64,128]{2,1,0:T(8,128)S(1)} %collective-permute-done.3.far, ...), custom_call_target="tpu_custom_call" | custom-call | bytes 21600000 | tf_op jit(solution)/shard_map/last/pallas_call | solution.py:534
  123.5 0.1 reduce_sum.28
  123.7 0.1 reduce_sum.29
  123.8 0.6 broadcast_in_dim.22
  124.5 10.9 %all-to-all-start.1 = ((f32[128,1,128]{2,1,0:T(1,128)}), f32[128,1,128]{2,1,0:T(1,128)S(1)}, u32[]{:S(2)}, u32[]{:S(2)}) async-start(f32[128,1,128]{2,1,0:T(1,128)} %bitcast.12), calls=%async_computation.1 | async-start | bytes 131072 | tf_op jit(solution)/shard_map/all_to_all | solution.py:541
  135.4 0.1 reshape.43
  135.5 6.2 %stencil.1.base = f32[3,2,32,128]{3,2,1,0:T(8,128)S(1)} custom-call(bf16[27,3,3,2,32,128]{5,4,3,2,1,0:T(8,128)(2,1)} %blocks.1, f32[3,2,32,128]{3,2,1,0:T(8,128)} %disp.3, f32[3,1,32,128]{3,2,1,0:T(8,128)} %copy-done.2, f32[3,1,32,128]{3,2,1,0:T(8,128)} %copy-done.3, f32[3,2,32,128]{3,2,1,0:T(8,128)} %external.1), custom_call_target="tpu_custom_call" | custom-call | bytes 18000000 | tf_op jit(solution)/shard_map/stencil/pallas_call | solution.py:391
  141.7 3.2 %all-to-all-done.1 = f32[128,1,128]{2,1,0:T(1,128)S(1)} async-done(((f32[128,1,128]{2,1,0:T(1,128)}), f32[128,1,128]{2,1,0:T(1,128)S(1)}, u32[]{:S(2)}, u32[]{:S(2)}) %all-to-all-start.1) | async-done | bytes 65568 | tf_op jit(solution)/shard_map/all_to_all | solution.py:541
  144.9 1.3 final.1
  (29 shorter events, 0.1 us)
Async XLA Ops:
  0.6 20.9 %copy-start.1 = (f32[3,2,32,128]{3,2,1,0:T(8,128)S(1)}, f32[3,2,32,128]{3,2,1,0:T(8,128)}, u32[]{:S(2)}) copy-start(f32[3,2,32,128]{3,2,1,0:T(8,128)} %disp.3) | copy-start | bytes 294916
  0.6 20.7 %copy-start.6 = (s32[2,1]{0,1:T(1,128)S(1)}, s32[2,1]{0,1:T(1,128)}, u32[]{:S(2)}) copy-start(s32[2,1]{0,1:T(1,128)} %param.16) | copy-start | bytes 28
  0.7 20.8 %copy-start.4 = (s32[2]{0:T(128)S(1)}, s32[2]{0:T(128)}, u32[]{:S(2)}) copy-start(s32[2]{0:T(128)} %node.3) | copy-start | bytes 28
  1.5 10.1 %collective-permute-start = (f32[3,1,32,128]{3,2,1,0:T(8,128)S(1)}, f32[3,1,32,128]{3,2,1,0:T(8,128)S(1)}, u32[]{:S(2)}, u32[]{:S(2)}) collective-permute-start(f32[3,1,32,128]{3,2,1,0:T(8,128)S(1)} %get-tuple-element.77), channel_id=1, source_target_pairs={{0,1},{1,2},{2,3},{3,4},{4,5},{5,6},{6,7},{7,8},{8,9},{9,10},{10,1... | collective-permute-start | bytes 147464 | tf_op jit(solution)/shard_map/ppermute | solution.py:456
  6.0 5.6 %collective-permute-start.1 = (f32[3,1,32,128]{3,2,1,0:T(8,128)S(1)}, f32[3,1,32,128]{3,2,1,0:T(8,128)S(1)}, u32[]{:S(2)}, u32[]{:S(2)}) collective-permute-start(f32[3,1,32,128]{3,2,1,0:T(8,128)S(1)} %get-tuple-element.76), channel_id=1, source_target_pairs={{1,0},{2,1},{3,2},{4,3},{5,4},{6,5},{7,6},{8,7},{9,8},{10,9},{11,1... | collective-permute-start | bytes 147464 | tf_op jit(solution)/shard_map/ppermute | solution.py:456
  11.6 29.6 %copy-start = (f32[36,64,128]{2,1,0:T(8,128)}, f32[36,64,128]{2,1,0:T(8,128)S(1)}, u32[]{:S(2)}) copy-start(f32[36,64,128]{2,1,0:T(8,128)S(1)} %get-tuple-element.48.own_c) | copy-start | bytes 3538948
  11.6 28.0 %copy-start.2 = (f32[3,1,32,128]{3,2,1,0:T(8,128)}, f32[3,1,32,128]{3,2,1,0:T(8,128)S(1)}, u32[]{:S(2)}) copy-start(f32[3,1,32,128]{3,2,1,0:T(8,128)S(1)} %collective-permute-done.before) | copy-start | bytes 147460
  11.6 28.0 %copy-start.3 = (f32[3,1,32,128]{3,2,1,0:T(8,128)}, f32[3,1,32,128]{3,2,1,0:T(8,128)S(1)}, u32[]{:S(2)}) copy-start(f32[3,1,32,128]{3,2,1,0:T(8,128)S(1)} %collective-permute-done.1.after) | copy-start | bytes 147460
  11.6 29.6 %collective-permute-start.5 = (f32[84,64,128]{2,1,0:T(8,128)}, f32[84,64,128]{2,1,0:T(8,128)}, u32[]{:S(2)}, u32[]{:S(2)}) collective-permute-start(f32[84,64,128]{2,1,0:T(8,128)} %get-tuple-element.49.own_s), channel_id=1, source_target_pairs={{0,1},{1,0},{2,3},{3,2},{4,5},{5,4},{6,7},{7,6},{8,9},{9,8},{10,11... | collective-permute-start | bytes 8257544 | tf_op jit(solution)/shard_map/ppermute | solution.py:456
  11.7 27.9 %collective-permute-start.2 = (f32[18,64,128]{2,1,0:T(8,128)}, f32[18,64,128]{2,1,0:T(8,128)S(1)}, u32[]{:S(2)}, u32[]{:S(2)}) collective-permute-start(f32[18,64,128]{2,1,0:T(8,128)} %get-tuple-element.43), channel_id=1, source_target_pairs={{0,31},{1,2},{2,1},{3,4},{4,3},{5,6},{6,5},{7,8},{8,7},{9,10},{10,... | collective-permute-start | bytes 1769480 | tf_op jit(solution)/shard_map/ppermute | solution.py:456
  13.5 26.1 %collective-permute-start.3 = (f32[18,64,128]{2,1,0:T(8,128)S(1)}, f32[18,64,128]{2,1,0:T(8,128)S(1)}, u32[]{:S(2)}, u32[]{:S(2)}) collective-permute-start(f32[18,64,128]{2,1,0:T(8,128)S(1)} %get-tuple-element.44), channel_id=1, source_target_pairs={{0,30},{1,3},{2,0},{3,5},{4,2},{5,7},{6,4},{7,9},{8,6},{9,11},{10,... | collective-permute-start | bytes 1769480 | tf_op jit(solution)/shard_map/ppermute | solution.py:456
  14.7 26.4 %collective-permute-start.4 = (f32[36,64,128]{2,1,0:T(8,128)S(1)}, f32[36,64,128]{2,1,0:T(8,128)}, u32[]{:S(2)}, u32[]{:S(2)}) collective-permute-start(f32[36,64,128]{2,1,0:T(8,128)S(1)} %get-tuple-element.48.own_c), channel_id=1, source_target_pairs={{0,1},{1,0},{2,3},{3,2},{4,5},{5,4},{6,7},{7,6},{8,9},{9,8},{10,11... | collective-permute-start | bytes 3538952 | tf_op jit(solution)/shard_map/ppermute | solution.py:456
  39.6 8.2 %collective-permute-start.6 = (f32[18,64,128]{2,1,0:T(8,128)S(1)}, f32[18,64,128]{2,1,0:T(8,128)S(1)}, u32[]{:S(2)}, u32[]{:S(2)}) collective-permute-start(f32[18,64,128]{2,1,0:T(8,128)S(1)} %collective-permute-done.2.near), channel_id=1, source_target_pairs={{0,1},{1,0},{2,3},{3,2},{4,5},{5,4},{6,7},{7,6},{8,9},{9,8},{10,11... | collective-permute-start | bytes 1769480 | tf_op jit(solution)/shard_map/ppermute | solution.py:456
  40.2 7.6 %collective-permute-start.7 = (f32[18,64,128]{2,1,0:T(8,128)S(1)}, f32[18,64,128]{2,1,0:T(8,128)S(1)}, u32[]{:S(2)}, u32[]{:S(2)}) collective-permute-start(f32[18,64,128]{2,1,0:T(8,128)S(1)} %collective-permute-done.3.far), channel_id=1, source_target_pairs={{0,1},{1,0},{2,3},{3,2},{4,5},{5,4},{6,7},{7,6},{8,9},{9,8},{10,11... | collective-permute-start | bytes 1769480 | tf_op jit(solution)/shard_map/ppermute | solution.py:456
  50.2 13.7 %collective-permute-start.16 = (f32[12,64,128]{2,1,0:T(8,128)S(1)}, f32[12,64,128]{2,1,0:T(8,128)S(1)}, u32[]{:S(2)}, u32[]{:S(2)}) collective-permute-start(f32[12,64,128]{2,1,0:T(8,128)S(1)} %get-tuple-element.67.refs_1_), channel_id=1, source_target_pairs={{0,2},{1,3},{2,4},{3,5},{4,6},{5,7},{6,8},{7,9},{8,10},{9,11},{10,... | collective-permute-start | bytes 1179656 | tf_op jit(solution)/shard_map/ppermute | solution.py:456
  50.2 13.6 %collective-permute-start.17 = (f32[12,64,128]{2,1,0:T(8,128)S(1)}, f32[12,64,128]{2,1,0:T(8,128)S(1)}, u32[]{:S(2)}, u32[]{:S(2)}) collective-permute-start(f32[12,64,128]{2,1,0:T(8,128)S(1)} %get-tuple-element.66.refs_0_), channel_id=1, source_target_pairs={{0,30},{1,31},{2,0},{3,1},{4,2},{5,3},{6,4},{7,5},{8,6},{9,7},{10,... | collective-permute-start | bytes 1179656 | tf_op jit(solution)/shard_map/ppermute | solution.py:456
  57.3 14.9 %collective-permute-start.8 = (f32[12,64,128]{2,1,0:T(8,128)S(1)}, f32[12,64,128]{2,1,0:T(8,128)S(1)}, u32[]{:S(2)}, u32[]{:S(2)}) collective-permute-start(f32[12,64,128]{2,1,0:T(8,128)S(1)} %get-tuple-element.57.refs_1_), channel_id=1, source_target_pairs={{0,2},{1,3},{2,4},{3,5},{4,6},{5,7},{6,8},{7,9},{8,10},{9,11},{10,... | collective-permute-start | bytes 1179656 | tf_op jit(solution)/shard_map/ppermute | solution.py:456
  57.4 14.8 %collective-permute-start.9 = (f32[12,64,128]{2,1,0:T(8,128)S(1)}, f32[12,64,128]{2,1,0:T(8,128)S(1)}, u32[]{:S(2)}, u32[]{:S(2)}) collective-permute-start(f32[12,64,128]{2,1,0:T(8,128)S(1)} %get-tuple-element.56.refs_0_), channel_id=1, source_target_pairs={{0,30},{1,31},{2,0},{3,1},{4,2},{5,3},{6,4},{7,5},{8,6},{9,7},{10,... | collective-permute-start | bytes 1179656 | tf_op jit(solution)/shard_map/ppermute | solution.py:456
  67.1 13.3 %collective-permute-start.18 = (f32[12,64,128]{2,1,0:T(8,128)S(1)}, f32[12,64,128]{2,1,0:T(8,128)S(1)}, u32[]{:S(2)}, u32[]{:S(2)}) collective-permute-start(f32[12,64,128]{2,1,0:T(8,128)S(1)} %get-tuple-element.69.refs_1_), channel_id=1, source_target_pairs={{0,2},{1,3},{2,4},{3,5},{4,6},{5,7},{6,8},{7,9},{8,10},{9,11},{10,... | collective-permute-start | bytes 1179656 | tf_op jit(solution)/shard_map/ppermute | solution.py:456
  67.1 13.2 %collective-permute-start.19 = (f32[12,64,128]{2,1,0:T(8,128)S(1)}, f32[12,64,128]{2,1,0:T(8,128)S(1)}, u32[]{:S(2)}, u32[]{:S(2)}) collective-permute-start(f32[12,64,128]{2,1,0:T(8,128)S(1)} %get-tuple-element.68.refs_0_), channel_id=1, source_target_pairs={{0,30},{1,31},{2,0},{3,1},{4,2},{5,3},{6,4},{7,5},{8,6},{9,7},{10,... | collective-permute-start | bytes 1179656 | tf_op jit(solution)/shard_map/ppermute | solution.py:456
  75.5 13.0 %collective-permute-start.10 = (f32[12,64,128]{2,1,0:T(8,128)S(1)}, f32[12,64,128]{2,1,0:T(8,128)S(1)}, u32[]{:S(2)}, u32[]{:S(2)}) collective-permute-start(f32[12,64,128]{2,1,0:T(8,128)S(1)} %get-tuple-element.59.refs_1_), channel_id=1, source_target_pairs={{0,2},{1,3},{2,4},{3,5},{4,6},{5,7},{6,8},{7,9},{8,10},{9,11},{10,... | collective-permute-start | bytes 1179656 | tf_op jit(solution)/shard_map/ppermute | solution.py:456
  75.6 12.9 %collective-permute-start.11 = (f32[12,64,128]{2,1,0:T(8,128)S(1)}, f32[12,64,128]{2,1,0:T(8,128)S(1)}, u32[]{:S(2)}, u32[]{:S(2)}) collective-permute-start(f32[12,64,128]{2,1,0:T(8,128)S(1)} %get-tuple-element.58.refs_0_), channel_id=1, source_target_pairs={{0,30},{1,31},{2,0},{3,1},{4,2},{5,3},{6,4},{7,5},{8,6},{9,7},{10,... | collective-permute-start | bytes 1179656 | tf_op jit(solution)/shard_map/ppermute | solution.py:456
  83.6 12.9 %collective-permute-start.20 = (f32[12,64,128]{2,1,0:T(8,128)S(1)}, f32[12,64,128]{2,1,0:T(8,128)S(1)}, u32[]{:S(2)}, u32[]{:S(2)}) collective-permute-start(f32[12,64,128]{2,1,0:T(8,128)S(1)} %get-tuple-element.71.refs_1_), channel_id=1, source_target_pairs={{0,2},{1,3},{2,4},{3,5},{4,6},{5,7},{6,8},{7,9},{8,10},{9,11},{10,... | collective-permute-start | bytes 1179656 | tf_op jit(solution)/shard_map/ppermute | solution.py:456
  83.7 12.9 %collective-permute-start.21 = (f32[12,64,128]{2,1,0:T(8,128)S(1)}, f32[12,64,128]{2,1,0:T(8,128)S(1)}, u32[]{:S(2)}, u32[]{:S(2)}) collective-permute-start(f32[12,64,128]{2,1,0:T(8,128)S(1)} %get-tuple-element.70.refs_0_), channel_id=1, source_target_pairs={{0,30},{1,31},{2,0},{3,1},{4,2},{5,3},{6,4},{7,5},{8,6},{9,7},{10,... | collective-permute-start | bytes 1179656 | tf_op jit(solution)/shard_map/ppermute | solution.py:456
  91.7 12.9 %collective-permute-start.12 = (f32[12,64,128]{2,1,0:T(8,128)S(1)}, f32[12,64,128]{2,1,0:T(8,128)S(1)}, u32[]{:S(2)}, u32[]{:S(2)}) collective-permute-start(f32[12,64,128]{2,1,0:T(8,128)S(1)} %get-tuple-element.61.refs_1_), channel_id=1, source_target_pairs={{0,2},{1,3},{2,4},{3,5},{4,6},{5,7},{6,8},{7,9},{8,10},{9,11},{10,... | collective-permute-start | bytes 1179656 | tf_op jit(solution)/shard_map/ppermute | solution.py:456
  91.8 12.9 %collective-permute-start.13 = (f32[12,64,128]{2,1,0:T(8,128)S(1)}, f32[12,64,128]{2,1,0:T(8,128)S(1)}, u32[]{:S(2)}, u32[]{:S(2)}) collective-permute-start(f32[12,64,128]{2,1,0:T(8,128)S(1)} %get-tuple-element.60.refs_0_), channel_id=1, source_target_pairs={{0,30},{1,31},{2,0},{3,1},{4,2},{5,3},{6,4},{7,5},{8,6},{9,7},{10,... | collective-permute-start | bytes 1179656 | tf_op jit(solution)/shard_map/ppermute | solution.py:456
  99.8 12.9 %collective-permute-start.22 = (f32[12,64,128]{2,1,0:T(8,128)S(1)}, f32[12,64,128]{2,1,0:T(8,128)S(1)}, u32[]{:S(2)}, u32[]{:S(2)}) collective-permute-start(f32[12,64,128]{2,1,0:T(8,128)S(1)} %get-tuple-element.73.x_1), channel_id=1, source_target_pairs={{0,2},{1,3},{2,4},{3,5},{4,6},{5,7},{6,8},{7,9},{8,10},{9,11},{10,... | collective-permute-start | bytes 1179656 | tf_op jit(solution)/shard_map/ppermute | solution.py:456
  99.8 12.9 %collective-permute-start.23 = (f32[12,64,128]{2,1,0:T(8,128)S(1)}, f32[12,64,128]{2,1,0:T(8,128)S(1)}, u32[]{:S(2)}, u32[]{:S(2)}) collective-permute-start(f32[12,64,128]{2,1,0:T(8,128)S(1)} %get-tuple-element.72.x_0), channel_id=1, source_target_pairs={{0,30},{1,31},{2,0},{3,1},{4,2},{5,3},{6,4},{7,5},{8,6},{9,7},{10,... | collective-permute-start | bytes 1179656 | tf_op jit(solution)/shard_map/ppermute | solution.py:456
  107.8 12.0 %collective-permute-start.14 = (f32[12,64,128]{2,1,0:T(8,128)S(1)}, f32[12,64,128]{2,1,0:T(8,128)S(1)}, u32[]{:S(2)}, u32[]{:S(2)}) collective-permute-start(f32[12,64,128]{2,1,0:T(8,128)S(1)} %get-tuple-element.63.x_1), channel_id=1, source_target_pairs={{0,2},{1,3},{2,4},{3,5},{4,6},{5,7},{6,8},{7,9},{8,10},{9,11},{10,... | collective-permute-start | bytes 1179656 | tf_op jit(solution)/shard_map/ppermute | solution.py:456
  107.9 11.9 %collective-permute-start.15 = (f32[12,64,128]{2,1,0:T(8,128)S(1)}, f32[12,64,128]{2,1,0:T(8,128)S(1)}, u32[]{:S(2)}, u32[]{:S(2)}) collective-permute-start(f32[12,64,128]{2,1,0:T(8,128)S(1)} %get-tuple-element.62.x_0), channel_id=1, source_target_pairs={{0,30},{1,31},{2,0},{3,1},{4,2},{5,3},{6,4},{7,5},{8,6},{9,7},{10,... | collective-permute-start | bytes 1179656 | tf_op jit(solution)/shard_map/ppermute | solution.py:456
  116.4 19.0 %copy-start.5 = (f32[2,18]{1,0:T(2,128)S(1)}, f32[2,18]{1,0:T(2,128)}, u32[]{:S(2)}) copy-start(f32[2,18]{1,0:T(2,128)} %param.17) | copy-start | bytes 436
  124.5 20.5 %all-to-all-start.1 = ((f32[128,1,128]{2,1,0:T(1,128)}), f32[128,1,128]{2,1,0:T(1,128)S(1)}, u32[]{:S(2)}, u32[]{:S(2)}) async-start(f32[128,1,128]{2,1,0:T(1,128)} %bitcast.12), calls=%async_computation.1 | async-start | bytes 131072 | tf_op jit(solution)/shard_map/all_to_all | solution.py:541

commit v4 on v3

--- a/solution.py
+++ b/solution.py
@@ -13,6 +13,7 @@
 ROWS = 64
 LANES = 128
 PER_CORE = 2
+FIRST = 1
 SLOTS = 1
 FIELDS = SLOTS * 6
 VMEM_LIMIT = 16 * 1024 * 1024
@@ -170,7 +171,7 @@
 
 
 def zero_kernel(side, ebar, own_c, own_s, other_c, other_s, own, other, *refs):
-    states, t_0, t_1, sems = refs[: 2 * PER_CORE], refs[-3], refs[-2], refs[-1]
+    t_0, t_1, sems = refs[2:]
     copies = [
         pltpu.make_async_copy(src, dst.at[low:high], sems.at[k])
         for k, (src, dst, low, high) in enumerate(
@@ -186,34 +187,39 @@
         copy.start()
     copies[0].wait()
     copies[1].wait()
-    for k in range(PER_CORE):
-        e_0, e_1 = states[2 * k : 2 * k + 2]
-
-        def start(c_0, c_1, k=k, e_0=e_0, e_1=e_1):
-            for c, t_ref, e_ref in ((c_0, t_0, e_0), (c_1, t_1, e_1)):
-
-                def body(at, c=c, t_ref=t_ref, e_ref=e_ref):
-                    strain = uniform(ebar, k)
-                    sig = times(c, at, strain)
-                    store(t_ref, at, sig)
-                    store(e_ref, at, relaxed(strain, sig))
-
-                chunks(body)
-
-        def end(c_0, c_1, e_0=e_0, e_1=e_1):
-            for c, t_ref, e_ref in ((c_0, t_0, e_0), (c_1, t_1, e_1)):
-
-                def body(at, c=c, t_ref=t_ref, e_ref=e_ref):
-                    store(e_ref, at, slip(c, at, load(t_ref, at), load(e_ref, at)))
-
-                chunks(body)
-
-        ordered(side, own, other, start)
-        beside(t_0, t_1, e_0, e_1)
-        if k == 0:
-            copies[2].wait()
-            copies[3].wait()
-        ordered(side, own, other, end)
+    ready = lambda: (copies[2].wait(), copies[3].wait())
+    zero_sweep(side, ebar, FIRST, own, other, *refs[:2], t_0, t_1, ready)
+
+
+def entire_kernel(slot, side, ebar, own, other, near, far, rest_near, rest_far, x_0, x_1, e_0, e_1, t_0, t_1):
+    zero_sweep(side, ebar, slot, own, other, e_0, e_1, t_0, t_1, lambda: None)
+    first_kernel(slot, side, ebar, own, other, near, far, rest_near, rest_far, e_0, e_1, x_0, x_1)
+
+
+def zero_sweep(side, ebar, slot, own, other, e_0, e_1, t_0, t_1, ready):
+    def start(c_0, c_1):
+        for c, t_ref, e_ref in ((c_0, t_0, e_0), (c_1, t_1, e_1)):
+
+            def body(at, c=c, t_ref=t_ref, e_ref=e_ref):
+                strain = uniform(ebar, slot)
+                sig = times(c, at, strain)
+                store(t_ref, at, sig)
+                store(e_ref, at, relaxed(strain, sig))
+
+            chunks(body)
+
+    def end(c_0, c_1):
+        for c, t_ref, e_ref in ((c_0, t_0, e_0), (c_1, t_1, e_1)):
+
+            def body(at, c=c, t_ref=t_ref, e_ref=e_ref):
+                store(e_ref, at, slip(c, at, load(t_ref, at), load(e_ref, at)))
+
+            chunks(body)
+
+    ordered(side, own, other, start)
+    beside(t_0, t_1, e_0, e_1)
+    ready()
+    ordered(side, own, other, end)
 
 
 def ordered(side, own, other, run):
@@ -508,18 +514,18 @@
         "zero",
         5,
         [SM] * 2 + [ANY] * 4,
-        [(120, ROWS, LANES)] * 2 + [plane] * (2 * PER_CORE),
+        [(120, ROWS, LANES)] * 2 + [plane] * 2,
         temps[:2] + [pltpu.SemaphoreType.DMA((4,))],
     )(side, ebar, *in_hbm(*own, *other))
     fixed = (*outs[:2], *ghosts)
-    state = []
+    state = [None] * PER_CORE
     for k in range(PER_CORE):
-        kernel = functools.partial(first_kernel, k)
-        state.append(
-            call(kernel, "first", 5, [SM] * 2 + [VM] * 8, [packed] * 2)(
-                side, ebar, *fixed, *outs[2 + 2 * k : 4 + 2 * k]
-            )
-        )
+        if k == FIRST:
+            kernel = functools.partial(first_kernel, k)
+            state[k] = call(kernel, "first", 5, [SM] * 2 + [VM] * 8, [packed] * 2)(side, ebar, *fixed, *outs[2:])
+        else:
+            kernel = functools.partial(entire_kernel, k)
+            state[k] = call(kernel, "entire", 5, [SM] * 2 + [VM] * 6, [packed] * 2, temps)(side, ebar, *fixed)
     sums = []
     for pair in range(4):
         for k in range(PER_CORE):

time: 147 us -> 145 us (0.986)
    pallas_call x0 -> x1, Pallas kernels: none -> 3.91 us  [per_device(): call(kernel, 'entire', 5, [SM] * 2 + [VM] * 6, [packed] * 2, temps)]
    pallas_call x2 -> x1, Pallas kernels: 4.63 us -> 2.31 us  [per_device(): call(kernel, 'first', 5, [SM] * 2 + [VM] * 8, [packed] * 2)]
    pallas_call x1, Pallas kernels: 6.6 us -> 5 us  [per_device(): call(zero_kernel, 'zero', 5, [SM] * 2 + [ANY] * 4, [(120, ROWS, LANES)] *...]
  transfers between devices with their start and end apart: 25 -> 25, of which waited for: 4 -> 5; matrix products, arithmetic and copies ran while one was open for 1% -> 1% of each run, Pallas kernels for 29% -> 29%
where the time goes in v4:
time: 145 us
  starting transfers between devices  65.9 us (45%)
  Pallas kernels  49.9 us (34%)
  blocking collectives  17.3 us (12%)
  waiting for transfers between devices  7.96 us (5%)
  local copies, waits for them, and re-layouts  1.74 us (1%)
    ppermute x24, starting transfers between devices, over(): return lax.ppermute(value, axis, pairs)  55.7 us
    pallas_call x6, Pallas kernels, per_device(): call(pair_kernel, 'pair', 5, [SM] + [VM] * 10, [packed] * 2, temps)  19.3 us
    all_to_all x1, blocking collectives, per_device(): lax.all_to_all(message.reshape(everyone, 1, LANES), both, 0, 0, tiled=True)  17.3 us
    all_to_all x1, starting transfers between devices, per_device(): lax.all_to_all(reply.reshape(everyone, 1, LANES), both, 0, 0, tiled=True)  10.2 us
    pallas_call x2, Pallas kernels, per_device(): call(last_kernel, 'last', 6, [SM] + [VM] * 10, [(FIELDS, CHUNK, LANES)],...  7.42 us
    pallas_call x1, Pallas kernels, stencil(): pl.pallas_call(stencil_kernel, name='stencil', cost_estimate=cost(5), gri...  6.23 us
    pallas_call x1, Pallas kernels, per_device(): call(zero_kernel, 'zero', 5, [SM] * 2 + [ANY] * 4, [(120, ROWS, LANES)] *...  5 us
    ppermute x24, waiting for transfers between devices, over(): return lax.ppermute(value, axis, pairs)  4.77 us
  transfers between devices with their start and end apart: 25, of which 5 were waited for; matrix products, arithmetic and copies ran while one was open for 1% of the time, Pallas kernels for 29%

profile of v4, /device:TPU:1, one launch (start us, length us, event | category | flops | bytes accessed | tf_op | source)
XLA Modules:
  0.0 144.9 jit_solution(9953654338297393954)
XLA Ops:
  0.6 0.0 copy-start.1
  0.7 0.9 fusion.1
  1.5 4.5 %collective-permute-start = (f32[3,1,32,128]{3,2,1,0:T(8,128)S(1)}, f32[3,1,32,128]{3,2,1,0:T(8,128)S(1)}, u32[]{:S(2)}, u32[]{:S(2)}) collective-permute-start(f32[3,1,32,128]{3,2,1,0:T(8,128)S(1)} %get-tuple-element.73), channel_id=1, source_target_pairs={{0,1},{1,2},{2,3},{3,4},{4,5},{5,6},{6,7},{7,8},{8,9},{9,10},{10,1... | collective-permute-start | bytes 147464 | tf_op jit(solution)/shard_map/ppermute | solution.py:462
  6.0 1.9 %collective-permute-start.1 = (f32[3,1,32,128]{3,2,1,0:T(8,128)S(1)}, f32[3,1,32,128]{3,2,1,0:T(8,128)S(1)}, u32[]{:S(2)}, u32[]{:S(2)}) collective-permute-start(f32[3,1,32,128]{3,2,1,0:T(8,128)S(1)} %get-tuple-element.72), channel_id=1, source_target_pairs={{1,0},{2,1},{3,2},{4,3},{5,4},{6,5},{7,6},{8,7},{9,8},{10,9},{11,1... | collective-permute-start | bytes 147464 | tf_op jit(solution)/shard_map/ppermute | solution.py:462
  8.0 3.6 %pack.1 = (f32[18,64,128]{2,1,0:T(8,128)}, f32[18,64,128]{2,1,0:T(8,128)S(1)}, f32[36,64,128]{2,1,0:T(8,128)S(1)}, f32[84,64,128]{2,1,0:T(8,128)}) custom-call(f32[6,64,128]{2,1,0:T(8,128)} %bitcast.22, f32[36,64,128]{2,1,0:T(8,128)} %bitcast.18, f32[72,64,128]{2,1,0:T(8,128)} %bitcast.17, f32[12,64,128]{2,1,0:T(8,128)} %bitcast.19, s32[64,128]{1,0:T(8,128)} %bitcast.23, ...), custom_call_target="tpu_custom_call" | custom-call | bytes 14400000 | tf_op jit(solution)/shard_map/pack/pallas_call | solution.py:81
  11.6 0.0 collective-permute-done.before
  11.6 0.1 collective-permute-start.5
  11.7 1.8 %collective-permute-start.2 = (f32[18,64,128]{2,1,0:T(8,128)}, f32[18,64,128]{2,1,0:T(8,128)S(1)}, u32[]{:S(2)}, u32[]{:S(2)}) collective-permute-start(f32[18,64,128]{2,1,0:T(8,128)} %get-tuple-element.41), channel_id=1, source_target_pairs={{0,31},{1,2},{2,1},{3,4},{4,3},{5,6},{6,5},{7,8},{8,7},{9,10},{10,... | collective-permute-start | bytes 1769480 | tf_op jit(solution)/shard_map/ppermute | solution.py:462
  13.5 1.2 collective-permute-start.3
  14.7 6.6 %collective-permute-start.4 = (f32[36,64,128]{2,1,0:T(8,128)S(1)}, f32[36,64,128]{2,1,0:T(8,128)}, u32[]{:S(2)}, u32[]{:S(2)}) collective-permute-start(f32[36,64,128]{2,1,0:T(8,128)S(1)} %get-tuple-element.46.own_c), channel_id=1, source_target_pairs={{0,1},{1,0},{2,3},{3,2},{4,5},{5,4},{6,7},{7,6},{8,9},{9,8},{10,11... | collective-permute-start | bytes 3538952 | tf_op jit(solution)/shard_map/ppermute | solution.py:462
  21.4 0.1 copy.19.owner
  21.5 0.7 strain.1
  22.3 17.3 %all_to_all.10 = f32[128,1,128]{2,1,0:T(1,128)} all-to-all(f32[128,1,128]{2,1,0:T(1,128)S(1)} %bitcast.21), channel_id=1, replica_groups=mesh['grp'=4,'rve'=32] {'grp','rve'}, dimensions={0} | all-to-all | bytes 131072 | tf_op jit(solution)/shard_map/all_to_all | solution.py:497
  39.6 0.0 collective-permute-done.2.near
  39.6 0.0 collective-permute-done.3.far
  39.6 0.6 collective-permute-start.6
  40.2 0.1 collective-permute-start.7
  40.3 0.9 bitcast_reduce_fusion
  41.2 0.0 collective-permute-done.5.other_s
  41.2 5.0 %zero.1 = (f32[120,64,128]{2,1,0:T(8,128)S(1)}, f32[120,64,128]{2,1,0:T(8,128)S(1)}, f32[6,64,128]{2,1,0:T(8,128)S(1)}, f32[6,64,128]{2,1,0:T(8,128)S(1)}) custom-call(s32[1]{0:T(128)} %bitcast.1.side, f32[2,128]{1,0:T(2,128)S(1)} %constant_dynamic-slice_fusion.ebar, f32[36,64,128]{2,1,0:T(8,128)} %copy-done, f32[84,64,128]{2,1,0:T(8,128)} %get-tuple-element.47.own_s, ...), custom_call_target="tpu_custom_call" | custom-call | bytes 18000000 | tf_op jit(solution)/shard_map/zero/pallas_call | solution.py:512
  46.2 0.0 collective-permute-done.6.rest_near
  46.2 2.3 %first.1 = (f32[12,64,128]{2,1,0:T(8,128)S(1)}, f32[12,64,128]{2,1,0:T(8,128)S(1)}) custom-call(s32[1]{0:T(128)} %bitcast.1.side, f32[2,128]{1,0:T(2,128)S(1)} %constant_dynamic-slice_fusion.ebar, f32[120,64,128]{2,1,0:T(8,128)S(1)} %get-tuple-element.48.own, f32[120,64,128]{2,1,0:T(8,128)S(1)} %get-tuple-element.49.other, ...), custom_call_target="tpu_custom_call" | custom-call | bytes 18000000 | tf_op jit(solution)/shard_map/first/pallas_call | solution.py:525
  48.6 0.1 collective-permute-start.16
  48.6 4.8 %collective-permute-start.17 = (f32[12,64,128]{2,1,0:T(8,128)S(1)}, f32[12,64,128]{2,1,0:T(8,128)S(1)}, u32[]{:S(2)}, u32[]{:S(2)}) collective-permute-start(f32[12,64,128]{2,1,0:T(8,128)S(1)} %get-tuple-element.62.refs_0_), channel_id=1, source_target_pairs={{0,30},{1,31},{2,0},{3,1},{4,2},{5,3},{6,4},{7,5},{8,6},{9,7},{10,... | collective-permute-start | bytes 1179656 | tf_op jit(solution)/shard_map/ppermute | solution.py:462
  53.4 3.9 %entire.1 = (f32[12,64,128]{2,1,0:T(8,128)S(1)}, f32[12,64,128]{2,1,0:T(8,128)S(1)}) custom-call(s32[1]{0:T(128)} %bitcast.1.side, f32[2,128]{1,0:T(2,128)S(1)} %constant_dynamic-slice_fusion.ebar, f32[120,64,128]{2,1,0:T(8,128)S(1)} %get-tuple-element.48.own, f32[120,64,128]{2,1,0:T(8,128)S(1)} %get-tuple-element.49.other, ...), custom_call_target="tpu_custom_call" | custom-call | bytes 18000000 | tf_op jit(solution)/shard_map/entire/pallas_call | solution.py:528
  57.3 0.1 collective-permute-start.8
  57.4 4.8 %collective-permute-start.9 = (f32[12,64,128]{2,1,0:T(8,128)S(1)}, f32[12,64,128]{2,1,0:T(8,128)S(1)}, u32[]{:S(2)}, u32[]{:S(2)}) collective-permute-start(f32[12,64,128]{2,1,0:T(8,128)S(1)} %get-tuple-element.52.refs_0_), channel_id=1, source_target_pairs={{0,30},{1,31},{2,0},{3,1},{4,2},{5,3},{6,4},{7,5},{8,6},{9,7},{10,... | collective-permute-start | bytes 1179656 | tf_op jit(solution)/shard_map/ppermute | solution.py:462
  62.2 0.0 collective-permute-done.16.refs_2_
  62.2 0.0 collective-permute-done.17.refs_3_
  62.2 3.2 %pair.9 = (f32[12,64,128]{2,1,0:T(8,128)S(1)}, f32[12,64,128]{2,1,0:T(8,128)S(1)}) custom-call(s32[1]{0:T(128)} %bitcast.1.side, f32[120,64,128]{2,1,0:T(8,128)S(1)} %get-tuple-element.48.own, f32[120,64,128]{2,1,0:T(8,128)S(1)} %get-tuple-element.49.other, f32[18,64,128]{2,1,0:T(8,128)S(1)} %collective-permute-done.2.near, ...), custom_call_target="tpu_custom_call" | custom-call | bytes 18000000 | tf_op jit(solution)/shard_map/pair/pallas_call | solution.py:537
  65.5 0.1 collective-permute-start.18
  65.5 4.8 %collective-permute-start.19 = (f32[12,64,128]{2,1,0:T(8,128)S(1)}, f32[12,64,128]{2,1,0:T(8,128)S(1)}, u32[]{:S(2)}, u32[]{:S(2)}) collective-permute-start(f32[12,64,128]{2,1,0:T(8,128)S(1)} %get-tuple-element.64.refs_0_), channel_id=1, source_target_pairs={{0,30},{1,31},{2,0},{3,1},{4,2},{5,3},{6,4},{7,5},{8,6},{9,7},{10,... | collective-permute-start | bytes 1179656 | tf_op jit(solution)/shard_map/ppermute | solution.py:462
  70.3 0.0 collective-permute-done.8.refs_2_
  70.4 3.2 %pair.6 = (f32[12,64,128]{2,1,0:T(8,128)S(1)}, f32[12,64,128]{2,1,0:T(8,128)S(1)}) custom-call(s32[1]{0:T(128)} %bitcast.1.side, f32[120,64,128]{2,1,0:T(8,128)S(1)} %get-tuple-element.48.own, f32[120,64,128]{2,1,0:T(8,128)S(1)} %get-tuple-element.49.other, f32[18,64,128]{2,1,0:T(8,128)S(1)} %collective-permute-done.2.near, ...), custom_call_target="tpu_custom_call" | custom-call | bytes 18000000 | tf_op jit(solution)/shard_map/pair/pallas_call | solution.py:537
  73.6 0.1 collective-permute-start.10
  73.7 4.8 %collective-permute-start.11 = (f32[12,64,128]{2,1,0:T(8,128)S(1)}, f32[12,64,128]{2,1,0:T(8,128)S(1)}, u32[]{:S(2)}, u32[]{:S(2)}) collective-permute-start(f32[12,64,128]{2,1,0:T(8,128)S(1)} %get-tuple-element.54.refs_0_), channel_id=1, source_target_pairs={{0,30},{1,31},{2,0},{3,1},{4,2},{5,3},{6,4},{7,5},{8,6},{9,7},{10,... | collective-permute-start | bytes 1179656 | tf_op jit(solution)/shard_map/ppermute | solution.py:462
  78.5 0.1 collective-permute-done.18.refs_2_
  78.5 3.2 %pair.10 = (f32[12,64,128]{2,1,0:T(8,128)S(1)}, f32[12,64,128]{2,1,0:T(8,128)S(1)}) custom-call(s32[1]{0:T(128)} %bitcast.1.side, f32[120,64,128]{2,1,0:T(8,128)S(1)} %get-tuple-element.48.own, f32[120,64,128]{2,1,0:T(8,128)S(1)} %get-tuple-element.49.other, f32[18,64,128]{2,1,0:T(8,128)S(1)} %collective-permute-done.2.near, ...), custom_call_target="tpu_custom_call" | custom-call | bytes 18000000 | tf_op jit(solution)/shard_map/pair/pallas_call | solution.py:537
  81.8 0.1 collective-permute-start.20
  81.9 4.8 %collective-permute-start.21 = (f32[12,64,128]{2,1,0:T(8,128)S(1)}, f32[12,64,128]{2,1,0:T(8,128)S(1)}, u32[]{:S(2)}, u32[]{:S(2)}) collective-permute-start(f32[12,64,128]{2,1,0:T(8,128)S(1)} %get-tuple-element.66.refs_0_), channel_id=1, source_target_pairs={{0,30},{1,31},{2,0},{3,1},{4,2},{5,3},{6,4},{7,5},{8,6},{9,7},{10,... | collective-permute-start | bytes 1179656 | tf_op jit(solution)/shard_map/ppermute | solution.py:462
  86.6 3.2 %pair.7 = (f32[12,64,128]{2,1,0:T(8,128)S(1)}, f32[12,64,128]{2,1,0:T(8,128)S(1)}) custom-call(s32[1]{0:T(128)} %bitcast.1.side, f32[120,64,128]{2,1,0:T(8,128)S(1)} %get-tuple-element.48.own, f32[120,64,128]{2,1,0:T(8,128)S(1)} %get-tuple-element.49.other, f32[18,64,128]{2,1,0:T(8,128)S(1)} %collective-permute-done.2.near, ...), custom_call_target="tpu_custom_call" | custom-call | bytes 18000000 | tf_op jit(solution)/shard_map/pair/pallas_call | solution.py:537
  89.9 0.1 collective-permute-start.12
  90.0 4.8 %collective-permute-start.13 = (f32[12,64,128]{2,1,0:T(8,128)S(1)}, f32[12,64,128]{2,1,0:T(8,128)S(1)}, u32[]{:S(2)}, u32[]{:S(2)}) collective-permute-start(f32[12,64,128]{2,1,0:T(8,128)S(1)} %get-tuple-element.56.refs_0_), channel_id=1, source_target_pairs={{0,30},{1,31},{2,0},{3,1},{4,2},{5,3},{6,4},{7,5},{8,6},{9,7},{10,... | collective-permute-start | bytes 1179656 | tf_op jit(solution)/shard_map/ppermute | solution.py:462
  94.7 0.1 collective-permute-done.20.refs_2_
  94.8 3.2 %pair.11 = (f32[12,64,128]{2,1,0:T(8,128)S(1)}, f32[12,64,128]{2,1,0:T(8,128)S(1)}) custom-call(s32[1]{0:T(128)} %bitcast.1.side, f32[120,64,128]{2,1,0:T(8,128)S(1)} %get-tuple-element.48.own, f32[120,64,128]{2,1,0:T(8,128)S(1)} %get-tuple-element.49.other, f32[18,64,128]{2,1,0:T(8,128)S(1)} %collective-permute-done.2.near, ...), custom_call_target="tpu_custom_call" | custom-call | bytes 18000000 | tf_op jit(solution)/shard_map/pair/pallas_call | solution.py:537
  98.0 0.1 collective-permute-start.22
  98.1 4.8 %collective-permute-start.23 = (f32[12,64,128]{2,1,0:T(8,128)S(1)}, f32[12,64,128]{2,1,0:T(8,128)S(1)}, u32[]{:S(2)}, u32[]{:S(2)}) collective-permute-start(f32[12,64,128]{2,1,0:T(8,128)S(1)} %get-tuple-element.68.x_0), channel_id=1, source_target_pairs={{0,30},{1,31},{2,0},{3,1},{4,2},{5,3},{6,4},{7,5},{8,6},{9,7},{10,... | collective-permute-start | bytes 1179656 | tf_op jit(solution)/shard_map/ppermute | solution.py:462
  102.9 0.1 collective-permute-done.12.refs_2_
  103.0 3.2 %pair.8 = (f32[12,64,128]{2,1,0:T(8,128)S(1)}, f32[12,64,128]{2,1,0:T(8,128)S(1)}) custom-call(s32[1]{0:T(128)} %bitcast.1.side, f32[120,64,128]{2,1,0:T(8,128)S(1)} %get-tuple-element.48.own, f32[120,64,128]{2,1,0:T(8,128)S(1)} %get-tuple-element.49.other, f32[18,64,128]{2,1,0:T(8,128)S(1)} %collective-permute-done.2.near, ...), custom_call_target="tpu_custom_call" | custom-call | bytes 18000000 | tf_op jit(solution)/shard_map/pair/pallas_call | solution.py:537
  106.2 0.1 collective-permute-start.14
  106.3 4.8 %collective-permute-start.15 = (f32[12,64,128]{2,1,0:T(8,128)S(1)}, f32[12,64,128]{2,1,0:T(8,128)S(1)}, u32[]{:S(2)}, u32[]{:S(2)}) collective-permute-start(f32[12,64,128]{2,1,0:T(8,128)S(1)} %get-tuple-element.58.x_0), channel_id=1, source_target_pairs={{0,30},{1,31},{2,0},{3,1},{4,2},{5,3},{6,4},{7,5},{8,6},{9,7},{10,... | collective-permute-start | bytes 1179656 | tf_op jit(solution)/shard_map/ppermute | solution.py:462
  111.1 0.0 collective-permute-done.22.f_0
  111.1 3.7 %last.3 = f32[6,16,128]{2,1,0:T(8,128)S(1)} custom-call(s32[1]{0:T(128)} %bitcast.1.side, f32[120,64,128]{2,1,0:T(8,128)S(1)} %get-tuple-element.48.own, f32[120,64,128]{2,1,0:T(8,128)S(1)} %get-tuple-element.49.other, f32[18,64,128]{2,1,0:T(8,128)S(1)} %collective-permute-done.2.near, f32[18,64,128]{2,1,0:T(8,128)S(1)} %collective-permute-done.3.far, ...), custom_call_target="tpu_custom_call" | custom-call | bytes 21600000 | tf_op jit(solution)/shard_map/last/pallas_call | solution.py:540
  114.8 0.0 copy-start.5
  114.8 4.4 %collective-permute-done.14.f_0 = f32[12,64,128]{2,1,0:T(8,128)S(1)} collective-permute-done((f32[12,64,128]{2,1,0:T(8,128)S(1)}, f32[12,64,128]{2,1,0:T(8,128)S(1)}, u32[]{:S(2)}, u32[]{:S(2)}) %collective-permute-start.14) | collective-permute-done | bytes 393248 | tf_op jit(solution)/shard_map/ppermute | solution.py:462
  119.2 3.7 %last.2 = f32[6,16,128]{2,1,0:T(8,128)S(1)} custom-call(s32[1]{0:T(128)} %bitcast.1.side, f32[120,64,128]{2,1,0:T(8,128)S(1)} %get-tuple-element.48.own, f32[120,64,128]{2,1,0:T(8,128)S(1)} %get-tuple-element.49.other, f32[18,64,128]{2,1,0:T(8,128)S(1)} %collective-permute-done.2.near, f32[18,64,128]{2,1,0:T(8,128)S(1)} %collective-permute-done.3.far, ...), custom_call_target="tpu_custom_call" | custom-call | bytes 21600000 | tf_op jit(solution)/shard_map/last/pallas_call | solution.py:540
  122.9 0.1 reduce_sum.28
  123.1 0.1 reduce_sum.29
  123.2 0.6 broadcast_in_dim.22
  123.8 10.2 %all-to-all-start.1 = ((f32[128,1,128]{2,1,0:T(1,128)}), f32[128,1,128]{2,1,0:T(1,128)S(1)}, u32[]{:S(2)}, u32[]{:S(2)}) async-start(f32[128,1,128]{2,1,0:T(1,128)} %bitcast.12), calls=%async_computation.1 | async-start | bytes 131072 | tf_op jit(solution)/shard_map/all_to_all | solution.py:547
  134.1 0.1 reshape.43
  134.2 6.2 %stencil.1.base = f32[3,2,32,128]{3,2,1,0:T(8,128)S(1)} custom-call(bf16[27,3,3,2,32,128]{5,4,3,2,1,0:T(8,128)(2,1)} %blocks.1, f32[3,2,32,128]{3,2,1,0:T(8,128)} %disp.3, f32[3,1,32,128]{3,2,1,0:T(8,128)} %copy-done.2, f32[3,1,32,128]{3,2,1,0:T(8,128)} %copy-done.3, f32[3,2,32,128]{3,2,1,0:T(8,128)} %external.1), custom_call_target="tpu_custom_call" | custom-call | bytes 18000000 | tf_op jit(solution)/shard_map/stencil/pallas_call | solution.py:397
  140.4 3.2 %all-to-all-done.1 = f32[128,1,128]{2,1,0:T(1,128)S(1)} async-done(((f32[128,1,128]{2,1,0:T(1,128)}), f32[128,1,128]{2,1,0:T(1,128)S(1)}, u32[]{:S(2)}, u32[]{:S(2)}) %all-to-all-start.1) | async-done | bytes 65568 | tf_op jit(solution)/shard_map/all_to_all | solution.py:547
  143.6 1.3 final.1
  (29 shorter events, 0.1 us)
Async XLA Ops:
  0.6 20.9 %copy-start.1 = (f32[3,2,32,128]{3,2,1,0:T(8,128)S(1)}, f32[3,2,32,128]{3,2,1,0:T(8,128)}, u32[]{:S(2)}) copy-start(f32[3,2,32,128]{3,2,1,0:T(8,128)} %disp.3) | copy-start | bytes 294916
  0.6 20.7 %copy-start.6 = (s32[2,1]{0,1:T(1,128)S(1)}, s32[2,1]{0,1:T(1,128)}, u32[]{:S(2)}) copy-start(s32[2,1]{0,1:T(1,128)} %param.16) | copy-start | bytes 28
  0.7 20.8 %copy-start.4 = (s32[2]{0:T(128)S(1)}, s32[2]{0:T(128)}, u32[]{:S(2)}) copy-start(s32[2]{0:T(128)} %node.3) | copy-start | bytes 28
  1.5 10.1 %collective-permute-start = (f32[3,1,32,128]{3,2,1,0:T(8,128)S(1)}, f32[3,1,32,128]{3,2,1,0:T(8,128)S(1)}, u32[]{:S(2)}, u32[]{:S(2)}) collective-permute-start(f32[3,1,32,128]{3,2,1,0:T(8,128)S(1)} %get-tuple-element.73), channel_id=1, source_target_pairs={{0,1},{1,2},{2,3},{3,4},{4,5},{5,6},{6,7},{7,8},{8,9},{9,10},{10,1... | collective-permute-start | bytes 147464 | tf_op jit(solution)/shard_map/ppermute | solution.py:462
  6.0 5.6 %collective-permute-start.1 = (f32[3,1,32,128]{3,2,1,0:T(8,128)S(1)}, f32[3,1,32,128]{3,2,1,0:T(8,128)S(1)}, u32[]{:S(2)}, u32[]{:S(2)}) collective-permute-start(f32[3,1,32,128]{3,2,1,0:T(8,128)S(1)} %get-tuple-element.72), channel_id=1, source_target_pairs={{1,0},{2,1},{3,2},{4,3},{5,4},{6,5},{7,6},{8,7},{9,8},{10,9},{11,1... | collective-permute-start | bytes 147464 | tf_op jit(solution)/shard_map/ppermute | solution.py:462
  11.6 29.6 %copy-start = (f32[36,64,128]{2,1,0:T(8,128)}, f32[36,64,128]{2,1,0:T(8,128)S(1)}, u32[]{:S(2)}) copy-start(f32[36,64,128]{2,1,0:T(8,128)S(1)} %get-tuple-element.46.own_c) | copy-start | bytes 3538948
  11.6 28.0 %copy-start.2 = (f32[3,1,32,128]{3,2,1,0:T(8,128)}, f32[3,1,32,128]{3,2,1,0:T(8,128)S(1)}, u32[]{:S(2)}) copy-start(f32[3,1,32,128]{3,2,1,0:T(8,128)S(1)} %collective-permute-done.before) | copy-start | bytes 147460
  11.6 28.0 %copy-start.3 = (f32[3,1,32,128]{3,2,1,0:T(8,128)}, f32[3,1,32,128]{3,2,1,0:T(8,128)S(1)}, u32[]{:S(2)}) copy-start(f32[3,1,32,128]{3,2,1,0:T(8,128)S(1)} %collective-permute-done.1.after) | copy-start | bytes 147460
  11.6 29.6 %collective-permute-start.5 = (f32[84,64,128]{2,1,0:T(8,128)}, f32[84,64,128]{2,1,0:T(8,128)}, u32[]{:S(2)}, u32[]{:S(2)}) collective-permute-start(f32[84,64,128]{2,1,0:T(8,128)} %get-tuple-element.47.own_s), channel_id=1, source_target_pairs={{0,1},{1,0},{2,3},{3,2},{4,5},{5,4},{6,7},{7,6},{8,9},{9,8},{10,11... | collective-permute-start | bytes 8257544 | tf_op jit(solution)/shard_map/ppermute | solution.py:462
  11.7 27.9 %collective-permute-start.2 = (f32[18,64,128]{2,1,0:T(8,128)}, f32[18,64,128]{2,1,0:T(8,128)S(1)}, u32[]{:S(2)}, u32[]{:S(2)}) collective-permute-start(f32[18,64,128]{2,1,0:T(8,128)} %get-tuple-element.41), channel_id=1, source_target_pairs={{0,31},{1,2},{2,1},{3,4},{4,3},{5,6},{6,5},{7,8},{8,7},{9,10},{10,... | collective-permute-start | bytes 1769480 | tf_op jit(solution)/shard_map/ppermute | solution.py:462
  13.5 26.1 %collective-permute-start.3 = (f32[18,64,128]{2,1,0:T(8,128)S(1)}, f32[18,64,128]{2,1,0:T(8,128)S(1)}, u32[]{:S(2)}, u32[]{:S(2)}) collective-permute-start(f32[18,64,128]{2,1,0:T(8,128)S(1)} %get-tuple-element.42), channel_id=1, source_target_pairs={{0,30},{1,3},{2,0},{3,5},{4,2},{5,7},{6,4},{7,9},{8,6},{9,11},{10,... | collective-permute-start | bytes 1769480 | tf_op jit(solution)/shard_map/ppermute | solution.py:462
  14.7 26.4 %collective-permute-start.4 = (f32[36,64,128]{2,1,0:T(8,128)S(1)}, f32[36,64,128]{2,1,0:T(8,128)}, u32[]{:S(2)}, u32[]{:S(2)}) collective-permute-start(f32[36,64,128]{2,1,0:T(8,128)S(1)} %get-tuple-element.46.own_c), channel_id=1, source_target_pairs={{0,1},{1,0},{2,3},{3,2},{4,5},{5,4},{6,7},{7,6},{8,9},{9,8},{10,11... | collective-permute-start | bytes 3538952 | tf_op jit(solution)/shard_map/ppermute | solution.py:462
  39.6 6.6 %collective-permute-start.6 = (f32[18,64,128]{2,1,0:T(8,128)S(1)}, f32[18,64,128]{2,1,0:T(8,128)S(1)}, u32[]{:S(2)}, u32[]{:S(2)}) collective-permute-start(f32[18,64,128]{2,1,0:T(8,128)S(1)} %collective-permute-done.2.near), channel_id=1, source_target_pairs={{0,1},{1,0},{2,3},{3,2},{4,5},{5,4},{6,7},{7,6},{8,9},{9,8},{10,11... | collective-permute-start | bytes 1769480 | tf_op jit(solution)/shard_map/ppermute | solution.py:462
  40.2 6.0 %collective-permute-start.7 = (f32[18,64,128]{2,1,0:T(8,128)S(1)}, f32[18,64,128]{2,1,0:T(8,128)S(1)}, u32[]{:S(2)}, u32[]{:S(2)}) collective-permute-start(f32[18,64,128]{2,1,0:T(8,128)S(1)} %collective-permute-done.3.far), channel_id=1, source_target_pairs={{0,1},{1,0},{2,3},{3,2},{4,5},{5,4},{6,7},{7,6},{8,9},{9,8},{10,11... | collective-permute-start | bytes 1769480 | tf_op jit(solution)/shard_map/ppermute | solution.py:462
  48.6 13.7 %collective-permute-start.16 = (f32[12,64,128]{2,1,0:T(8,128)S(1)}, f32[12,64,128]{2,1,0:T(8,128)S(1)}, u32[]{:S(2)}, u32[]{:S(2)}) collective-permute-start(f32[12,64,128]{2,1,0:T(8,128)S(1)} %get-tuple-element.63.refs_1_), channel_id=1, source_target_pairs={{0,2},{1,3},{2,4},{3,5},{4,6},{5,7},{6,8},{7,9},{8,10},{9,11},{10,... | collective-permute-start | bytes 1179656 | tf_op jit(solution)/shard_map/ppermute | solution.py:462
  48.6 13.6 %collective-permute-start.17 = (f32[12,64,128]{2,1,0:T(8,128)S(1)}, f32[12,64,128]{2,1,0:T(8,128)S(1)}, u32[]{:S(2)}, u32[]{:S(2)}) collective-permute-start(f32[12,64,128]{2,1,0:T(8,128)S(1)} %get-tuple-element.62.refs_0_), channel_id=1, source_target_pairs={{0,30},{1,31},{2,0},{3,1},{4,2},{5,3},{6,4},{7,5},{8,6},{9,7},{10,... | collective-permute-start | bytes 1179656 | tf_op jit(solution)/shard_map/ppermute | solution.py:462
  57.3 13.0 %collective-permute-start.8 = (f32[12,64,128]{2,1,0:T(8,128)S(1)}, f32[12,64,128]{2,1,0:T(8,128)S(1)}, u32[]{:S(2)}, u32[]{:S(2)}) collective-permute-start(f32[12,64,128]{2,1,0:T(8,128)S(1)} %get-tuple-element.53.refs_1_), channel_id=1, source_target_pairs={{0,2},{1,3},{2,4},{3,5},{4,6},{5,7},{6,8},{7,9},{8,10},{9,11},{10,... | collective-permute-start | bytes 1179656 | tf_op jit(solution)/shard_map/ppermute | solution.py:462
  57.4 12.9 %collective-permute-start.9 = (f32[12,64,128]{2,1,0:T(8,128)S(1)}, f32[12,64,128]{2,1,0:T(8,128)S(1)}, u32[]{:S(2)}, u32[]{:S(2)}) collective-permute-start(f32[12,64,128]{2,1,0:T(8,128)S(1)} %get-tuple-element.52.refs_0_), channel_id=1, source_target_pairs={{0,30},{1,31},{2,0},{3,1},{4,2},{5,3},{6,4},{7,5},{8,6},{9,7},{10,... | collective-permute-start | bytes 1179656 | tf_op jit(solution)/shard_map/ppermute | solution.py:462
  65.5 13.1 %collective-permute-start.18 = (f32[12,64,128]{2,1,0:T(8,128)S(1)}, f32[12,64,128]{2,1,0:T(8,128)S(1)}, u32[]{:S(2)}, u32[]{:S(2)}) collective-permute-start(f32[12,64,128]{2,1,0:T(8,128)S(1)} %get-tuple-element.65.refs_1_), channel_id=1, source_target_pairs={{0,2},{1,3},{2,4},{3,5},{4,6},{5,7},{6,8},{7,9},{8,10},{9,11},{10,... | collective-permute-start | bytes 1179656 | tf_op jit(solution)/shard_map/ppermute | solution.py:462
  65.5 13.0 %collective-permute-start.19 = (f32[12,64,128]{2,1,0:T(8,128)S(1)}, f32[12,64,128]{2,1,0:T(8,128)S(1)}, u32[]{:S(2)}, u32[]{:S(2)}) collective-permute-start(f32[12,64,128]{2,1,0:T(8,128)S(1)} %get-tuple-element.64.refs_0_), channel_id=1, source_target_pairs={{0,30},{1,31},{2,0},{3,1},{4,2},{5,3},{6,4},{7,5},{8,6},{9,7},{10,... | collective-permute-start | bytes 1179656 | tf_op jit(solution)/shard_map/ppermute | solution.py:462
  73.6 13.0 %collective-permute-start.10 = (f32[12,64,128]{2,1,0:T(8,128)S(1)}, f32[12,64,128]{2,1,0:T(8,128)S(1)}, u32[]{:S(2)}, u32[]{:S(2)}) collective-permute-start(f32[12,64,128]{2,1,0:T(8,128)S(1)} %get-tuple-element.55.refs_1_), channel_id=1, source_target_pairs={{0,2},{1,3},{2,4},{3,5},{4,6},{5,7},{6,8},{7,9},{8,10},{9,11},{10,... | collective-permute-start | bytes 1179656 | tf_op jit(solution)/shard_map/ppermute | solution.py:462
  73.7 13.0 %collective-permute-start.11 = (f32[12,64,128]{2,1,0:T(8,128)S(1)}, f32[12,64,128]{2,1,0:T(8,128)S(1)}, u32[]{:S(2)}, u32[]{:S(2)}) collective-permute-start(f32[12,64,128]{2,1,0:T(8,128)S(1)} %get-tuple-element.54.refs_0_), channel_id=1, source_target_pairs={{0,30},{1,31},{2,0},{3,1},{4,2},{5,3},{6,4},{7,5},{8,6},{9,7},{10,... | collective-permute-start | bytes 1179656 | tf_op jit(solution)/shard_map/ppermute | solution.py:462
  81.8 13.0 %collective-permute-start.20 = (f32[12,64,128]{2,1,0:T(8,128)S(1)}, f32[12,64,128]{2,1,0:T(8,128)S(1)}, u32[]{:S(2)}, u32[]{:S(2)}) collective-permute-start(f32[12,64,128]{2,1,0:T(8,128)S(1)} %get-tuple-element.67.refs_1_), channel_id=1, source_target_pairs={{0,2},{1,3},{2,4},{3,5},{4,6},{5,7},{6,8},{7,9},{8,10},{9,11},{10,... | collective-permute-start | bytes 1179656 | tf_op jit(solution)/shard_map/ppermute | solution.py:462
  81.9 12.9 %collective-permute-start.21 = (f32[12,64,128]{2,1,0:T(8,128)S(1)}, f32[12,64,128]{2,1,0:T(8,128)S(1)}, u32[]{:S(2)}, u32[]{:S(2)}) collective-permute-start(f32[12,64,128]{2,1,0:T(8,128)S(1)} %get-tuple-element.66.refs_0_), channel_id=1, source_target_pairs={{0,30},{1,31},{2,0},{3,1},{4,2},{5,3},{6,4},{7,5},{8,6},{9,7},{10,... | collective-permute-start | bytes 1179656 | tf_op jit(solution)/shard_map/ppermute | solution.py:462
  89.9 13.1 %collective-permute-start.12 = (f32[12,64,128]{2,1,0:T(8,128)S(1)}, f32[12,64,128]{2,1,0:T(8,128)S(1)}, u32[]{:S(2)}, u32[]{:S(2)}) collective-permute-start(f32[12,64,128]{2,1,0:T(8,128)S(1)} %get-tuple-element.57.refs_1_), channel_id=1, source_target_pairs={{0,2},{1,3},{2,4},{3,5},{4,6},{5,7},{6,8},{7,9},{8,10},{9,11},{10,... | collective-permute-start | bytes 1179656 | tf_op jit(solution)/shard_map/ppermute | solution.py:462
  90.0 13.0 %collective-permute-start.13 = (f32[12,64,128]{2,1,0:T(8,128)S(1)}, f32[12,64,128]{2,1,0:T(8,128)S(1)}, u32[]{:S(2)}, u32[]{:S(2)}) collective-permute-start(f32[12,64,128]{2,1,0:T(8,128)S(1)} %get-tuple-element.56.refs_0_), channel_id=1, source_target_pairs={{0,30},{1,31},{2,0},{3,1},{4,2},{5,3},{6,4},{7,5},{8,6},{9,7},{10,... | collective-permute-start | bytes 1179656 | tf_op jit(solution)/shard_map/ppermute | solution.py:462
  98.0 13.1 %collective-permute-start.22 = (f32[12,64,128]{2,1,0:T(8,128)S(1)}, f32[12,64,128]{2,1,0:T(8,128)S(1)}, u32[]{:S(2)}, u32[]{:S(2)}) collective-permute-start(f32[12,64,128]{2,1,0:T(8,128)S(1)} %get-tuple-element.69.x_1), channel_id=1, source_target_pairs={{0,2},{1,3},{2,4},{3,5},{4,6},{5,7},{6,8},{7,9},{8,10},{9,11},{10,... | collective-permute-start | bytes 1179656 | tf_op jit(solution)/shard_map/ppermute | solution.py:462
  98.1 13.0 %collective-permute-start.23 = (f32[12,64,128]{2,1,0:T(8,128)S(1)}, f32[12,64,128]{2,1,0:T(8,128)S(1)}, u32[]{:S(2)}, u32[]{:S(2)}) collective-permute-start(f32[12,64,128]{2,1,0:T(8,128)S(1)} %get-tuple-element.68.x_0), channel_id=1, source_target_pairs={{0,30},{1,31},{2,0},{3,1},{4,2},{5,3},{6,4},{7,5},{8,6},{9,7},{10,... | collective-permute-start | bytes 1179656 | tf_op jit(solution)/shard_map/ppermute | solution.py:462
  106.2 13.0 %collective-permute-start.14 = (f32[12,64,128]{2,1,0:T(8,128)S(1)}, f32[12,64,128]{2,1,0:T(8,128)S(1)}, u32[]{:S(2)}, u32[]{:S(2)}) collective-permute-start(f32[12,64,128]{2,1,0:T(8,128)S(1)} %get-tuple-element.59.x_1), channel_id=1, source_target_pairs={{0,2},{1,3},{2,4},{3,5},{4,6},{5,7},{6,8},{7,9},{8,10},{9,11},{10,... | collective-permute-start | bytes 1179656 | tf_op jit(solution)/shard_map/ppermute | solution.py:462
  106.3 12.9 %collective-permute-start.15 = (f32[12,64,128]{2,1,0:T(8,128)S(1)}, f32[12,64,128]{2,1,0:T(8,128)S(1)}, u32[]{:S(2)}, u32[]{:S(2)}) collective-permute-start(f32[12,64,128]{2,1,0:T(8,128)S(1)} %get-tuple-element.58.x_0), channel_id=1, source_target_pairs={{0,30},{1,31},{2,0},{3,1},{4,2},{5,3},{6,4},{7,5},{8,6},{9,7},{10,... | collective-permute-start | bytes 1179656 | tf_op jit(solution)/shard_map/ppermute | solution.py:462
  114.8 19.3 %copy-start.5 = (f32[2,18]{1,0:T(2,128)S(1)}, f32[2,18]{1,0:T(2,128)}, u32[]{:S(2)}) copy-start(f32[2,18]{1,0:T(2,128)} %param.17) | copy-start | bytes 436
  123.8 19.8 %all-to-all-start.1 = ((f32[128,1,128]{2,1,0:T(1,128)}), f32[128,1,128]{2,1,0:T(1,128)S(1)}, u32[]{:S(2)}, u32[]{:S(2)}) async-start(f32[128,1,128]{2,1,0:T(1,128)} %bitcast.12), calls=%async_computation.1 | async-start | bytes 131072 | tf_op jit(solution)/shard_map/all_to_all | solution.py:547

commit v5 on v4

--- a/solution.py
+++ b/solution.py
@@ -51,12 +51,12 @@
     lax.fori_loop(0, ROWS // CHUNK, step, 0)
 
 
-def pack_kernel(diag, off, schmid, crss, branch, rate, low, high, matrix, slips):
+def pack_kernel(diag, off, schmid, crss, branch, rate, low, high, coef):
     for i in range(6):
         for j in range(6):
             k = 6 * i + j
             v = off[k] + diag[i] if i == j else off[k]
-            matrix[k] = v
+            coef[k] = v
             if k < HALF:
                 low[k] = v
             else:
@@ -67,9 +67,9 @@
         limit = crss[a]
         inverse = 1.0 / limit
         for j in range(6):
-            slips[6 * a + j] = schmid[6 * a + j] * inverse
+            coef[36 + 6 * a + j] = schmid[6 * a + j] * inverse
         active = (jnp.right_shift(bits, a) & 1).astype(F32)
-        slips[6 * SLIP + a] = active * speed * (limit * limit)
+        coef[108 + a] = active * speed * (limit * limit)
 
 
 def in_hbm(*arrays):
@@ -158,28 +158,24 @@
     return lambda k, at: ref[k, at, :]
 
 
-def joined(low, high):
-    return lambda k, at: low[k, at, :] if k < HALF else high[k - HALF, at, :]
-
-
 def split(side, coefficients, run):
-    own, other, near, far, rest_near, rest_far = coefficients
-    early = joined(near, rest_far)
-    late = joined(rest_near, far)
+    own, other, near, far, rest = coefficients
+    early = lambda k, at: near[k, at, :] if k < HALF else rest[k, at, :]
+    late = lambda k, at: rest[k, at, :] if k < HALF else far[k - HALF, at, :]
     pl.when(side[0] == 0)(lambda: run(whole(own), whole(other), early, late))
     pl.when(side[0] == 1)(lambda: run(whole(other), whole(own), late, early))
 
 
-def zero_kernel(side, ebar, own_c, own_s, other_c, other_s, own, other, *refs):
+def zero_kernel(side, ebar, own_hbm, other_hbm, own, other, *refs):
     t_0, t_1, sems = refs[2:]
     copies = [
-        pltpu.make_async_copy(src, dst.at[low:high], sems.at[k])
+        pltpu.make_async_copy(src.at[low:high], dst.at[low:high], sems.at[k])
         for k, (src, dst, low, high) in enumerate(
             (
-                (own_c, own, 0, 36),
-                (other_c, other, 0, 36),
-                (own_s, own, 36, 120),
-                (other_s, other, 36, 120),
+                (own_hbm, own, 0, 36),
+                (other_hbm, other, 0, 36),
+                (own_hbm, own, 36, 120),
+                (other_hbm, other, 36, 120),
             )
         )
     ]
@@ -191,9 +187,9 @@
     zero_sweep(side, ebar, FIRST, own, other, *refs[:2], t_0, t_1, ready)
 
 
-def entire_kernel(slot, side, ebar, own, other, near, far, rest_near, rest_far, x_0, x_1, e_0, e_1, t_0, t_1):
+def entire_kernel(slot, side, ebar, own, other, near, far, rest, x_0, x_1, e_0, e_1, t_0, t_1):
     zero_sweep(side, ebar, slot, own, other, e_0, e_1, t_0, t_1, lambda: None)
-    first_kernel(slot, side, ebar, own, other, near, far, rest_near, rest_far, e_0, e_1, x_0, x_1)
+    first_kernel(slot, side, ebar, own, other, near, far, rest, e_0, e_1, x_0, x_1)
 
 
 def zero_sweep(side, ebar, slot, own, other, e_0, e_1, t_0, t_1, ready):
@@ -231,7 +227,7 @@
     return [[jnp.full((CHUNK, LANES), ebar[k, i], F32) for i in range(6)]]
 
 
-def first_kernel(slot, side, ebar, own, other, near, far, rest_near, rest_far, e_0, e_1, x_0, x_1):
+def first_kernel(slot, side, ebar, own, other, near, far, rest, e_0, e_1, x_0, x_1):
     def run(c_0, c_1, g_0, g_1):
         for c, g, e_ref, x_ref in ((c_0, g_0, e_0, x_0), (c_1, g_1, e_1, x_1)):
 
@@ -242,7 +238,7 @@
 
             chunks(body)
 
-    split(side, (own, other, near, far, rest_near, rest_far), run)
+    split(side, (own, other, near, far, rest), run)
     beside_own(x_0, x_1)
 
 
@@ -289,11 +285,11 @@
     beside_own(y_0, y_1)
 
 
-def pair_kernel(side, own, other, near, far, rest_near, rest_far, *refs):
-    split(side, (own, other, near, far, rest_near, rest_far), lambda *c: two_sweeps(*c, *refs))
-
-
-def last_kernel(side, own, other, near, far, rest_near, rest_far, x_0, x_1, f_0, f_1, out, y_0, y_1, *temps):
+def pair_kernel(side, own, other, near, far, rest, *refs):
+    split(side, (own, other, near, far, rest), lambda *c: two_sweeps(*c, *refs))
+
+
+def last_kernel(side, own, other, near, far, rest, x_0, x_1, f_0, f_1, out, y_0, y_1, *temps):
     def run(c_0, c_1, g_0, g_1):
         two_sweeps(c_0, c_1, g_0, g_1, x_0, x_1, f_0, f_1, y_0, y_1, *temps)
         for k in range(FIELDS):
@@ -309,7 +305,7 @@
 
             chunks(body)
 
-    split(side, (own, other, near, far, rest_near, rest_far), run)
+    split(side, (own, other, near, far, rest), run)
 
 
 def strain_kernel(node, owner, member, disp, before, after, out, grid):
@@ -473,15 +469,15 @@
     before = over(displacement[:, 1:2], upward, both)
     after = over(displacement[:, 0:1], downward, both)
 
-    low, high, *own = pack(
+    low, high, own = pack(
         (moduli_diag[0, :, 0], moduli_off[0, :, 0], schmid[0, :, 0], crss[0, :, 0], branch[0, 0], rate[0, 0]),
-        (HALF, HALF, 36, 84),
+        (HALF, HALF, 120),
         32,
     )
     before, after, low, high, own = lax.optimization_barrier((before, after, low, high, own))
     near = over(low, across)
     far = over(high, along)
-    other = [over(v, partner) for v in own]
+    other = over(own, partner)
     core = member % 2
 
     where = member.reshape(1).astype(jnp.int32)
@@ -496,8 +492,7 @@
     message = jnp.broadcast_to(message[:groups, None, None, :], (groups, members, 1, LANES))
     arrived = lax.all_to_all(message.reshape(everyone, 1, LANES), both, 0, 0, tiled=True)
     near, far, arrived = lax.optimization_barrier((near, far, arrived))
-    rest_near = over(near, partner)
-    rest_far = over(far, partner)
+    rest = over(jnp.concatenate([near, far], axis=0), partner)
     strains = jnp.sum(arrived.reshape(groups, members, LANES), axis=1)
     ebar = lax.dynamic_slice_in_dim(strains, core * PER_CORE, PER_CORE, axis=0)
 
@@ -507,25 +502,25 @@
     packed = (2 * FIELDS, ROWS, LANES)
     temps = [pltpu.VMEM(plane, F32)] * 4
     side = core.reshape(1).astype(jnp.int32)
-    ghosts = (near, far, rest_near, rest_far)
+    ghosts = (near, far, rest)
     ANY = pl.BlockSpec(memory_space=pl.ANY)
     outs = call(
         zero_kernel,
         "zero",
         5,
-        [SM] * 2 + [ANY] * 4,
+        [SM] * 2 + [ANY] * 2,
         [(120, ROWS, LANES)] * 2 + [plane] * 2,
         temps[:2] + [pltpu.SemaphoreType.DMA((4,))],
-    )(side, ebar, *in_hbm(*own, *other))
+    )(side, ebar, *in_hbm(own, other))
     fixed = (*outs[:2], *ghosts)
     state = [None] * PER_CORE
     for k in range(PER_CORE):
         if k == FIRST:
             kernel = functools.partial(first_kernel, k)
-            state[k] = call(kernel, "first", 5, [SM] * 2 + [VM] * 8, [packed] * 2)(side, ebar, *fixed, *outs[2:])
+            state[k] = call(kernel, "first", 5, [SM] * 2 + [VM] * 7, [packed] * 2)(side, ebar, *fixed, *outs[2:])
         else:
             kernel = functools.partial(entire_kernel, k)
-            state[k] = call(kernel, "entire", 5, [SM] * 2 + [VM] * 6, [packed] * 2, temps)(side, ebar, *fixed)
+            state[k] = call(kernel, "entire", 5, [SM] * 2 + [VM] * 5, [packed] * 2, temps)(side, ebar, *fixed)
     sums = []
     for pair in range(4):
         for k in range(PER_CORE):
@@ -534,10 +529,10 @@
             f_1 = over(x_0, leftward)
             operands = (side, *fixed, x_0, x_1, f_0, f_1)
             if pair < 3:
-                state[k] = call(pair_kernel, "pair", 5, [SM] + [VM] * 10, [packed] * 2, temps)(*operands)
+                state[k] = call(pair_kernel, "pair", 5, [SM] + [VM] * 9, [packed] * 2, temps)(*operands)
             else:
                 sizes = [pltpu.VMEM(packed, F32)] * 2 + temps
-                sums += call(last_kernel, "last", 6, [SM] + [VM] * 10, [(FIELDS, CHUNK, LANES)], sizes)(*operands)
+                sums += call(last_kernel, "last", 6, [SM] + [VM] * 9, [(FIELDS, CHUNK, LANES)], sizes)(*operands)
 
     totals = jnp.stack([jnp.sum(v, axis=(1, 2)) for v in lax.optimization_barrier(sums)])
     totals = jnp.pad(totals, ((0, 0), (0, LANES - 6)))

time: 145 us -> 146 us (level)
  starting transfers between devices: 65.9 us -> 59 us
  blocking collectives: 17.3 us -> 23.6 us
    ppermute x24 -> x22, starting transfers between devices: 55.7 us -> 49 us  [over(): return lax.ppermute(value, axis, pairs)]
    all_to_all x1, blocking collectives: 17.3 us -> 23.6 us  [per_device(): lax.all_to_all(message.reshape(everyone, 1, LANES), both, 0, 0, tiled=True)]
    ppermute x24 -> x22, waiting for transfers between devices: 4.77 us -> 5.28 us  [over(): return lax.ppermute(value, axis, pairs)]
  transfers between devices with their start and end apart: 25 -> 23, of which waited for: 5 -> 7; matrix products, arithmetic and copies ran while one was open for 1% -> 1% of each run, Pallas kernels for 29% -> 29%
where the time goes in v5:
time: 146 us; the launch traced here: 145 us
  starting transfers between devices  59 us (40%)
  Pallas kernels  50.1 us (34%)
  blocking collectives  23.6 us (16%)
  waiting for transfers between devices  8.51 us (6%)
  local copies, waits for them, and re-layouts  1.74 us (1%)
  other arithmetic  1.49 us (1%)
    ppermute x22, starting transfers between devices, over(): return lax.ppermute(value, axis, pairs)  49 us
    all_to_all x1, blocking collectives, per_device(): lax.all_to_all(message.reshape(everyone, 1, LANES), both, 0, 0, tiled=True)  23.6 us
    pallas_call x6, Pallas kernels, per_device(): call(pair_kernel, 'pair', 5, [SM] + [VM] * 9, [packed] * 2, temps)  19.2 us
    all_to_all x1, starting transfers between devices, per_device(): lax.all_to_all(reply.reshape(everyone, 1, LANES), both, 0, 0, tiled=True)  9.99 us
    pallas_call x2, Pallas kernels, per_device(): call(last_kernel, 'last', 6, [SM] + [VM] * 9, [(FIELDS, CHUNK, LANES)], s...  7.43 us
    pallas_call x1, Pallas kernels, stencil(): pl.pallas_call(stencil_kernel, name='stencil', cost_estimate=cost(5), gri...  6.19 us
    ppermute x22, waiting for transfers between devices, over(): return lax.ppermute(value, axis, pairs)  5.28 us
    pallas_call x1, Pallas kernels, per_device(): call(zero_kernel, 'zero', 5, [SM] * 2 + [ANY] * 2, [(120, ROWS, LANES)] *...  5.02 us
  transfers between devices with their start and end apart: 23, of which 7 were waited for; matrix products, arithmetic and copies ran while one was open for 1% of the time, Pallas kernels for 29%

profile of v5, /device:TPU:1, one launch (start us, length us, event | category | flops | bytes accessed | tf_op | source)
XLA Modules:
  0.0 145.3 jit_solution(2007098723346660080)
XLA Ops:
  0.6 0.0 copy-start
  0.7 0.9 fusion.1
  1.5 4.5 %collective-permute-start = (f32[3,1,32,128]{3,2,1,0:T(8,128)S(1)}, f32[3,1,32,128]{3,2,1,0:T(8,128)S(1)}, u32[]{:S(2)}, u32[]{:S(2)}) collective-permute-start(f32[3,1,32,128]{3,2,1,0:T(8,128)S(1)} %get-tuple-element.69), channel_id=1, source_target_pairs={{0,1},{1,2},{2,3},{3,4},{4,5},{5,6},{6,7},{7,8},{8,9},{9,10},{10,1... | collective-permute-start | bytes 147464 | tf_op jit(solution)/shard_map/ppermute | solution.py:458
  6.0 1.9 %collective-permute-start.1 = (f32[3,1,32,128]{3,2,1,0:T(8,128)S(1)}, f32[3,1,32,128]{3,2,1,0:T(8,128)S(1)}, u32[]{:S(2)}, u32[]{:S(2)}) collective-permute-start(f32[3,1,32,128]{3,2,1,0:T(8,128)S(1)} %get-tuple-element.68), channel_id=1, source_target_pairs={{1,0},{2,1},{3,2},{4,3},{5,4},{6,5},{7,6},{8,7},{9,8},{10,9},{11,1... | collective-permute-start | bytes 147464 | tf_op jit(solution)/shard_map/ppermute | solution.py:458
  8.0 3.7 %pack.1 = (f32[18,64,128]{2,1,0:T(8,128)S(1)}, f32[18,64,128]{2,1,0:T(8,128)S(1)}, f32[120,64,128]{2,1,0:T(8,128)}) custom-call(f32[6,64,128]{2,1,0:T(8,128)} %bitcast.22, f32[36,64,128]{2,1,0:T(8,128)} %bitcast.18, f32[72,64,128]{2,1,0:T(8,128)} %bitcast.17, f32[12,64,128]{2,1,0:T(8,128)} %bitcast.19, s32[64,128]{1,0:T(8,128)} %bitcast.23, f32[64,128]{1,0:T(8,128)} %bitcast.24), custom_call_target="tpu_custom_call" | custom-call | bytes 14400000 | tf_op jit(solution)/shard_map/pack/pallas_call | solution.py:81
  11.7 0.0 collective-permute-done.before
  11.7 0.0 collective-permute-done.1.after
  11.7 0.1 collective-permute-start.4
  11.8 1.8 %collective-permute-start.2 = (f32[18,64,128]{2,1,0:T(8,128)S(1)}, f32[18,64,128]{2,1,0:T(8,128)S(1)}, u32[]{:S(2)}, u32[]{:S(2)}) collective-permute-start(f32[18,64,128]{2,1,0:T(8,128)S(1)} %get-tuple-element.38), channel_id=1, source_target_pairs={{0,31},{1,2},{2,1},{3,4},{4,3},{5,6},{6,5},{7,8},{8,7},{9,10},{10,... | collective-permute-start | bytes 1769480 | tf_op jit(solution)/shard_map/ppermute | solution.py:458
  13.6 1.2 collective-permute-start.3
  14.9 0.1 copy.19.owner
  15.0 0.7 strain.1
  15.7 23.6 %all_to_all.10 = f32[128,1,128]{2,1,0:T(1,128)S(1)} all-to-all(f32[128,1,128]{2,1,0:T(1,128)S(1)} %bitcast.21), channel_id=1, replica_groups=mesh['grp'=4,'rve'=32] {'grp','rve'}, dimensions={0} | all-to-all | bytes 131072 | tf_op jit(solution)/shard_map/all_to_all | solution.py:493
  39.3 0.0 collective-permute-done.2.near
  39.3 1.2 pad_maximum_fusion
  40.5 0.7 collective-permute-start.5
  41.2 0.0 collective-permute-done.4.other_hbm
  41.2 5.0 %zero.1 = (f32[120,64,128]{2,1,0:T(8,128)S(1)}, f32[120,64,128]{2,1,0:T(8,128)S(1)}, f32[6,64,128]{2,1,0:T(8,128)S(1)}, f32[6,64,128]{2,1,0:T(8,128)S(1)}) custom-call(s32[1]{0:T(128)} %bitcast.1.side, f32[2,128]{1,0:T(2,128)S(1)} %constant_dynamic-slice_fusion.ebar, f32[120,64,128]{2,1,0:T(8,128)} %get-tuple-element.43.own_hbm, ...), custom_call_target="tpu_custom_call" | custom-call | bytes 18000000 | tf_op jit(solution)/shard_map/zero/pallas_call | solution.py:507
  46.2 0.0 collective-permute-done.5.rest
  46.3 2.4 %first.1 = (f32[12,64,128]{2,1,0:T(8,128)S(1)}, f32[12,64,128]{2,1,0:T(8,128)S(1)}) custom-call(s32[1]{0:T(128)} %bitcast.1.side, f32[2,128]{1,0:T(2,128)S(1)} %constant_dynamic-slice_fusion.ebar, f32[120,64,128]{2,1,0:T(8,128)S(1)} %get-tuple-element.44.own, f32[120,64,128]{2,1,0:T(8,128)S(1)} %get-tuple-element.45.other, ...), custom_call_target="tpu_custom_call" | custom-call | bytes 18000000 | tf_op jit(solution)/shard_map/first/pallas_call | solution.py:520
  48.6 0.1 collective-permute-start.14
  48.7 4.8 %collective-permute-start.15 = (f32[12,64,128]{2,1,0:T(8,128)S(1)}, f32[12,64,128]{2,1,0:T(8,128)S(1)}, u32[]{:S(2)}, u32[]{:S(2)}) collective-permute-start(f32[12,64,128]{2,1,0:T(8,128)S(1)} %get-tuple-element.58.refs_0_), channel_id=1, source_target_pairs={{0,30},{1,31},{2,0},{3,1},{4,2},{5,3},{6,4},{7,5},{8,6},{9,7},{10,... | collective-permute-start | bytes 1179656 | tf_op jit(solution)/shard_map/ppermute | solution.py:458
  53.5 4.0 %entire.1 = (f32[12,64,128]{2,1,0:T(8,128)S(1)}, f32[12,64,128]{2,1,0:T(8,128)S(1)}) custom-call(s32[1]{0:T(128)} %bitcast.1.side, f32[2,128]{1,0:T(2,128)S(1)} %constant_dynamic-slice_fusion.ebar, f32[120,64,128]{2,1,0:T(8,128)S(1)} %get-tuple-element.44.own, f32[120,64,128]{2,1,0:T(8,128)S(1)} %get-tuple-element.45.other, ...), custom_call_target="tpu_custom_call" | custom-call | bytes 18000000 | tf_op jit(solution)/shard_map/entire/pallas_call | solution.py:523
  57.5 0.1 collective-permute-start.6
  57.6 4.8 %collective-permute-start.7 = (f32[12,64,128]{2,1,0:T(8,128)S(1)}, f32[12,64,128]{2,1,0:T(8,128)S(1)}, u32[]{:S(2)}, u32[]{:S(2)}) collective-permute-start(f32[12,64,128]{2,1,0:T(8,128)S(1)} %get-tuple-element.48.refs_0_), channel_id=1, source_target_pairs={{0,30},{1,31},{2,0},{3,1},{4,2},{5,3},{6,4},{7,5},{8,6},{9,7},{10,... | collective-permute-start | bytes 1179656 | tf_op jit(solution)/shard_map/ppermute | solution.py:458
  62.4 0.4 collective-permute-done.14.refs_2_
  62.8 0.0 collective-permute-done.15.refs_3_
  62.8 3.2 %pair.9 = (f32[12,64,128]{2,1,0:T(8,128)S(1)}, f32[12,64,128]{2,1,0:T(8,128)S(1)}) custom-call(s32[1]{0:T(128)} %bitcast.1.side, f32[120,64,128]{2,1,0:T(8,128)S(1)} %get-tuple-element.44.own, f32[120,64,128]{2,1,0:T(8,128)S(1)} %get-tuple-element.45.other, f32[18,64,128]{2,1,0:T(8,128)S(1)} %collective-permute-done.2.near, ...), custom_call_target="tpu_custom_call" | custom-call | bytes 18000000 | tf_op jit(solution)/shard_map/pair/pallas_call | solution.py:532
  66.0 0.1 collective-permute-start.16
  66.1 4.8 %collective-permute-start.17 = (f32[12,64,128]{2,1,0:T(8,128)S(1)}, f32[12,64,128]{2,1,0:T(8,128)S(1)}, u32[]{:S(2)}, u32[]{:S(2)}) collective-permute-start(f32[12,64,128]{2,1,0:T(8,128)S(1)} %get-tuple-element.60.refs_0_), channel_id=1, source_target_pairs={{0,30},{1,31},{2,0},{3,1},{4,2},{5,3},{6,4},{7,5},{8,6},{9,7},{10,... | collective-permute-start | bytes 1179656 | tf_op jit(solution)/shard_map/ppermute | solution.py:458
  70.9 0.2 collective-permute-done.6.refs_2_
  71.0 0.0 collective-permute-done.7.refs_3_
  71.0 3.2 %pair.6 = (f32[12,64,128]{2,1,0:T(8,128)S(1)}, f32[12,64,128]{2,1,0:T(8,128)S(1)}) custom-call(s32[1]{0:T(128)} %bitcast.1.side, f32[120,64,128]{2,1,0:T(8,128)S(1)} %get-tuple-element.44.own, f32[120,64,128]{2,1,0:T(8,128)S(1)} %get-tuple-element.45.other, f32[18,64,128]{2,1,0:T(8,128)S(1)} %collective-permute-done.2.near, ...), custom_call_target="tpu_custom_call" | custom-call | bytes 18000000 | tf_op jit(solution)/shard_map/pair/pallas_call | solution.py:532
  74.3 0.1 collective-permute-start.8
  74.4 4.8 %collective-permute-start.9 = (f32[12,64,128]{2,1,0:T(8,128)S(1)}, f32[12,64,128]{2,1,0:T(8,128)S(1)}, u32[]{:S(2)}, u32[]{:S(2)}) collective-permute-start(f32[12,64,128]{2,1,0:T(8,128)S(1)} %get-tuple-element.50.refs_0_), channel_id=1, source_target_pairs={{0,30},{1,31},{2,0},{3,1},{4,2},{5,3},{6,4},{7,5},{8,6},{9,7},{10,... | collective-permute-start | bytes 1179656 | tf_op jit(solution)/shard_map/ppermute | solution.py:458
  79.1 0.1 collective-permute-done.16.refs_2_
  79.2 0.0 collective-permute-done.17.refs_3_
  79.2 3.2 %pair.10 = (f32[12,64,128]{2,1,0:T(8,128)S(1)}, f32[12,64,128]{2,1,0:T(8,128)S(1)}) custom-call(s32[1]{0:T(128)} %bitcast.1.side, f32[120,64,128]{2,1,0:T(8,128)S(1)} %get-tuple-element.44.own, f32[120,64,128]{2,1,0:T(8,128)S(1)} %get-tuple-element.45.other, f32[18,64,128]{2,1,0:T(8,128)S(1)} %collective-permute-done.2.near, ...), custom_call_target="tpu_custom_call" | custom-call | bytes 18000000 | tf_op jit(solution)/shard_map/pair/pallas_call | solution.py:532
  82.5 0.1 collective-permute-start.18
  82.5 4.8 %collective-permute-start.19 = (f32[12,64,128]{2,1,0:T(8,128)S(1)}, f32[12,64,128]{2,1,0:T(8,128)S(1)}, u32[]{:S(2)}, u32[]{:S(2)}) collective-permute-start(f32[12,64,128]{2,1,0:T(8,128)S(1)} %get-tuple-element.62.refs_0_), channel_id=1, source_target_pairs={{0,30},{1,31},{2,0},{3,1},{4,2},{5,3},{6,4},{7,5},{8,6},{9,7},{10,... | collective-permute-start | bytes 1179656 | tf_op jit(solution)/shard_map/ppermute | solution.py:458
  87.3 3.2 %pair.7 = (f32[12,64,128]{2,1,0:T(8,128)S(1)}, f32[12,64,128]{2,1,0:T(8,128)S(1)}) custom-call(s32[1]{0:T(128)} %bitcast.1.side, f32[120,64,128]{2,1,0:T(8,128)S(1)} %get-tuple-element.44.own, f32[120,64,128]{2,1,0:T(8,128)S(1)} %get-tuple-element.45.other, f32[18,64,128]{2,1,0:T(8,128)S(1)} %collective-permute-done.2.near, ...), custom_call_target="tpu_custom_call" | custom-call | bytes 18000000 | tf_op jit(solution)/shard_map/pair/pallas_call | solution.py:532
  90.5 0.1 collective-permute-start.10
  90.6 4.8 %collective-permute-start.11 = (f32[12,64,128]{2,1,0:T(8,128)S(1)}, f32[12,64,128]{2,1,0:T(8,128)S(1)}, u32[]{:S(2)}, u32[]{:S(2)}) collective-permute-start(f32[12,64,128]{2,1,0:T(8,128)S(1)} %get-tuple-element.52.refs_0_), channel_id=1, source_target_pairs={{0,30},{1,31},{2,0},{3,1},{4,2},{5,3},{6,4},{7,5},{8,6},{9,7},{10,... | collective-permute-start | bytes 1179656 | tf_op jit(solution)/shard_map/ppermute | solution.py:458
  95.4 0.0 collective-permute-done.18.refs_2_
  95.4 3.2 %pair.11 = (f32[12,64,128]{2,1,0:T(8,128)S(1)}, f32[12,64,128]{2,1,0:T(8,128)S(1)}) custom-call(s32[1]{0:T(128)} %bitcast.1.side, f32[120,64,128]{2,1,0:T(8,128)S(1)} %get-tuple-element.44.own, f32[120,64,128]{2,1,0:T(8,128)S(1)} %get-tuple-element.45.other, f32[18,64,128]{2,1,0:T(8,128)S(1)} %collective-permute-done.2.near, ...), custom_call_target="tpu_custom_call" | custom-call | bytes 18000000 | tf_op jit(solution)/shard_map/pair/pallas_call | solution.py:532
  98.6 0.1 collective-permute-start.20
  98.7 4.8 %collective-permute-start.21 = (f32[12,64,128]{2,1,0:T(8,128)S(1)}, f32[12,64,128]{2,1,0:T(8,128)S(1)}, u32[]{:S(2)}, u32[]{:S(2)}) collective-permute-start(f32[12,64,128]{2,1,0:T(8,128)S(1)} %get-tuple-element.64.x_0), channel_id=1, source_target_pairs={{0,30},{1,31},{2,0},{3,1},{4,2},{5,3},{6,4},{7,5},{8,6},{9,7},{10,... | collective-permute-start | bytes 1179656 | tf_op jit(solution)/shard_map/ppermute | solution.py:458
  103.5 0.2 collective-permute-done.10.refs_2_
  103.6 3.2 %pair.8 = (f32[12,64,128]{2,1,0:T(8,128)S(1)}, f32[12,64,128]{2,1,0:T(8,128)S(1)}) custom-call(s32[1]{0:T(128)} %bitcast.1.side, f32[120,64,128]{2,1,0:T(8,128)S(1)} %get-tuple-element.44.own, f32[120,64,128]{2,1,0:T(8,128)S(1)} %get-tuple-element.45.other, f32[18,64,128]{2,1,0:T(8,128)S(1)} %collective-permute-done.2.near, ...), custom_call_target="tpu_custom_call" | custom-call | bytes 18000000 | tf_op jit(solution)/shard_map/pair/pallas_call | solution.py:532
  106.8 0.1 collective-permute-start.12
  106.9 4.8 %collective-permute-start.13 = (f32[12,64,128]{2,1,0:T(8,128)S(1)}, f32[12,64,128]{2,1,0:T(8,128)S(1)}, u32[]{:S(2)}, u32[]{:S(2)}) collective-permute-start(f32[12,64,128]{2,1,0:T(8,128)S(1)} %get-tuple-element.54.x_0), channel_id=1, source_target_pairs={{0,30},{1,31},{2,0},{3,1},{4,2},{5,3},{6,4},{7,5},{8,6},{9,7},{10,... | collective-permute-start | bytes 1179656 | tf_op jit(solution)/shard_map/ppermute | solution.py:458
  111.7 0.1 collective-permute-done.20.f_0
  111.7 3.7 %last.3 = f32[6,16,128]{2,1,0:T(8,128)S(1)} custom-call(s32[1]{0:T(128)} %bitcast.1.side, f32[120,64,128]{2,1,0:T(8,128)S(1)} %get-tuple-element.44.own, f32[120,64,128]{2,1,0:T(8,128)S(1)} %get-tuple-element.45.other, f32[18,64,128]{2,1,0:T(8,128)S(1)} %collective-permute-done.2.near, f32[18,64,128]{2,1,0:T(8,128)S(1)} %collective-permute-done.3.far, ...), custom_call_target="tpu_custom_call" | custom-call | bytes 21600000 | tf_op jit(solution)/shard_map/last/pallas_call | solution.py:535
  115.5 0.0 copy-start.4
  115.5 4.3 %collective-permute-done.12.f_0 = f32[12,64,128]{2,1,0:T(8,128)S(1)} collective-permute-done((f32[12,64,128]{2,1,0:T(8,128)S(1)}, f32[12,64,128]{2,1,0:T(8,128)S(1)}, u32[]{:S(2)}, u32[]{:S(2)}) %collective-permute-start.12) | collective-permute-done | bytes 393248 | tf_op jit(solution)/shard_map/ppermute | solution.py:458
  119.8 3.7 %last.2 = f32[6,16,128]{2,1,0:T(8,128)S(1)} custom-call(s32[1]{0:T(128)} %bitcast.1.side, f32[120,64,128]{2,1,0:T(8,128)S(1)} %get-tuple-element.44.own, f32[120,64,128]{2,1,0:T(8,128)S(1)} %get-tuple-element.45.other, f32[18,64,128]{2,1,0:T(8,128)S(1)} %collective-permute-done.2.near, f32[18,64,128]{2,1,0:T(8,128)S(1)} %collective-permute-done.3.far, ...), custom_call_target="tpu_custom_call" | custom-call | bytes 21600000 | tf_op jit(solution)/shard_map/last/pallas_call | solution.py:535
  123.5 0.1 reduce_sum.28
  123.7 0.1 reduce_sum.29
  123.8 0.6 broadcast_in_dim.22
  124.5 10.0 %all-to-all-start.1 = ((f32[128,1,128]{2,1,0:T(1,128)}), f32[128,1,128]{2,1,0:T(1,128)S(1)}, u32[]{:S(2)}, u32[]{:S(2)}) async-start(f32[128,1,128]{2,1,0:T(1,128)} %bitcast.12), calls=%async_computation.1 | async-start | bytes 131072 | tf_op jit(solution)/shard_map/all_to_all | solution.py:542
  134.5 0.1 reshape.43
  134.6 6.2 %stencil.1.base = f32[3,2,32,128]{3,2,1,0:T(8,128)S(1)} custom-call(bf16[27,3,3,2,32,128]{5,4,3,2,1,0:T(8,128)(2,1)} %blocks.1, f32[3,2,32,128]{3,2,1,0:T(8,128)} %disp.3, f32[3,1,32,128]{3,2,1,0:T(8,128)} %copy-done.1, f32[3,1,32,128]{3,2,1,0:T(8,128)} %copy-done.2, f32[3,2,32,128]{3,2,1,0:T(8,128)} %external.1), custom_call_target="tpu_custom_call" | custom-call | bytes 18000000 | tf_op jit(solution)/shard_map/stencil/pallas_call | solution.py:393
  140.8 3.2 %all-to-all-done.1 = f32[128,1,128]{2,1,0:T(1,128)S(1)} async-done(((f32[128,1,128]{2,1,0:T(1,128)}), f32[128,1,128]{2,1,0:T(1,128)S(1)}, u32[]{:S(2)}, u32[]{:S(2)}) %all-to-all-start.1) | async-done | bytes 65568 | tf_op jit(solution)/shard_map/all_to_all | solution.py:542
  144.0 1.3 final.1
  (24 shorter events, 0.1 us)
Async XLA Ops:
  0.6 14.3 %copy-start = (f32[3,2,32,128]{3,2,1,0:T(8,128)S(1)}, f32[3,2,32,128]{3,2,1,0:T(8,128)}, u32[]{:S(2)}) copy-start(f32[3,2,32,128]{3,2,1,0:T(8,128)} %disp.3) | copy-start | bytes 294916
  0.6 14.2 %copy-start.5 = (s32[2,1]{0,1:T(1,128)S(1)}, s32[2,1]{0,1:T(1,128)}, u32[]{:S(2)}) copy-start(s32[2,1]{0,1:T(1,128)} %param.16) | copy-start | bytes 28
  0.7 14.3 %copy-start.3 = (s32[2]{0:T(128)S(1)}, s32[2]{0:T(128)}, u32[]{:S(2)}) copy-start(s32[2]{0:T(128)} %node.3) | copy-start | bytes 28
  1.5 10.2 %collective-permute-start = (f32[3,1,32,128]{3,2,1,0:T(8,128)S(1)}, f32[3,1,32,128]{3,2,1,0:T(8,128)S(1)}, u32[]{:S(2)}, u32[]{:S(2)}) collective-permute-start(f32[3,1,32,128]{3,2,1,0:T(8,128)S(1)} %get-tuple-element.69), channel_id=1, source_target_pairs={{0,1},{1,2},{2,3},{3,4},{4,5},{5,6},{6,7},{7,8},{8,9},{9,10},{10,1... | collective-permute-start | bytes 147464 | tf_op jit(solution)/shard_map/ppermute | solution.py:458
  6.0 5.7 %collective-permute-start.1 = (f32[3,1,32,128]{3,2,1,0:T(8,128)S(1)}, f32[3,1,32,128]{3,2,1,0:T(8,128)S(1)}, u32[]{:S(2)}, u32[]{:S(2)}) collective-permute-start(f32[3,1,32,128]{3,2,1,0:T(8,128)S(1)} %get-tuple-element.68), channel_id=1, source_target_pairs={{1,0},{2,1},{3,2},{4,3},{5,4},{6,5},{7,6},{8,7},{9,8},{10,9},{11,1... | collective-permute-start | bytes 147464 | tf_op jit(solution)/shard_map/ppermute | solution.py:458
  11.7 34.5 %copy-start.1 = (f32[3,1,32,128]{3,2,1,0:T(8,128)}, f32[3,1,32,128]{3,2,1,0:T(8,128)S(1)}, u32[]{:S(2)}) copy-start(f32[3,1,32,128]{3,2,1,0:T(8,128)S(1)} %collective-permute-done.before) | copy-start | bytes 147460
  11.7 34.5 %copy-start.2 = (f32[3,1,32,128]{3,2,1,0:T(8,128)}, f32[3,1,32,128]{3,2,1,0:T(8,128)S(1)}, u32[]{:S(2)}) copy-start(f32[3,1,32,128]{3,2,1,0:T(8,128)S(1)} %collective-permute-done.1.after) | copy-start | bytes 147460
  11.7 29.5 %collective-permute-start.4 = (f32[120,64,128]{2,1,0:T(8,128)}, f32[120,64,128]{2,1,0:T(8,128)}, u32[]{:S(2)}, u32[]{:S(2)}) collective-permute-start(f32[120,64,128]{2,1,0:T(8,128)} %get-tuple-element.43.own_hbm), channel_id=1, source_target_pairs={{0,1},{1,0},{2,3},{3,2},{4,5},{5,4},{6,7},{7,6},{8,9},{9,8},{10,11... | collective-permute-start | bytes 11796488 | tf_op jit(solution)/shard_map/ppermute | solution.py:458
  11.8 27.5 %collective-permute-start.2 = (f32[18,64,128]{2,1,0:T(8,128)S(1)}, f32[18,64,128]{2,1,0:T(8,128)S(1)}, u32[]{:S(2)}, u32[]{:S(2)}) collective-permute-start(f32[18,64,128]{2,1,0:T(8,128)S(1)} %get-tuple-element.38), channel_id=1, source_target_pairs={{0,31},{1,2},{2,1},{3,4},{4,3},{5,6},{6,5},{7,8},{8,7},{9,10},{10,... | collective-permute-start | bytes 1769480 | tf_op jit(solution)/shard_map/ppermute | solution.py:458
  13.6 25.6 %collective-permute-start.3 = (f32[18,64,128]{2,1,0:T(8,128)S(1)}, f32[18,64,128]{2,1,0:T(8,128)S(1)}, u32[]{:S(2)}, u32[]{:S(2)}) collective-permute-start(f32[18,64,128]{2,1,0:T(8,128)S(1)} %get-tuple-element.39), channel_id=1, source_target_pairs={{0,30},{1,3},{2,0},{3,5},{4,2},{5,7},{6,4},{7,9},{8,6},{9,11},{10,... | collective-permute-start | bytes 1769480 | tf_op jit(solution)/shard_map/ppermute | solution.py:458
  40.5 5.8 %collective-permute-start.5 = (f32[36,64,128]{2,1,0:T(8,128)}, f32[36,64,128]{2,1,0:T(8,128)S(1)}, u32[]{:S(2)}, u32[]{:S(2)}) collective-permute-start(f32[36,64,128]{2,1,0:T(8,128)} %pad_maximum_fusion), channel_id=1, source_target_pairs={{0,1},{1,0},{2,3},{3,2},{4,5},{5,4},{6,7},{7,6},{8,9},{9,8},{10,11... | collective-permute-start | bytes 3538952 | tf_op jit(solution)/shard_map/ppermute | solution.py:458
  48.6 14.1 %collective-permute-start.14 = (f32[12,64,128]{2,1,0:T(8,128)S(1)}, f32[12,64,128]{2,1,0:T(8,128)S(1)}, u32[]{:S(2)}, u32[]{:S(2)}) collective-permute-start(f32[12,64,128]{2,1,0:T(8,128)S(1)} %get-tuple-element.59.refs_1_), channel_id=1, source_target_pairs={{0,2},{1,3},{2,4},{3,5},{4,6},{5,7},{6,8},{7,9},{8,10},{9,11},{10,... | collective-permute-start | bytes 1179656 | tf_op jit(solution)/shard_map/ppermute | solution.py:458
  48.7 14.1 %collective-permute-start.15 = (f32[12,64,128]{2,1,0:T(8,128)S(1)}, f32[12,64,128]{2,1,0:T(8,128)S(1)}, u32[]{:S(2)}, u32[]{:S(2)}) collective-permute-start(f32[12,64,128]{2,1,0:T(8,128)S(1)} %get-tuple-element.58.refs_0_), channel_id=1, source_target_pairs={{0,30},{1,31},{2,0},{3,1},{4,2},{5,3},{6,4},{7,5},{8,6},{9,7},{10,... | collective-permute-start | bytes 1179656 | tf_op jit(solution)/shard_map/ppermute | solution.py:458
  57.5 13.5 %collective-permute-start.6 = (f32[12,64,128]{2,1,0:T(8,128)S(1)}, f32[12,64,128]{2,1,0:T(8,128)S(1)}, u32[]{:S(2)}, u32[]{:S(2)}) collective-permute-start(f32[12,64,128]{2,1,0:T(8,128)S(1)} %get-tuple-element.49.refs_1_), channel_id=1, source_target_pairs={{0,2},{1,3},{2,4},{3,5},{4,6},{5,7},{6,8},{7,9},{8,10},{9,11},{10,... | collective-permute-start | bytes 1179656 | tf_op jit(solution)/shard_map/ppermute | solution.py:458
  57.6 13.4 %collective-permute-start.7 = (f32[12,64,128]{2,1,0:T(8,128)S(1)}, f32[12,64,128]{2,1,0:T(8,128)S(1)}, u32[]{:S(2)}, u32[]{:S(2)}) collective-permute-start(f32[12,64,128]{2,1,0:T(8,128)S(1)} %get-tuple-element.48.refs_0_), channel_id=1, source_target_pairs={{0,30},{1,31},{2,0},{3,1},{4,2},{5,3},{6,4},{7,5},{8,6},{9,7},{10,... | collective-permute-start | bytes 1179656 | tf_op jit(solution)/shard_map/ppermute | solution.py:458
  66.0 13.2 %collective-permute-start.16 = (f32[12,64,128]{2,1,0:T(8,128)S(1)}, f32[12,64,128]{2,1,0:T(8,128)S(1)}, u32[]{:S(2)}, u32[]{:S(2)}) collective-permute-start(f32[12,64,128]{2,1,0:T(8,128)S(1)} %get-tuple-element.61.refs_1_), channel_id=1, source_target_pairs={{0,2},{1,3},{2,4},{3,5},{4,6},{5,7},{6,8},{7,9},{8,10},{9,11},{10,... | collective-permute-start | bytes 1179656 | tf_op jit(solution)/shard_map/ppermute | solution.py:458
  66.1 13.2 %collective-permute-start.17 = (f32[12,64,128]{2,1,0:T(8,128)S(1)}, f32[12,64,128]{2,1,0:T(8,128)S(1)}, u32[]{:S(2)}, u32[]{:S(2)}) collective-permute-start(f32[12,64,128]{2,1,0:T(8,128)S(1)} %get-tuple-element.60.refs_0_), channel_id=1, source_target_pairs={{0,30},{1,31},{2,0},{3,1},{4,2},{5,3},{6,4},{7,5},{8,6},{9,7},{10,... | collective-permute-start | bytes 1179656 | tf_op jit(solution)/shard_map/ppermute | solution.py:458
  74.3 13.0 %collective-permute-start.8 = (f32[12,64,128]{2,1,0:T(8,128)S(1)}, f32[12,64,128]{2,1,0:T(8,128)S(1)}, u32[]{:S(2)}, u32[]{:S(2)}) collective-permute-start(f32[12,64,128]{2,1,0:T(8,128)S(1)} %get-tuple-element.51.refs_1_), channel_id=1, source_target_pairs={{0,2},{1,3},{2,4},{3,5},{4,6},{5,7},{6,8},{7,9},{8,10},{9,11},{10,... | collective-permute-start | bytes 1179656 | tf_op jit(solution)/shard_map/ppermute | solution.py:458
  74.4 13.0 %collective-permute-start.9 = (f32[12,64,128]{2,1,0:T(8,128)S(1)}, f32[12,64,128]{2,1,0:T(8,128)S(1)}, u32[]{:S(2)}, u32[]{:S(2)}) collective-permute-start(f32[12,64,128]{2,1,0:T(8,128)S(1)} %get-tuple-element.50.refs_0_), channel_id=1, source_target_pairs={{0,30},{1,31},{2,0},{3,1},{4,2},{5,3},{6,4},{7,5},{8,6},{9,7},{10,... | collective-permute-start | bytes 1179656 | tf_op jit(solution)/shard_map/ppermute | solution.py:458
  82.5 12.9 %collective-permute-start.18 = (f32[12,64,128]{2,1,0:T(8,128)S(1)}, f32[12,64,128]{2,1,0:T(8,128)S(1)}, u32[]{:S(2)}, u32[]{:S(2)}) collective-permute-start(f32[12,64,128]{2,1,0:T(8,128)S(1)} %get-tuple-element.63.refs_1_), channel_id=1, source_target_pairs={{0,2},{1,3},{2,4},{3,5},{4,6},{5,7},{6,8},{7,9},{8,10},{9,11},{10,... | collective-permute-start | bytes 1179656 | tf_op jit(solution)/shard_map/ppermute | solution.py:458
  82.5 12.9 %collective-permute-start.19 = (f32[12,64,128]{2,1,0:T(8,128)S(1)}, f32[12,64,128]{2,1,0:T(8,128)S(1)}, u32[]{:S(2)}, u32[]{:S(2)}) collective-permute-start(f32[12,64,128]{2,1,0:T(8,128)S(1)} %get-tuple-element.62.refs_0_), channel_id=1, source_target_pairs={{0,30},{1,31},{2,0},{3,1},{4,2},{5,3},{6,4},{7,5},{8,6},{9,7},{10,... | collective-permute-start | bytes 1179656 | tf_op jit(solution)/shard_map/ppermute | solution.py:458
  90.5 13.1 %collective-permute-start.10 = (f32[12,64,128]{2,1,0:T(8,128)S(1)}, f32[12,64,128]{2,1,0:T(8,128)S(1)}, u32[]{:S(2)}, u32[]{:S(2)}) collective-permute-start(f32[12,64,128]{2,1,0:T(8,128)S(1)} %get-tuple-element.53.refs_1_), channel_id=1, source_target_pairs={{0,2},{1,3},{2,4},{3,5},{4,6},{5,7},{6,8},{7,9},{8,10},{9,11},{10,... | collective-permute-start | bytes 1179656 | tf_op jit(solution)/shard_map/ppermute | solution.py:458
  90.6 13.0 %collective-permute-start.11 = (f32[12,64,128]{2,1,0:T(8,128)S(1)}, f32[12,64,128]{2,1,0:T(8,128)S(1)}, u32[]{:S(2)}, u32[]{:S(2)}) collective-permute-start(f32[12,64,128]{2,1,0:T(8,128)S(1)} %get-tuple-element.52.refs_0_), channel_id=1, source_target_pairs={{0,30},{1,31},{2,0},{3,1},{4,2},{5,3},{6,4},{7,5},{8,6},{9,7},{10,... | collective-permute-start | bytes 1179656 | tf_op jit(solution)/shard_map/ppermute | solution.py:458
  98.6 13.1 %collective-permute-start.20 = (f32[12,64,128]{2,1,0:T(8,128)S(1)}, f32[12,64,128]{2,1,0:T(8,128)S(1)}, u32[]{:S(2)}, u32[]{:S(2)}) collective-permute-start(f32[12,64,128]{2,1,0:T(8,128)S(1)} %get-tuple-element.65.x_1), channel_id=1, source_target_pairs={{0,2},{1,3},{2,4},{3,5},{4,6},{5,7},{6,8},{7,9},{8,10},{9,11},{10,... | collective-permute-start | bytes 1179656 | tf_op jit(solution)/shard_map/ppermute | solution.py:458
  98.7 13.1 %collective-permute-start.21 = (f32[12,64,128]{2,1,0:T(8,128)S(1)}, f32[12,64,128]{2,1,0:T(8,128)S(1)}, u32[]{:S(2)}, u32[]{:S(2)}) collective-permute-start(f32[12,64,128]{2,1,0:T(8,128)S(1)} %get-tuple-element.64.x_0), channel_id=1, source_target_pairs={{0,30},{1,31},{2,0},{3,1},{4,2},{5,3},{6,4},{7,5},{8,6},{9,7},{10,... | collective-permute-start | bytes 1179656 | tf_op jit(solution)/shard_map/ppermute | solution.py:458
  106.8 13.0 %collective-permute-start.12 = (f32[12,64,128]{2,1,0:T(8,128)S(1)}, f32[12,64,128]{2,1,0:T(8,128)S(1)}, u32[]{:S(2)}, u32[]{:S(2)}) collective-permute-start(f32[12,64,128]{2,1,0:T(8,128)S(1)} %get-tuple-element.55.x_1), channel_id=1, source_target_pairs={{0,2},{1,3},{2,4},{3,5},{4,6},{5,7},{6,8},{7,9},{8,10},{9,11},{10,... | collective-permute-start | bytes 1179656 | tf_op jit(solution)/shard_map/ppermute | solution.py:458
  106.9 12.9 %collective-permute-start.13 = (f32[12,64,128]{2,1,0:T(8,128)S(1)}, f32[12,64,128]{2,1,0:T(8,128)S(1)}, u32[]{:S(2)}, u32[]{:S(2)}) collective-permute-start(f32[12,64,128]{2,1,0:T(8,128)S(1)} %get-tuple-element.54.x_0), channel_id=1, source_target_pairs={{0,30},{1,31},{2,0},{3,1},{4,2},{5,3},{6,4},{7,5},{8,6},{9,7},{10,... | collective-permute-start | bytes 1179656 | tf_op jit(solution)/shard_map/ppermute | solution.py:458
  115.5 19.0 %copy-start.4 = (f32[2,18]{1,0:T(2,128)S(1)}, f32[2,18]{1,0:T(2,128)}, u32[]{:S(2)}) copy-start(f32[2,18]{1,0:T(2,128)} %param.17) | copy-start | bytes 436
  124.5 19.5 %all-to-all-start.1 = ((f32[128,1,128]{2,1,0:T(1,128)}), f32[128,1,128]{2,1,0:T(1,128)S(1)}, u32[]{:S(2)}, u32[]{:S(2)}) async-start(f32[128,1,128]{2,1,0:T(1,128)} %bitcast.12), calls=%async_computation.1 | async-start | bytes 131072 | tf_op jit(solution)/shard_map/all_to_all | solution.py:542
